TPU v7x, 512 devices: a whole 4x8x8 slice. The times are simulated.
512 devices in a mesh: row: 32 (over y, z_hi, core), col: 16 (over x, z_lo).
Axes of the slice: x: 4, y: 8, z: 8 (z_hi: 2, z_lo: 4; z = z_hi * 4 + z_lo), core: 2. Of those that a mesh axis runs over, the one named last changes fastest.
Arguments:
- traces: bfloat16 [2048, 64, 512], P(('row', 'col')), may hold values from -6 to 6
- live_flags: int32 [2048], P(('row', 'col')), may hold values 0 or 1
Outputs:
- correlations: bfloat16 [2048, 2048, 128], P('row', 'col')
Inputs may be any that keep to these rules, and one draw needn't show every extreme that they name: `live_flags`: 1 marks a working channel.
All inputs are finite; a program needn't handle non-finite values. No bound on the sum of `live_flags` on one device may be relied on, other than what follows from the above.
Results may differ from a plain program's by a relative error of at most 0.0058.
Values may be sent and summed in bfloat16 or wider, within the bound.
No kernel may reach another device: no remote copies, remote signals or barrier semaphores. Data moves between devices by JAX's collectives and lax.ppermute only.
A program may use at most 64 MiB of HBM per device.

v0:
```python
import math

import jax
import jax.numpy as jnp
import numpy as np
from jax import lax
from jax.experimental import pallas as pl
from jax.experimental.pallas import tpu as pltpu
from jax.sharding import PartitionSpec as P

F = 256
LAGS = 128
SAMP = 512
NW = 64
N_Y, N_H, N_C, N_X, N_L = 8, 2, 2, 4, 4
HALF = F // 2
PIECE = HALF * 8
AXES = ("row", "col")


def bf16_parts(table, count):
    parts = []
    rest = table.astype(np.float32)
    for _ in range(count):
        part = rest.astype(jnp.bfloat16)
        parts.append(part)
        rest = rest - part.astype(np.float32)
    return np.stack(parts)


def make_tables():
    samples = np.arange(SAMP)
    bins = np.arange(F)
    angle = 2.0 * math.pi * (bins[:, None] * samples[None, :] % SAMP) / SAMP
    forward = np.concatenate([np.cos(angle), -np.sin(angle)], axis=0)
    taper = 0.5 - 0.5 * np.cos(2.0 * math.pi * samples / SAMP)
    dft = bf16_parts(forward * taper[None, :], 3)
    near = (np.abs(bins[:, None] - bins[None, :]) <= 4).astype(np.float32)
    lags = np.arange(LAGS) - LAGS // 2
    langle = 2.0 * math.pi * (bins[:, None] * lags[None, :] % SAMP) / SAMP
    shift = 1.0 / (math.sqrt(NW) * math.sqrt(F))
    cs = np.cos(langle).astype(np.float32).astype(jnp.bfloat16).astype(np.float32)
    sn = np.sin(langle).astype(np.float32).astype(jnp.bfloat16).astype(np.float32)
    inverse = []
    for half in range(2):
        part = slice(half * HALF, (half + 1) * HALF)
        table = np.concatenate([cs[part], -sn[part]], axis=0) * shift
        inverse.append(table.T.astype(jnp.bfloat16))
    return dft, near, np.stack(inverse)


def whiten_kernel(flags_ref, core_ref, x_ref, dft_ref, near_ref, keep_ref, send_ref, rows_ref):
    x = x_ref[...]
    spectra = None
    for part in (2, 1, 0):
        term = lax.dot_general(
            dft_ref[part], x, (((1,), (1,)), ((), ())), preferred_element_type=jnp.float32
        )
        spectra = term if spectra is None else spectra + term
    re = spectra[:F]
    im = spectra[F:]
    power = re * re + im * im
    bins = lax.broadcasted_iota(jnp.int32, (F, 1), 0)
    counts = jnp.minimum(bins + 4, F - 1) - jnp.maximum(bins - 4, 0) + 1
    smooth = jnp.dot(
        near_ref[...], power, precision=lax.Precision.HIGHEST, preferred_element_type=jnp.float32
    ) / counts.astype(jnp.float32)
    level = jnp.mean(power, axis=0, keepdims=True)
    lane = lax.broadcasted_iota(jnp.int32, (1, 4 * NW), 1) // NW
    alive = jnp.zeros((1, 4 * NW), jnp.float32)
    for ch in range(4):
        alive = jnp.where(lane == ch, flags_ref[ch].astype(jnp.float32), alive)
    scale = lax.rsqrt(smooth + 0.05 * level + 1e-06) * alive
    re = re * scale
    im = im * scale
    low = lax.broadcasted_iota(jnp.int32, (F, 2 * NW), 1) < NW
    for pair in range(2):
        lanes = slice(pair * 2 * NW, (pair + 1) * 2 * NW)
        re2, im2 = re[:, lanes], im[:, lanes]
        rows_ref[pl.ds(2 * pair, F, stride=4), :] = jnp.where(low, re2, pltpu.roll(im2, NW, 1))
        rows_ref[pl.ds(2 * pair + 1, F, stride=4), :] = jnp.where(low, pltpu.roll(re2, NW, 1), im2)
    size = HALF * 4
    core = core_ref[0]
    keep_ref[...] = rows_ref[pl.ds(pl.multiple_of(core * size, size), size), :].astype(jnp.bfloat16)
    send_ref[...] = rows_ref[pl.ds(pl.multiple_of((1 - core) * size, size), size), :].astype(jnp.bfloat16)


def whiten(traces, live_flags, core, dft, near):
    vmem = pl.BlockSpec(memory_space=pltpu.VMEM)
    smem = pl.BlockSpec(memory_space=pltpu.SMEM)
    shape = jax.ShapeDtypeStruct((HALF * 4, 2 * NW), jnp.bfloat16)
    return pl.pallas_call(
        whiten_kernel,
        out_shape=(shape, shape),
        in_specs=[smem, smem, vmem, vmem, vmem],
        out_specs=(vmem, vmem),
        scratch_shapes=[pltpu.VMEM((F * 4, 2 * NW), jnp.float32)],
        name="whiten",
    )(live_flags, core, traces.reshape(4 * NW, SAMP), dft, near)


def merge_kernel(core_ref, keep_ref, got_ref, out_ref):
    keep = keep_ref[...].astype(jnp.float32).reshape(HALF // 2, 8, 2 * NW)
    got = got_ref[...].astype(jnp.float32).reshape(HALF // 2, 8, 2 * NW)
    first = core_ref[0] == 0
    a = jnp.where(first, keep, got)
    b = jnp.where(first, got, keep)
    low = lax.broadcasted_iota(jnp.int32, (HALF // 2, 8, 2 * NW), 1) < 4
    even = jnp.where(low, a, pltpu.roll(b, 4, 1))
    odd = jnp.where(low, pltpu.roll(a, 4, 1), b)
    both = jnp.concatenate([even[:, None], odd[:, None]], axis=1)
    out_ref[...] = both.reshape(PIECE, 2 * NW).astype(jnp.bfloat16)


def merge(core, keep, got):
    vmem = pl.BlockSpec(memory_space=pltpu.VMEM)
    return pl.pallas_call(
        merge_kernel,
        out_shape=jax.ShapeDtypeStruct((PIECE, 2 * NW), jnp.bfloat16),
        in_specs=[pl.BlockSpec(memory_space=pltpu.SMEM), vmem, vmem],
        out_specs=vmem,
        name="merge",
    )(core, keep, got)


N_CHUNK = 4
PITCH = 2 * HALF + 8
CHUNK = HALF // N_CHUNK


def cross_kernel(n_first, n_second, where_ref, core_ref, *refs):
    n_in = len(n_first) + len(n_second)
    inputs = refs[:n_in]
    inv_ref, send_ref, own_ref, a_ref, b_ref, s_ref, sem = refs[n_in:]
    copies = []
    for chunk in range(N_CHUNK):
        row = []
        slot = 0
        for index, ref in enumerate(inputs):
            count = (n_first + n_second)[index]
            dst = a_ref if index < len(n_first) else b_ref
            for piece in range(count):
                src = ref.at[piece] if count > 1 else ref
                place = pl.multiple_of(where_ref[slot] * 8, 8)
                bins = pl.ds(chunk * CHUNK, CHUNK)
                copy = pltpu.make_async_copy(
                    src.at[bins], dst.at[bins, pl.ds(place, 8), :], sem.at[chunk, slot]
                )
                copy.start()
                row.append(copy)
                slot += 1
        copies.append(row)
    sign = jnp.where(
        lax.broadcasted_iota(jnp.int32, (128, 2 * NW), 1) < NW, 1.0, -1.0
    ).astype(jnp.bfloat16)
    contract = (((1,), (1,)), ((), ()))

    def one_bin(f, carry):
        a = a_ref[f]
        b = b_ref[f]
        turned = jnp.concatenate([a[:, NW:], a[:, :NW]], axis=1) * sign
        both = jnp.concatenate([a, turned], axis=0)
        terms = lax.dot_general(both, b, contract, preferred_element_type=jnp.float32)
        s_ref[pl.ds(f, 128, stride=PITCH), :] = terms[:128]
        s_ref[pl.ds(f + HALF, 128, stride=PITCH), :] = terms[128:]
        return carry

    for chunk in range(N_CHUNK):
        for copy in copies[chunk]:
            copy.wait()
        lax.fori_loop(chunk * CHUNK, (chunk + 1) * CHUNK, one_bin, 0, unroll=16)

    core = core_ref[0]
    table = inv_ref[...]

    def lag_pair(step, which, out_ref):
        piece, half = step // 2, step % 2
        row = piece * 8 + which * 4 + half * 2
        start = pl.multiple_of(row * PITCH, 8)
        w0 = s_ref[pl.ds(start, 2 * HALF), :].astype(jnp.bfloat16)
        w1 = s_ref[pl.ds(pl.multiple_of(start + PITCH, 8), 2 * HALF), :].astype(jnp.bfloat16)
        both = jnp.concatenate([w0, w1], axis=1)
        lagged = jnp.dot(table, both, preferred_element_type=jnp.float32)
        i = piece * 4 + half * 2
        out_ref[i] = lagged[:, :128].T.astype(out_ref.dtype)
        out_ref[i + 1] = lagged[:, 128:].T.astype(out_ref.dtype)

    def send_step(step, carry):
        lag_pair(step, 1 - core, send_ref)
        return carry

    def own_step(step, carry):
        lag_pair(step, core, own_ref)
        return carry

    lax.fori_loop(0, 32, send_step, 0, unroll=8)
    lax.fori_loop(0, 32, own_step, 0, unroll=8)


def cross(where, core, firsts, seconds, inverse):
    count = lambda x: 1 if x.ndim == 3 else x.shape[0]
    n_first = tuple(count(x) for x in firsts)
    n_second = tuple(count(x) for x in seconds)
    kernel = lambda *refs: cross_kernel(n_first, n_second, *refs)
    anywhere = pl.BlockSpec(memory_space=pl.ANY)
    vmem = pl.BlockSpec(memory_space=pltpu.VMEM)
    smem = pl.BlockSpec(memory_space=pltpu.SMEM)
    n_in = len(firsts) + len(seconds)
    return pl.pallas_call(
        kernel,
        out_shape=(
            jax.ShapeDtypeStruct((64, 128, LAGS), jnp.bfloat16),
            jax.ShapeDtypeStruct((64, 128, LAGS), jnp.float32),
        ),
        in_specs=[smem, smem] + [anywhere] * n_in + [vmem],
        out_specs=(vmem, vmem),
        scratch_shapes=[
            pltpu.VMEM((HALF, 128, 2 * NW), jnp.bfloat16),
            pltpu.VMEM((HALF, 128, 2 * NW), jnp.bfloat16),
            pltpu.VMEM((128 * PITCH, 128), jnp.float32),
            pltpu.SemaphoreType.DMA((N_CHUNK, 32)),
        ],
        compiler_params=pltpu.CompilerParams(vmem_limit_bytes=56 * 1024 * 1024),
        name="cross",
    )(where, core, *firsts, *seconds, inverse)


def permutation(move):
    pairs = []
    for index in range(N_Y * N_H * N_C * N_X * N_L):
        rest, l = divmod(index, N_L)
        rest, x = divmod(rest, N_X)
        rest, c = divmod(rest, N_C)
        y, h = divmod(rest, N_H)
        y, h, c, x, l = move(y, h, c, x, l)
        pairs.append((index, (((y % N_Y * N_H + h) * N_C + c) * N_X + x % N_X) * N_L + l % N_L))
    return pairs


SWAP_CORE = permutation(lambda y, h, c, x, l: (y, h, 1 - c, x, l))
SWAP_H = permutation(lambda y, h, c, x, l: (y, 1 - h, c, x, l))
STEP_L = [permutation(lambda y, h, c, x, l, d=d: (y, h, c, x, l + d)) for d in range(4)]
Y_UP = permutation(lambda y, h, c, x, l: (y + 1, h, c, x, l))
Y_DOWN = permutation(lambda y, h, c, x, l: (y - 1, h, c, x, l))
X_UP = permutation(lambda y, h, c, x, l: (y, h, c, x + 1, l))
X_DOWN = permutation(lambda y, h, c, x, l: (y, h, c, x - 1, l))


def move(value, pairs):
    return lax.ppermute(value, AXES, pairs)


def correlate(traces, live_flags):
    dft, near, inverse = make_tables()
    row = lax.axis_index("row")
    col = lax.axis_index("col")
    y, h, c = row // 4, row // 2 % 2, row % 2
    x, l = col // N_L, col % N_L
    core = c.reshape(1)
    keep, send = whiten(traces, live_flags, core, jnp.asarray(dft), jnp.asarray(near))
    piece = merge(core, keep, move(send, SWAP_CORE)).reshape(HALF, 8, 2 * NW)

    other = move(piece, SWAP_H)
    up1, down1 = move(piece, Y_UP), move(piece, Y_DOWN)
    l1, l3 = move(piece, STEP_L[1]), move(piece, STEP_L[3])
    up2 = move(jnp.stack([up1, other]), Y_UP)
    down2 = move(jnp.stack([down1, other]), Y_DOWN)
    l2 = move(piece, STEP_L[2])
    x1 = jnp.stack([piece, l1])
    x1_up, x1_down = move(x1, X_UP), move(x1, X_DOWN)
    up3, down3 = move(up2, Y_UP), move(down2, Y_DOWN)
    x2 = jnp.stack([l3, l2])
    x2_up, x2_down = move(x2, X_UP), move(x2, X_DOWN)
    x1_far = move(x1_up, X_UP)
    up4 = move(up3, Y_UP)
    down4 = move(down3[1], Y_DOWN)
    x2_far = move(x2_down, X_DOWN)
    down5 = move(down4, Y_DOWN)

    lead = [l, (l - 1) % N_L]
    rest = [(l - 3) % N_L, (l - 2) % N_L]
    firsts = (x1, x2, x1_up, x2_up, x1_down, x2_down, x1_far, x2_far)
    first_at = []
    for d in (0, -1, 1, 2):
        first_at += [(x + d) % N_X * N_L + q for q in lead + rest]
    seconds = (piece, up1, down1, up2, down2, up3, down3, up4, down4, down5)
    spot = lambda d, mine: (y + d) % N_Y * N_H + (h if mine else 1 - h)
    second_at = [spot(0, True), spot(-1, True), spot(1, True)]
    second_at += [spot(-2, True), spot(-1, False), spot(2, True), spot(1, False)]
    second_at += [spot(-3, True), spot(-2, False), spot(3, True), spot(2, False)]
    second_at += [spot(-4, True), spot(-3, False), spot(3, False), spot(4, False)]
    seconds += (other,)
    second_at += [spot(0, False)]
    where = jnp.stack(first_at + second_at).astype(jnp.int32)
    table = lax.dynamic_index_in_dim(jnp.asarray(inverse), c, 0, keepdims=False)
    sent, own = cross(where, core, firsts, seconds, table)
    corr = own + move(sent, SWAP_CORE).astype(jnp.float32)

    rows, cols = corr.shape[:2]
    chan_i = row * rows + jnp.arange(rows, dtype=jnp.int32)
    local_j = jnp.arange(cols, dtype=jnp.int32)
    chan_j = (local_j // 4 * (N_X * N_L) + col) * 4 + local_j % 4
    same = chan_i[:, None] == chan_j[None, :]
    corr = jnp.where(same[:, :, None], 0.0, corr)
    return corr.astype(jnp.bfloat16)


def solution(mesh):
    in_specs = (P(("row", "col"), None, None), P(("row", "col")))
    out_specs = P("row", "col", None)
    return jax.shard_map(
        correlate, mesh=mesh, in_specs=in_specs, out_specs=out_specs, check_vma=False
    )
```

profile of v0, /device:TPU:1, one launch (start us, length us, event | category | flops | bytes accessed | tf_op | source)
XLA Modules:
  0.0 148.0 jit_solution(1745760839252471977)
XLA Ops:
  0.0 3.7 %whiten.1 = (bf16[512,128]{1,0:T(8,128)(2,1)}, bf16[512,128]{1,0:T(8,128)(2,1)}) custom-call(s32[4]{0:T(128)} %flags_ref.1, s32[1]{0:T(128)} %bitcast.32.core_ref.refs_1_, bf16[256,512]{1,0:T(8,128)(2,1)} %bitcast.60, bf16[3,512,512]{2,1,0:T(8,128)(2,1)} %constant.219.clone.dft_ref, f32[256,256]{1,0:T(8,128)} %constant.220.clone.near_ref), custom_call_target="tpu_custom_call" | custom-call | tf_op jit(solution)/shard_map/whiten/pallas_call | solution.py:92
  3.7 8.7 %collective-permute-start = (bf16[512,128]{1,0:T(8,128)(2,1)}, bf16[512,128]{1,0:T(8,128)(2,1)S(1)}, u32[]{:S(2)}, u32[]{:S(2)}) collective-permute-start(bf16[512,128]{1,0:T(8,128)(2,1)} %get-tuple-element.10), channel_id=1, source_target_pairs={{0,16},{1,17},{2,18},{3,19},{4,20},{5,21},{6,22},{7,23},{8,24},{9,... | collective-permute-start | bytes 393224 | tf_op jit(solution)/shard_map/ppermute | solution.py:250
  14.3 1.7 %merge.1 = bf16[1024,128]{1,0:T(8,128)(2,1)} custom-call(s32[1]{0:T(128)} %bitcast.32.core_ref.refs_1_, bf16[512,128]{1,0:T(8,128)(2,1)} %get-tuple-element.9.keep_ref, bf16[512,128]{1,0:T(8,128)(2,1)} %copy-done.9), custom_call_target="tpu_custom_call" | custom-call | tf_op jit(solution)/shard_map/merge/pallas_call | solution.py:117
  16.0 1.9 %collective-permute-start.10 = (bf16[128,8,128]{2,1,0:T(8,128)(2,1)}, bf16[128,8,128]{2,1,0:T(8,128)(2,1)S(1)}, u32[]{:S(2)}, u32[]{:S(2)}) collective-permute-start(bf16[128,8,128]{2,1,0:T(8,128)(2,1)} %bitcast.46), channel_id=1, source_target_pairs={{0,64},{1,65},{2,66},{3,67},{4,68},{5,69},{6,70},{7,71},{8,72},{9,... | collective-permute-start | bytes 786440 | tf_op jit(solution)/shard_map/ppermute | solution.py:250
  17.9 6.6 %collective-permute-start.12 = (bf16[128,8,128]{2,1,0:T(8,128)(2,1)}, bf16[128,8,128]{2,1,0:T(8,128)(2,1)S(1)}, u32[]{:S(2)}, u32[]{:S(2)}) collective-permute-start(bf16[128,8,128]{2,1,0:T(8,128)(2,1)} %bitcast.47), channel_id=1, source_target_pairs={{0,32},{1,33},{2,34},{3,35},{4,36},{5,37},{6,38},{7,39},{8,40},{9,... | collective-permute-start | bytes 786440 | tf_op jit(solution)/shard_map/ppermute | solution.py:250
  24.5 3.8 %collective-permute-start.11 = (bf16[128,8,128]{2,1,0:T(8,128)(2,1)}, bf16[128,8,128]{2,1,0:T(8,128)(2,1)S(1)}, u32[]{:S(2)}, u32[]{:S(2)}) collective-permute-start(bf16[128,8,128]{2,1,0:T(8,128)(2,1)} %bitcast.48), channel_id=1, source_target_pairs={{0,448},{1,449},{2,450},{3,451},{4,452},{5,453},{6,454},{7,455},{8... | collective-permute-start | bytes 786440 | tf_op jit(solution)/shard_map/ppermute | solution.py:250
  28.4 3.7 %collective-permute-done.12.refs_20_ = bf16[128,8,128]{2,1,0:T(8,128)(2,1)S(1)} collective-permute-done((bf16[128,8,128]{2,1,0:T(8,128)(2,1)}, bf16[128,8,128]{2,1,0:T(8,128)(2,1)S(1)}, u32[]{:S(2)}, u32[]{:S(2)}) %collective-permute-start.12) | collective-permute-done | bytes 262176 | tf_op jit(solution)/shard_map/ppermute | solution.py:250
  32.1 1.6 %collective-permute-done.11.refs_12_ = bf16[128,8,128]{2,1,0:T(8,128)(2,1)S(1)} collective-permute-done((bf16[128,8,128]{2,1,0:T(8,128)(2,1)}, bf16[128,8,128]{2,1,0:T(8,128)(2,1)S(1)}, u32[]{:S(2)}, u32[]{:S(2)}) %collective-permute-start.11) | collective-permute-done | bytes 262176 | tf_op jit(solution)/shard_map/ppermute | solution.py:250
  33.7 5.2 %collective-permute-start.14 = (bf16[2,128,8,128]{3,2,1,0:T(8,128)(2,1)S(1)}, bf16[2,128,8,128]{3,2,1,0:T(8,128)(2,1)S(1)}, u32[]{:S(2)}, u32[]{:S(2)}) collective-permute-start(bf16[2,128,8,128]{3,2,1,0:T(8,128)(2,1)S(1)} %get-tuple-element.13), channel_id=1, source_target_pairs={{0,448},{1,449},{2,450},{3,451},{4,452},{5,453},{6,454},{7,455},{8... | collective-permute-start | bytes 1572872 | tf_op jit(solution)/shard_map/ppermute | solution.py:250
  39.0 4.9 %collective-permute-start.2 = (bf16[128,8,128]{2,1,0:T(8,128)(2,1)}, bf16[128,8,128]{2,1,0:T(8,128)(2,1)S(1)}, u32[]{:S(2)}, u32[]{:S(2)}) collective-permute-start(bf16[128,8,128]{2,1,0:T(8,128)(2,1)} %bitcast.49), channel_id=1, source_target_pairs={{0,3},{1,0},{2,1},{3,2},{4,7},{5,4},{6,5},{7,6},{8,11},{9,8},{10,9... | collective-permute-start | bytes 786440 | tf_op jit(solution)/shard_map/ppermute | solution.py:250
  43.9 2.9 %collective-permute-start.3 = (bf16[128,8,128]{2,1,0:T(8,128)(2,1)}, bf16[128,8,128]{2,1,0:T(8,128)(2,1)S(1)}, u32[]{:S(2)}, u32[]{:S(2)}) collective-permute-start(bf16[128,8,128]{2,1,0:T(8,128)(2,1)} %bitcast.50), channel_id=1, source_target_pairs={{0,2},{1,3},{2,0},{3,1},{4,6},{5,7},{6,4},{7,5},{8,10},{9,11},{10,... | collective-permute-start | bytes 786440 | tf_op jit(solution)/shard_map/ppermute | solution.py:250
  46.8 3.1 %collective-permute-start.1 = (bf16[128,8,128]{2,1,0:T(8,128)(2,1)}, bf16[128,8,128]{2,1,0:T(8,128)(2,1)S(1)}, u32[]{:S(2)}, u32[]{:S(2)}) collective-permute-start(bf16[128,8,128]{2,1,0:T(8,128)(2,1)} %bitcast.51), channel_id=1, source_target_pairs={{0,1},{1,2},{2,3},{3,0},{4,5},{5,6},{6,7},{7,4},{8,9},{9,10},{10,1... | collective-permute-start | bytes 786440 | tf_op jit(solution)/shard_map/ppermute | solution.py:250
  49.9 1.9 %collective-permute-start.13 = (bf16[2,128,8,128]{3,2,1,0:T(8,128)(2,1)S(1)}, bf16[2,128,8,128]{3,2,1,0:T(8,128)(2,1)S(1)}, u32[]{:S(2)}, u32[]{:S(2)}) collective-permute-start(bf16[2,128,8,128]{3,2,1,0:T(8,128)(2,1)S(1)} %get-tuple-element.14), channel_id=1, source_target_pairs={{0,64},{1,65},{2,66},{3,67},{4,68},{5,69},{6,70},{7,71},{8,72},{9,... | collective-permute-start | bytes 1572872 | tf_op jit(solution)/shard_map/ppermute | solution.py:250
  51.8 15.1 %collective-permute-done.3 = bf16[128,8,128]{2,1,0:T(8,128)(2,1)S(1)} collective-permute-done((bf16[128,8,128]{2,1,0:T(8,128)(2,1)}, bf16[128,8,128]{2,1,0:T(8,128)(2,1)S(1)}, u32[]{:S(2)}, u32[]{:S(2)}) %collective-permute-start.3) | collective-permute-done | bytes 262176 | tf_op jit(solution)/shard_map/ppermute | solution.py:250
  67.0 4.8 %collective-permute-start.7 = (bf16[2,128,8,128]{3,2,1,0:T(8,128)(2,1)S(1)}, bf16[2,128,8,128]{3,2,1,0:T(8,128)(2,1)}, u32[]{:S(2)}, u32[]{:S(2)}) collective-permute-start(bf16[2,128,8,128]{3,2,1,0:T(8,128)(2,1)S(1)} %pad_maximum_fusion.3.refs_3_), channel_id=1, source_target_pairs={{0,12},{1,13},{2,14},{3,15},{4,0},{5,1},{6,2},{7,3},{8,4},{9,5},{1... | collective-permute-start | bytes 1572872 | tf_op jit(solution)/shard_map/ppermute | solution.py:250
  72.8 1.9 %collective-permute-start.4 = (bf16[2,128,8,128]{3,2,1,0:T(8,128)(2,1)S(1)}, bf16[2,128,8,128]{3,2,1,0:T(8,128)(2,1)}, u32[]{:S(2)}, u32[]{:S(2)}) collective-permute-start(bf16[2,128,8,128]{3,2,1,0:T(8,128)(2,1)S(1)} %pad_maximum_fusion.2.refs_2_), channel_id=1, source_target_pairs={{0,4},{1,5},{2,6},{3,7},{4,8},{5,9},{6,10},{7,11},{8,12},{9,13},{1... | collective-permute-start | bytes 1572872 | tf_op jit(solution)/shard_map/ppermute | solution.py:250
  74.8 3.3 %collective-permute-start.16 = (bf16[2,128,8,128]{3,2,1,0:T(8,128)(2,1)S(1)}, bf16[2,128,8,128]{3,2,1,0:T(8,128)(2,1)S(1)}, u32[]{:S(2)}, u32[]{:S(2)}) collective-permute-start(bf16[2,128,8,128]{3,2,1,0:T(8,128)(2,1)S(1)} %collective-permute-done.14.refs_14_), channel_id=1, source_target_pairs={{0,448},{1,449},{2,450},{3,451},{4,452},{5,453},{6,454},{7,455},{8... | collective-permute-start | bytes 1572872 | tf_op jit(solution)/shard_map/ppermute | solution.py:250
  78.1 2.1 %collective-permute-start.5 = (bf16[2,128,8,128]{3,2,1,0:T(8,128)(2,1)S(1)}, bf16[2,128,8,128]{3,2,1,0:T(8,128)(2,1)S(1)}, u32[]{:S(2)}, u32[]{:S(2)}) collective-permute-start(bf16[2,128,8,128]{3,2,1,0:T(8,128)(2,1)S(1)} %pad_maximum_fusion.3.refs_3_), channel_id=1, source_target_pairs={{0,4},{1,5},{2,6},{3,7},{4,8},{5,9},{6,10},{7,11},{8,12},{9,13},{1... | collective-permute-start | bytes 1572872 | tf_op jit(solution)/shard_map/ppermute | solution.py:250
  80.2 2.0 %collective-permute-start.15 = (bf16[2,128,8,128]{3,2,1,0:T(8,128)(2,1)S(1)}, bf16[2,128,8,128]{3,2,1,0:T(8,128)(2,1)}, u32[]{:S(2)}, u32[]{:S(2)}) collective-permute-start(bf16[2,128,8,128]{3,2,1,0:T(8,128)(2,1)S(1)} %collective-permute-done.13.refs_13_), channel_id=1, source_target_pairs={{0,64},{1,65},{2,66},{3,67},{4,68},{5,69},{6,70},{7,71},{8,72},{9,... | collective-permute-start | bytes 1572872 | tf_op jit(solution)/shard_map/ppermute | solution.py:250
  82.2 4.4 %collective-permute-start.6 = (bf16[2,128,8,128]{3,2,1,0:T(8,128)(2,1)S(1)}, bf16[2,128,8,128]{3,2,1,0:T(8,128)(2,1)}, u32[]{:S(2)}, u32[]{:S(2)}) collective-permute-start(bf16[2,128,8,128]{3,2,1,0:T(8,128)(2,1)S(1)} %pad_maximum_fusion.2.refs_2_), channel_id=1, source_target_pairs={{0,12},{1,13},{2,14},{3,15},{4,0},{5,1},{6,2},{7,3},{8,4},{9,5},{1... | collective-permute-start | bytes 1572872 | tf_op jit(solution)/shard_map/ppermute | solution.py:250
  87.2 2.8 %collective-permute-start.9 = (bf16[2,128,8,128]{3,2,1,0:T(8,128)(2,1)}, bf16[2,128,8,128]{3,2,1,0:T(8,128)(2,1)}, u32[]{:S(2)}, u32[]{:S(2)}) collective-permute-start(bf16[2,128,8,128]{3,2,1,0:T(8,128)(2,1)} %collective-permute-done.7.refs_7_), channel_id=1, source_target_pairs={{0,12},{1,13},{2,14},{3,15},{4,0},{5,1},{6,2},{7,3},{8,4},{9,5},{1... | collective-permute-start | bytes 1572872 | tf_op jit(solution)/shard_map/ppermute | solution.py:250
  90.0 2.5 %collective-permute-start.8 = (bf16[2,128,8,128]{3,2,1,0:T(8,128)(2,1)}, bf16[2,128,8,128]{3,2,1,0:T(8,128)(2,1)}, u32[]{:S(2)}, u32[]{:S(2)}) collective-permute-start(bf16[2,128,8,128]{3,2,1,0:T(8,128)(2,1)} %collective-permute-done.4.refs_4_), channel_id=1, source_target_pairs={{0,4},{1,5},{2,6},{3,7},{4,8},{5,9},{6,10},{7,11},{8,12},{9,13},{1... | collective-permute-start | bytes 1572872 | tf_op jit(solution)/shard_map/ppermute | solution.py:250
  92.6 5.8 %collective-permute-done.5.refs_5_ = bf16[2,128,8,128]{3,2,1,0:T(8,128)(2,1)S(1)} collective-permute-done((bf16[2,128,8,128]{3,2,1,0:T(8,128)(2,1)S(1)}, bf16[2,128,8,128]{3,2,1,0:T(8,128)(2,1)S(1)}, u32[]{:S(2)}, u32[]{:S(2)}) %collective-permute-start.5) | collective-permute-done | bytes 524320 | tf_op jit(solution)/shard_map/ppermute | solution.py:250
  98.4 3.3 %collective-permute-start.18 = (bf16[128,8,128]{2,1,0:T(8,128)(2,1)S(1)}, bf16[128,8,128]{2,1,0:T(8,128)(2,1)}, u32[]{:S(2)}, u32[]{:S(2)}) collective-permute-start(bf16[128,8,128]{2,1,0:T(8,128)(2,1)S(1)} %slice_bitcast_fusion), channel_id=1, source_target_pairs={{0,448},{1,449},{2,450},{3,451},{4,452},{5,453},{6,454},{7,455},{8... | collective-permute-start | bytes 786440 | tf_op jit(solution)/shard_map/ppermute | solution.py:250
  101.7 2.0 %collective-permute-start.17 = (bf16[2,128,8,128]{3,2,1,0:T(8,128)(2,1)}, bf16[2,128,8,128]{3,2,1,0:T(8,128)(2,1)}, u32[]{:S(2)}, u32[]{:S(2)}) collective-permute-start(bf16[2,128,8,128]{3,2,1,0:T(8,128)(2,1)} %collective-permute-done.15.refs_15_), channel_id=1, source_target_pairs={{0,64},{1,65},{2,66},{3,67},{4,68},{5,69},{6,70},{7,71},{8,72},{9,... | collective-permute-start | bytes 1572872 | tf_op jit(solution)/shard_map/ppermute | solution.py:250
  103.7 2.2 %collective-permute-done.18.refs_18_ = bf16[128,8,128]{2,1,0:T(8,128)(2,1)} collective-permute-done((bf16[128,8,128]{2,1,0:T(8,128)(2,1)S(1)}, bf16[128,8,128]{2,1,0:T(8,128)(2,1)}, u32[]{:S(2)}, u32[]{:S(2)}) %collective-permute-start.18) | collective-permute-done | bytes 262176 | tf_op jit(solution)/shard_map/ppermute | solution.py:250
  105.9 4.5 %collective-permute-start.19 = (bf16[128,8,128]{2,1,0:T(8,128)(2,1)}, bf16[128,8,128]{2,1,0:T(8,128)(2,1)}, u32[]{:S(2)}, u32[]{:S(2)}) collective-permute-start(bf16[128,8,128]{2,1,0:T(8,128)(2,1)} %collective-permute-done.18.refs_18_), channel_id=1, source_target_pairs={{0,448},{1,449},{2,450},{3,451},{4,452},{5,453},{6,454},{7,455},{8... | collective-permute-start | bytes 786440 | tf_op jit(solution)/shard_map/ppermute | solution.py:250
  112.0 3.1 %collective-permute-done.19.refs_19_ = bf16[128,8,128]{2,1,0:T(8,128)(2,1)} collective-permute-done((bf16[128,8,128]{2,1,0:T(8,128)(2,1)}, bf16[128,8,128]{2,1,0:T(8,128)(2,1)}, u32[]{:S(2)}, u32[]{:S(2)}) %collective-permute-start.19) | collective-permute-done | bytes 262176 | tf_op jit(solution)/shard_map/ppermute | solution.py:250
  115.1 14.6 %cross.1 = (bf16[64,128,128]{2,1,0:T(8,128)(2,1)}, f32[64,128,128]{2,1,0:T(8,128)}) custom-call(s32[32]{0:T(128)} %stack.162.refs_0_, s32[1]{0:T(128)} %bitcast.32.core_ref.refs_1_, bf16[2,128,8,128]{3,2,1,0:T(8,128)(2,1)} %copy-done.1, bf16[2,128,8,128]{3,2,1,0:T(8,128)(2,1)} %copy-done, bf16[2,128,8,128]{3,2,1,0:T(8,128)(2,1)} %collective-permute-done.4.refs_4_, ...), custom_call_target="tpu_custom_call" | custom-call | tf_op jit(solution)/shard_map/cross/pallas_call | solution.py:209
  129.7 9.5 %collective-permute-start.20 = (bf16[64,128,128]{2,1,0:T(8,128)(2,1)}, bf16[64,128,128]{2,1,0:T(8,128)(2,1)S(1)}, u32[]{:S(2)}, u32[]{:S(2)}) collective-permute-start(bf16[64,128,128]{2,1,0:T(8,128)(2,1)} %get-tuple-element.12), channel_id=1, source_target_pairs={{0,16},{1,17},{2,18},{3,19},{4,20},{5,21},{6,22},{7,23},{8,24},{9,... | collective-permute-start | bytes 6291464 | tf_op jit(solution)/shard_map/ppermute | solution.py:250
  139.3 3.9 %collective-permute-done.20 = bf16[64,128,128]{2,1,0:T(8,128)(2,1)S(1)} collective-permute-done((bf16[64,128,128]{2,1,0:T(8,128)(2,1)}, bf16[64,128,128]{2,1,0:T(8,128)(2,1)S(1)}, u32[]{:S(2)}, u32[]{:S(2)}) %collective-permute-start.20) | collective-permute-done | bytes 2097184 | tf_op jit(solution)/shard_map/ppermute | solution.py:250
  143.2 4.8 %select_convert_fusion = bf16[64,128,128]{2,1,0:T(8,128)(2,1)} fusion(f32[64,128,128]{2,1,0:T(8,128)} %get-tuple-element.11, bf16[64,128,128]{2,1,0:T(8,128)(2,1)S(1)} %collective-permute-done.20, pred[64,128]{1,0:T(8,128)(4,1)S(1)} %broadcast_compare_fusion), kind=kLoop, calls=%fused_computation | loop fusion | flops 4194304 | bytes 8396800 | tf_op jit(solution)/shard_map/convert_element_type | solution.py:305
  (45 shorter events, 5.0 us)
Async XLA Ops:
  0.0 111.3 %copy-start.10 = (bf16[2,128,256]{2,1,0:T(8,128)(2,1)S(1)}, bf16[2,128,256]{2,1,0:T(8,128)(2,1)}, u32[]{:S(2)}) copy-start(bf16[2,128,256]{2,1,0:T(8,128)(2,1)} %constant.221.clone) | copy-start | bytes 393220
  3.7 9.9 %collective-permute-start = (bf16[512,128]{1,0:T(8,128)(2,1)}, bf16[512,128]{1,0:T(8,128)(2,1)S(1)}, u32[]{:S(2)}, u32[]{:S(2)}) collective-permute-start(bf16[512,128]{1,0:T(8,128)(2,1)} %get-tuple-element.10), channel_id=1, source_target_pairs={{0,16},{1,17},{2,18},{3,19},{4,20},{5,21},{6,22},{7,23},{8,24},{9,... | collective-permute-start | bytes 393224 | tf_op jit(solution)/shard_map/ppermute | solution.py:250
  13.6 0.6 copy-start.9
  16.0 12.3 %collective-permute-start.10 = (bf16[128,8,128]{2,1,0:T(8,128)(2,1)}, bf16[128,8,128]{2,1,0:T(8,128)(2,1)S(1)}, u32[]{:S(2)}, u32[]{:S(2)}) collective-permute-start(bf16[128,8,128]{2,1,0:T(8,128)(2,1)} %bitcast.46), channel_id=1, source_target_pairs={{0,64},{1,65},{2,66},{3,67},{4,68},{5,69},{6,70},{7,71},{8,72},{9,... | collective-permute-start | bytes 786440 | tf_op jit(solution)/shard_map/ppermute | solution.py:250
  17.9 14.1 %collective-permute-start.12 = (bf16[128,8,128]{2,1,0:T(8,128)(2,1)}, bf16[128,8,128]{2,1,0:T(8,128)(2,1)S(1)}, u32[]{:S(2)}, u32[]{:S(2)}) collective-permute-start(bf16[128,8,128]{2,1,0:T(8,128)(2,1)} %bitcast.47), channel_id=1, source_target_pairs={{0,32},{1,33},{2,34},{3,35},{4,36},{5,37},{6,38},{7,39},{8,40},{9,... | collective-permute-start | bytes 786440 | tf_op jit(solution)/shard_map/ppermute | solution.py:250
  24.5 9.1 %collective-permute-start.11 = (bf16[128,8,128]{2,1,0:T(8,128)(2,1)}, bf16[128,8,128]{2,1,0:T(8,128)(2,1)S(1)}, u32[]{:S(2)}, u32[]{:S(2)}) collective-permute-start(bf16[128,8,128]{2,1,0:T(8,128)(2,1)} %bitcast.48), channel_id=1, source_target_pairs={{0,448},{1,449},{2,450},{3,451},{4,452},{5,453},{6,454},{7,455},{8... | collective-permute-start | bytes 786440 | tf_op jit(solution)/shard_map/ppermute | solution.py:250
  28.4 86.7 %copy-start.3 = (bf16[128,8,128]{2,1,0:T(8,128)(2,1)}, bf16[128,8,128]{2,1,0:T(8,128)(2,1)S(1)}, u32[]{:S(2)}) copy-start(bf16[128,8,128]{2,1,0:T(8,128)(2,1)S(1)} %collective-permute-done.10.refs_11_) | copy-start | bytes 786436
  32.1 83.0 %copy-start.4 = (bf16[128,8,128]{2,1,0:T(8,128)(2,1)}, bf16[128,8,128]{2,1,0:T(8,128)(2,1)S(1)}, u32[]{:S(2)}) copy-start(bf16[128,8,128]{2,1,0:T(8,128)(2,1)S(1)} %collective-permute-done.12.refs_20_) | copy-start | bytes 786436
  33.7 81.4 %copy-start.5 = (bf16[128,8,128]{2,1,0:T(8,128)(2,1)}, bf16[128,8,128]{2,1,0:T(8,128)(2,1)S(1)}, u32[]{:S(2)}) copy-start(bf16[128,8,128]{2,1,0:T(8,128)(2,1)S(1)} %collective-permute-done.11.refs_12_) | copy-start | bytes 786436
  33.7 41.0 %collective-permute-start.14 = (bf16[2,128,8,128]{3,2,1,0:T(8,128)(2,1)S(1)}, bf16[2,128,8,128]{3,2,1,0:T(8,128)(2,1)S(1)}, u32[]{:S(2)}, u32[]{:S(2)}) collective-permute-start(bf16[2,128,8,128]{3,2,1,0:T(8,128)(2,1)S(1)} %get-tuple-element.13), channel_id=1, source_target_pairs={{0,448},{1,449},{2,450},{3,451},{4,452},{5,453},{6,454},{7,455},{8... | collective-permute-start | bytes 1572872 | tf_op jit(solution)/shard_map/ppermute | solution.py:250
  39.0 12.9 %collective-permute-start.2 = (bf16[128,8,128]{2,1,0:T(8,128)(2,1)}, bf16[128,8,128]{2,1,0:T(8,128)(2,1)S(1)}, u32[]{:S(2)}, u32[]{:S(2)}) collective-permute-start(bf16[128,8,128]{2,1,0:T(8,128)(2,1)} %bitcast.49), channel_id=1, source_target_pairs={{0,3},{1,0},{2,1},{3,2},{4,7},{5,4},{6,5},{7,6},{8,11},{9,8},{10,9... | collective-permute-start | bytes 786440 | tf_op jit(solution)/shard_map/ppermute | solution.py:250
  43.9 23.0 %collective-permute-start.3 = (bf16[128,8,128]{2,1,0:T(8,128)(2,1)}, bf16[128,8,128]{2,1,0:T(8,128)(2,1)S(1)}, u32[]{:S(2)}, u32[]{:S(2)}) collective-permute-start(bf16[128,8,128]{2,1,0:T(8,128)(2,1)} %bitcast.50), channel_id=1, source_target_pairs={{0,2},{1,3},{2,0},{3,1},{4,6},{5,7},{6,4},{7,5},{8,10},{9,11},{10,... | collective-permute-start | bytes 786440 | tf_op jit(solution)/shard_map/ppermute | solution.py:250
  46.8 25.0 %collective-permute-start.1 = (bf16[128,8,128]{2,1,0:T(8,128)(2,1)}, bf16[128,8,128]{2,1,0:T(8,128)(2,1)S(1)}, u32[]{:S(2)}, u32[]{:S(2)}) collective-permute-start(bf16[128,8,128]{2,1,0:T(8,128)(2,1)} %bitcast.51), channel_id=1, source_target_pairs={{0,1},{1,2},{2,3},{3,0},{4,5},{5,6},{6,7},{7,4},{8,9},{9,10},{10,1... | collective-permute-start | bytes 786440 | tf_op jit(solution)/shard_map/ppermute | solution.py:250
  49.9 30.3 %collective-permute-start.13 = (bf16[2,128,8,128]{3,2,1,0:T(8,128)(2,1)S(1)}, bf16[2,128,8,128]{3,2,1,0:T(8,128)(2,1)S(1)}, u32[]{:S(2)}, u32[]{:S(2)}) collective-permute-start(bf16[2,128,8,128]{3,2,1,0:T(8,128)(2,1)S(1)} %get-tuple-element.14), channel_id=1, source_target_pairs={{0,64},{1,65},{2,66},{3,67},{4,68},{5,69},{6,70},{7,71},{8,72},{9,... | collective-permute-start | bytes 1572872 | tf_op jit(solution)/shard_map/ppermute | solution.py:250
  67.0 48.1 %copy-start = (bf16[2,128,8,128]{3,2,1,0:T(8,128)(2,1)}, bf16[2,128,8,128]{3,2,1,0:T(8,128)(2,1)S(1)}, u32[]{:S(2)}) copy-start(bf16[2,128,8,128]{3,2,1,0:T(8,128)(2,1)S(1)} %pad_maximum_fusion.3.refs_3_) | copy-start | bytes 1572868
  67.0 15.2 %collective-permute-start.7 = (bf16[2,128,8,128]{3,2,1,0:T(8,128)(2,1)S(1)}, bf16[2,128,8,128]{3,2,1,0:T(8,128)(2,1)}, u32[]{:S(2)}, u32[]{:S(2)}) collective-permute-start(bf16[2,128,8,128]{3,2,1,0:T(8,128)(2,1)S(1)} %pad_maximum_fusion.3.refs_3_), channel_id=1, source_target_pairs={{0,12},{1,13},{2,14},{3,15},{4,0},{5,1},{6,2},{7,3},{8,4},{9,5},{1... | collective-permute-start | bytes 1572872 | tf_op jit(solution)/shard_map/ppermute | solution.py:250
  72.8 42.3 %copy-start.1 = (bf16[2,128,8,128]{3,2,1,0:T(8,128)(2,1)}, bf16[2,128,8,128]{3,2,1,0:T(8,128)(2,1)S(1)}, u32[]{:S(2)}) copy-start(bf16[2,128,8,128]{3,2,1,0:T(8,128)(2,1)S(1)} %pad_maximum_fusion.2.refs_2_) | copy-start | bytes 1572868
  72.8 14.4 %collective-permute-start.4 = (bf16[2,128,8,128]{3,2,1,0:T(8,128)(2,1)S(1)}, bf16[2,128,8,128]{3,2,1,0:T(8,128)(2,1)}, u32[]{:S(2)}, u32[]{:S(2)}) collective-permute-start(bf16[2,128,8,128]{3,2,1,0:T(8,128)(2,1)S(1)} %pad_maximum_fusion.2.refs_2_), channel_id=1, source_target_pairs={{0,4},{1,5},{2,6},{3,7},{4,8},{5,9},{6,10},{7,11},{8,12},{9,13},{1... | collective-permute-start | bytes 1572872 | tf_op jit(solution)/shard_map/ppermute | solution.py:250
  74.8 40.3 %copy-start.6 = (bf16[2,128,8,128]{3,2,1,0:T(8,128)(2,1)}, bf16[2,128,8,128]{3,2,1,0:T(8,128)(2,1)S(1)}, u32[]{:S(2)}) copy-start(bf16[2,128,8,128]{3,2,1,0:T(8,128)(2,1)S(1)} %collective-permute-done.14.refs_14_) | copy-start | bytes 1572868
  74.8 15.2 %collective-permute-start.16 = (bf16[2,128,8,128]{3,2,1,0:T(8,128)(2,1)S(1)}, bf16[2,128,8,128]{3,2,1,0:T(8,128)(2,1)S(1)}, u32[]{:S(2)}, u32[]{:S(2)}) collective-permute-start(bf16[2,128,8,128]{3,2,1,0:T(8,128)(2,1)S(1)} %collective-permute-done.14.refs_14_), channel_id=1, source_target_pairs={{0,448},{1,449},{2,450},{3,451},{4,452},{5,453},{6,454},{7,455},{8... | collective-permute-start | bytes 1572872 | tf_op jit(solution)/shard_map/ppermute | solution.py:250
  78.1 20.3 %collective-permute-start.5 = (bf16[2,128,8,128]{3,2,1,0:T(8,128)(2,1)S(1)}, bf16[2,128,8,128]{3,2,1,0:T(8,128)(2,1)S(1)}, u32[]{:S(2)}, u32[]{:S(2)}) collective-permute-start(bf16[2,128,8,128]{3,2,1,0:T(8,128)(2,1)S(1)} %pad_maximum_fusion.3.refs_3_), channel_id=1, source_target_pairs={{0,4},{1,5},{2,6},{3,7},{4,8},{5,9},{6,10},{7,11},{8,12},{9,13},{1... | collective-permute-start | bytes 1572872 | tf_op jit(solution)/shard_map/ppermute | solution.py:250
  80.2 34.9 %copy-start.7 = (bf16[2,128,8,128]{3,2,1,0:T(8,128)(2,1)}, bf16[2,128,8,128]{3,2,1,0:T(8,128)(2,1)S(1)}, u32[]{:S(2)}) copy-start(bf16[2,128,8,128]{3,2,1,0:T(8,128)(2,1)S(1)} %collective-permute-done.13.refs_13_) | copy-start | bytes 1572868
  80.2 21.4 %collective-permute-start.15 = (bf16[2,128,8,128]{3,2,1,0:T(8,128)(2,1)S(1)}, bf16[2,128,8,128]{3,2,1,0:T(8,128)(2,1)}, u32[]{:S(2)}, u32[]{:S(2)}) collective-permute-start(bf16[2,128,8,128]{3,2,1,0:T(8,128)(2,1)S(1)} %collective-permute-done.13.refs_13_), channel_id=1, source_target_pairs={{0,64},{1,65},{2,66},{3,67},{4,68},{5,69},{6,70},{7,71},{8,72},{9,... | collective-permute-start | bytes 1572872 | tf_op jit(solution)/shard_map/ppermute | solution.py:250
  82.2 29.7 %collective-permute-start.6 = (bf16[2,128,8,128]{3,2,1,0:T(8,128)(2,1)S(1)}, bf16[2,128,8,128]{3,2,1,0:T(8,128)(2,1)}, u32[]{:S(2)}, u32[]{:S(2)}) collective-permute-start(bf16[2,128,8,128]{3,2,1,0:T(8,128)(2,1)S(1)} %pad_maximum_fusion.2.refs_2_), channel_id=1, source_target_pairs={{0,12},{1,13},{2,14},{3,15},{4,0},{5,1},{6,2},{7,3},{8,4},{9,5},{1... | collective-permute-start | bytes 1572872 | tf_op jit(solution)/shard_map/ppermute | solution.py:250
  87.2 24.7 %collective-permute-start.9 = (bf16[2,128,8,128]{3,2,1,0:T(8,128)(2,1)}, bf16[2,128,8,128]{3,2,1,0:T(8,128)(2,1)}, u32[]{:S(2)}, u32[]{:S(2)}) collective-permute-start(bf16[2,128,8,128]{3,2,1,0:T(8,128)(2,1)} %collective-permute-done.7.refs_7_), channel_id=1, source_target_pairs={{0,12},{1,13},{2,14},{3,15},{4,0},{5,1},{6,2},{7,3},{8,4},{9,5},{1... | collective-permute-start | bytes 1572872 | tf_op jit(solution)/shard_map/ppermute | solution.py:250
  90.0 25.1 %copy-start.2 = (bf16[2,128,8,128]{3,2,1,0:T(8,128)(2,1)}, bf16[2,128,8,128]{3,2,1,0:T(8,128)(2,1)S(1)}, u32[]{:S(2)}) copy-start(bf16[2,128,8,128]{3,2,1,0:T(8,128)(2,1)S(1)} %collective-permute-done.16.refs_16_) | copy-start | bytes 1572868
  90.0 21.9 %collective-permute-start.8 = (bf16[2,128,8,128]{3,2,1,0:T(8,128)(2,1)}, bf16[2,128,8,128]{3,2,1,0:T(8,128)(2,1)}, u32[]{:S(2)}, u32[]{:S(2)}) collective-permute-start(bf16[2,128,8,128]{3,2,1,0:T(8,128)(2,1)} %collective-permute-done.4.refs_4_), channel_id=1, source_target_pairs={{0,4},{1,5},{2,6},{3,7},{4,8},{5,9},{6,10},{7,11},{8,12},{9,13},{1... | collective-permute-start | bytes 1572872 | tf_op jit(solution)/shard_map/ppermute | solution.py:250
  98.4 3.3 %copy-start.8 = (bf16[2,128,8,128]{3,2,1,0:T(8,128)(2,1)}, bf16[2,128,8,128]{3,2,1,0:T(8,128)(2,1)S(1)}, u32[]{:S(2)}) copy-start(bf16[2,128,8,128]{3,2,1,0:T(8,128)(2,1)S(1)} %collective-permute-done.5.refs_5_) | copy-start | bytes 1572868
  98.4 7.5 %collective-permute-start.18 = (bf16[128,8,128]{2,1,0:T(8,128)(2,1)S(1)}, bf16[128,8,128]{2,1,0:T(8,128)(2,1)}, u32[]{:S(2)}, u32[]{:S(2)}) collective-permute-start(bf16[128,8,128]{2,1,0:T(8,128)(2,1)S(1)} %slice_bitcast_fusion), channel_id=1, source_target_pairs={{0,448},{1,449},{2,450},{3,451},{4,452},{5,453},{6,454},{7,455},{8... | collective-permute-start | bytes 786440 | tf_op jit(solution)/shard_map/ppermute | solution.py:250
  101.7 13.4 %collective-permute-start.17 = (bf16[2,128,8,128]{3,2,1,0:T(8,128)(2,1)}, bf16[2,128,8,128]{3,2,1,0:T(8,128)(2,1)}, u32[]{:S(2)}, u32[]{:S(2)}) collective-permute-start(bf16[2,128,8,128]{3,2,1,0:T(8,128)(2,1)} %collective-permute-done.15.refs_15_), channel_id=1, source_target_pairs={{0,64},{1,65},{2,66},{3,67},{4,68},{5,69},{6,70},{7,71},{8,72},{9,... | collective-permute-start | bytes 1572872 | tf_op jit(solution)/shard_map/ppermute | solution.py:250
  105.9 9.2 %collective-permute-start.19 = (bf16[128,8,128]{2,1,0:T(8,128)(2,1)}, bf16[128,8,128]{2,1,0:T(8,128)(2,1)}, u32[]{:S(2)}, u32[]{:S(2)}) collective-permute-start(bf16[128,8,128]{2,1,0:T(8,128)(2,1)} %collective-permute-done.18.refs_18_), channel_id=1, source_target_pairs={{0,448},{1,449},{2,450},{3,451},{4,452},{5,453},{6,454},{7,455},{8... | collective-permute-start | bytes 786440 | tf_op jit(solution)/shard_map/ppermute | solution.py:250
  129.7 13.5 %collective-permute-start.20 = (bf16[64,128,128]{2,1,0:T(8,128)(2,1)}, bf16[64,128,128]{2,1,0:T(8,128)(2,1)S(1)}, u32[]{:S(2)}, u32[]{:S(2)}) collective-permute-start(bf16[64,128,128]{2,1,0:T(8,128)(2,1)} %get-tuple-element.12), channel_id=1, source_target_pairs={{0,16},{1,17},{2,18},{3,19},{4,20},{5,21},{6,22},{7,23},{8,24},{9,... | collective-permute-start | bytes 6291464 | tf_op jit(solution)/shard_map/ppermute | solution.py:250
where the time goes:
time: 149 us; the launch traced here: 148 us
  starting transfers between devices  82.1 us (55%)
  waiting for transfers between devices  37.1 us (25%)
  Pallas kernels  20 us (13%)
  other arithmetic  6.02 us (4%)
  local copies, waits for them, and re-layouts  1.96 us (1%)
    ppermute x21, starting transfers between devices, move(): return lax.ppermute(value, AXES, pairs)  82.1 us
    ppermute x21, waiting for transfers between devices, move(): return lax.ppermute(value, AXES, pairs)  37.1 us
    pallas_call x1, Pallas kernels, cross(): pl.pallas_call(kernel, out_shape=(jax.ShapeDtypeStruct((64, 128, LAGS), j...  14.6 us
    convert_element_type x1, other arithmetic, correlate(): return corr.astype(jnp.bfloat16)  4.8 us
    pallas_call x1, Pallas kernels, whiten(): pl.pallas_call(whiten_kernel, out_shape=(shape, shape), in_specs=[smem, s...  3.72 us
  transfers between devices with their start and end apart: 21, of which 9 were waited for; matrix products, arithmetic and copies ran while one was open for 2% of the time, Pallas kernels for 0%

commit v1 on v0

--- a/solution.py
+++ b/solution.py
@@ -49,7 +49,7 @@
     return dft, near, np.stack(inverse)
 
 
-def whiten_kernel(flags_ref, core_ref, x_ref, dft_ref, near_ref, keep_ref, send_ref, rows_ref):
+def whiten_kernel(flags_ref, x_ref, dft_ref, near_ref, keep_ref, send_ref, rows_ref):
     x = x_ref[...]
     spectra = None
     for part in (2, 1, 0):
@@ -80,29 +80,29 @@
         rows_ref[pl.ds(2 * pair, F, stride=4), :] = jnp.where(low, re2, pltpu.roll(im2, NW, 1))
         rows_ref[pl.ds(2 * pair + 1, F, stride=4), :] = jnp.where(low, pltpu.roll(re2, NW, 1), im2)
     size = HALF * 4
-    core = core_ref[0]
+    core = lax.axis_index("row") % N_C
     keep_ref[...] = rows_ref[pl.ds(pl.multiple_of(core * size, size), size), :].astype(jnp.bfloat16)
     send_ref[...] = rows_ref[pl.ds(pl.multiple_of((1 - core) * size, size), size), :].astype(jnp.bfloat16)
 
 
-def whiten(traces, live_flags, core, dft, near):
+def whiten(traces, live_flags, dft, near):
     vmem = pl.BlockSpec(memory_space=pltpu.VMEM)
     smem = pl.BlockSpec(memory_space=pltpu.SMEM)
     shape = jax.ShapeDtypeStruct((HALF * 4, 2 * NW), jnp.bfloat16)
     return pl.pallas_call(
         whiten_kernel,
         out_shape=(shape, shape),
-        in_specs=[smem, smem, vmem, vmem, vmem],
+        in_specs=[smem, vmem, vmem, vmem],
         out_specs=(vmem, vmem),
         scratch_shapes=[pltpu.VMEM((F * 4, 2 * NW), jnp.float32)],
         name="whiten",
-    )(live_flags, core, traces.reshape(4 * NW, SAMP), dft, near)
-
-
-def merge_kernel(core_ref, keep_ref, got_ref, out_ref):
+    )(live_flags, traces.reshape(4 * NW, SAMP), dft, near)
+
+
+def merge_kernel(keep_ref, got_ref, out_ref):
     keep = keep_ref[...].astype(jnp.float32).reshape(HALF // 2, 8, 2 * NW)
     got = got_ref[...].astype(jnp.float32).reshape(HALF // 2, 8, 2 * NW)
-    first = core_ref[0] == 0
+    first = lax.axis_index("row") % N_C == 0
     a = jnp.where(first, keep, got)
     b = jnp.where(first, got, keep)
     low = lax.broadcasted_iota(jnp.int32, (HALF // 2, 8, 2 * NW), 1) < 4
@@ -112,15 +112,15 @@
     out_ref[...] = both.reshape(PIECE, 2 * NW).astype(jnp.bfloat16)
 
 
-def merge(core, keep, got):
+def merge(keep, got):
     vmem = pl.BlockSpec(memory_space=pltpu.VMEM)
     return pl.pallas_call(
         merge_kernel,
         out_shape=jax.ShapeDtypeStruct((PIECE, 2 * NW), jnp.bfloat16),
-        in_specs=[pl.BlockSpec(memory_space=pltpu.SMEM), vmem, vmem],
+        in_specs=[vmem, vmem],
         out_specs=vmem,
         name="merge",
-    )(core, keep, got)
+    )(keep, got)
 
 
 N_CHUNK = 4
@@ -128,28 +128,47 @@
 CHUNK = HALF // N_CHUNK
 
 
-def cross_kernel(n_first, n_second, where_ref, core_ref, *refs):
+def placements():
+    row, col = lax.axis_index("row"), lax.axis_index("col")
+    y, h = row // 4, row // 2 % 2
+    x, l = col // N_L, col % N_L
+    firsts = []
+    for d in (0, -1, 1, 2):
+        firsts += [(x + d) % N_X * N_L + (l + q) % N_L for q in (0, 3, 1, 2)]
+    spot = lambda d, mine: (y + d) % N_Y * N_H + (h if mine else 1 - h)
+    seconds = [spot(0, True), spot(0, False), spot(-1, True)]
+    for d in (1, 2, 3):
+        seconds += [spot(-d - 1, True), spot(-d, False)]
+    for d in (1, 2, 3):
+        seconds += [spot(d, True), spot(d, False)]
+    seconds += [spot(4, False)]
+    return row, col, firsts + seconds
+
+
+def cross_kernel(n_first, n_second, *refs):
+    row, col, where = placements()
+    core = row % N_C
     n_in = len(n_first) + len(n_second)
     inputs = refs[:n_in]
     inv_ref, send_ref, own_ref, a_ref, b_ref, s_ref, sem = refs[n_in:]
     copies = []
     for chunk in range(N_CHUNK):
-        row = []
+        started = []
         slot = 0
         for index, ref in enumerate(inputs):
             count = (n_first + n_second)[index]
             dst = a_ref if index < len(n_first) else b_ref
             for piece in range(count):
                 src = ref.at[piece] if count > 1 else ref
-                place = pl.multiple_of(where_ref[slot] * 8, 8)
+                place = pl.multiple_of(where[slot] * 8, 8)
                 bins = pl.ds(chunk * CHUNK, CHUNK)
                 copy = pltpu.make_async_copy(
                     src.at[bins], dst.at[bins, pl.ds(place, 8), :], sem.at[chunk, slot]
                 )
                 copy.start()
-                row.append(copy)
+                started.append(copy)
                 slot += 1
-        copies.append(row)
+        copies.append(started)
     sign = jnp.where(
         lax.broadcasted_iota(jnp.int32, (128, 2 * NW), 1) < NW, 1.0, -1.0
     ).astype(jnp.bfloat16)
@@ -170,8 +189,14 @@
             copy.wait()
         lax.fori_loop(chunk * CHUNK, (chunk + 1) * CHUNK, one_bin, 0, unroll=16)
 
-    core = core_ref[0]
-    table = inv_ref[...]
+    lane = lax.broadcasted_iota(jnp.int32, (2 * HALF, 128), 1)
+    for side in range(N_C):
+        for ch in range(4):
+            start = pl.multiple_of((col * 8 + side * 4 + ch) * PITCH, 8)
+            same = lane == (row - core + side) * 4 + ch
+            stacked = s_ref[pl.ds(start, 2 * HALF), :]
+            s_ref[pl.ds(start, 2 * HALF), :] = jnp.where(same, 0.0, stacked)
+    table = inv_ref[core]
 
     def lag_pair(step, which, out_ref):
         piece, half = step // 2, step % 2
@@ -197,22 +222,21 @@
     lax.fori_loop(0, 32, own_step, 0, unroll=8)
 
 
-def cross(where, core, firsts, seconds, inverse):
+def cross(firsts, seconds, inverse):
     count = lambda x: 1 if x.ndim == 3 else x.shape[0]
     n_first = tuple(count(x) for x in firsts)
     n_second = tuple(count(x) for x in seconds)
     kernel = lambda *refs: cross_kernel(n_first, n_second, *refs)
     anywhere = pl.BlockSpec(memory_space=pl.ANY)
     vmem = pl.BlockSpec(memory_space=pltpu.VMEM)
-    smem = pl.BlockSpec(memory_space=pltpu.SMEM)
     n_in = len(firsts) + len(seconds)
     return pl.pallas_call(
         kernel,
         out_shape=(
-            jax.ShapeDtypeStruct((64, 128, LAGS), jnp.bfloat16),
-            jax.ShapeDtypeStruct((64, 128, LAGS), jnp.float32),
+            pltpu.VMEM((64, 128, LAGS), jnp.bfloat16),
+            pltpu.VMEM((64, 128, LAGS), jnp.float32),
         ),
-        in_specs=[smem, smem] + [anywhere] * n_in + [vmem],
+        in_specs=[anywhere] * n_in + [vmem],
         out_specs=(vmem, vmem),
         scratch_shapes=[
             pltpu.VMEM((HALF, 128, 2 * NW), jnp.bfloat16),
@@ -222,7 +246,7 @@
         ],
         compiler_params=pltpu.CompilerParams(vmem_limit_bytes=56 * 1024 * 1024),
         name="cross",
-    )(where, core, *firsts, *seconds, inverse)
+    )(*firsts, *seconds, inverse)
 
 
 def permutation(move):
@@ -252,57 +276,31 @@
 
 def correlate(traces, live_flags):
     dft, near, inverse = make_tables()
-    row = lax.axis_index("row")
-    col = lax.axis_index("col")
-    y, h, c = row // 4, row // 2 % 2, row % 2
-    x, l = col // N_L, col % N_L
-    core = c.reshape(1)
-    keep, send = whiten(traces, live_flags, core, jnp.asarray(dft), jnp.asarray(near))
-    piece = merge(core, keep, move(send, SWAP_CORE)).reshape(HALF, 8, 2 * NW)
+    keep, send = whiten(traces, live_flags, jnp.asarray(dft), jnp.asarray(near))
+    piece = merge(keep, move(send, SWAP_CORE)).reshape(HALF, 8, 2 * NW)
 
     other = move(piece, SWAP_H)
-    up1, down1 = move(piece, Y_UP), move(piece, Y_DOWN)
+    up1 = move(piece, Y_UP)
     l1, l3 = move(piece, STEP_L[1]), move(piece, STEP_L[3])
     up2 = move(jnp.stack([up1, other]), Y_UP)
-    down2 = move(jnp.stack([down1, other]), Y_DOWN)
+    down0 = jnp.stack([piece, other])
+    down1 = move(down0, Y_DOWN)
     l2 = move(piece, STEP_L[2])
     x1 = jnp.stack([piece, l1])
     x1_up, x1_down = move(x1, X_UP), move(x1, X_DOWN)
-    up3, down3 = move(up2, Y_UP), move(down2, Y_DOWN)
+    up3, down2 = move(up2, Y_UP), move(down1, Y_DOWN)
     x2 = jnp.stack([l3, l2])
     x2_up, x2_down = move(x2, X_UP), move(x2, X_DOWN)
     x1_far = move(x1_up, X_UP)
-    up4 = move(up3, Y_UP)
+    up4, down3 = move(up3, Y_UP), move(down2, Y_DOWN)
+    x2_far = move(x2_down, X_DOWN)
     down4 = move(down3[1], Y_DOWN)
-    x2_far = move(x2_down, X_DOWN)
-    down5 = move(down4, Y_DOWN)
-
-    lead = [l, (l - 1) % N_L]
-    rest = [(l - 3) % N_L, (l - 2) % N_L]
+
     firsts = (x1, x2, x1_up, x2_up, x1_down, x2_down, x1_far, x2_far)
-    first_at = []
-    for d in (0, -1, 1, 2):
-        first_at += [(x + d) % N_X * N_L + q for q in lead + rest]
-    seconds = (piece, up1, down1, up2, down2, up3, down3, up4, down4, down5)
-    spot = lambda d, mine: (y + d) % N_Y * N_H + (h if mine else 1 - h)
-    second_at = [spot(0, True), spot(-1, True), spot(1, True)]
-    second_at += [spot(-2, True), spot(-1, False), spot(2, True), spot(1, False)]
-    second_at += [spot(-3, True), spot(-2, False), spot(3, True), spot(2, False)]
-    second_at += [spot(-4, True), spot(-3, False), spot(3, False), spot(4, False)]
-    seconds += (other,)
-    second_at += [spot(0, False)]
-    where = jnp.stack(first_at + second_at).astype(jnp.int32)
-    table = lax.dynamic_index_in_dim(jnp.asarray(inverse), c, 0, keepdims=False)
-    sent, own = cross(where, core, firsts, seconds, table)
-    corr = own + move(sent, SWAP_CORE).astype(jnp.float32)
-
-    rows, cols = corr.shape[:2]
-    chan_i = row * rows + jnp.arange(rows, dtype=jnp.int32)
-    local_j = jnp.arange(cols, dtype=jnp.int32)
-    chan_j = (local_j // 4 * (N_X * N_L) + col) * 4 + local_j % 4
-    same = chan_i[:, None] == chan_j[None, :]
-    corr = jnp.where(same[:, :, None], 0.0, corr)
-    return corr.astype(jnp.bfloat16)
+    seconds = (down0, up1, up2, up3, up4, down1, down2, down3, down4)
+    sent, own = cross(firsts, seconds, jnp.asarray(inverse))
+    got = move(sent, SWAP_CORE)
+    return (own + got.astype(jnp.float32)).astype(jnp.bfloat16)
 
 
 def solution(mesh):

time: 149 us -> 152 us (1.020)
  the two profiles are of different devices: /device:TPU:1 before, /device:TPU:71 now
where the time goes in v1:
time: 152 us; the launch traced here: 151 us
  starting transfers between devices  68.8 us (45%)
  waiting for transfers between devices  57.8 us (38%)
  Pallas kernels  17.9 us (12%)
  local copies, waits for them, and re-layouts  3.15 us (2%)
  other arithmetic  3.11 us (2%)
    ppermute x20, starting transfers between devices, move(): return lax.ppermute(value, AXES, pairs)  68.8 us
    ppermute x20, waiting for transfers between devices, move(): return lax.ppermute(value, AXES, pairs)  57.8 us
    pallas_call x1, Pallas kernels, cross(): pl.pallas_call(kernel, out_shape=(pltpu.VMEM((64, 128, LAGS), jnp.bfloat1...  12.4 us
    pallas_call x1, Pallas kernels, whiten(): pl.pallas_call(whiten_kernel, out_shape=(shape, shape), in_specs=[smem, v...  3.72 us
    unnamed x38, local copies, waits for them, and re-layouts  3.13 us
  transfers between devices with their start and end apart: 20, of which 10 were waited for; matrix products, arithmetic and copies ran while one was open for 0% of the time, Pallas kernels for 0%

profile of v1, /device:TPU:71, one launch (start us, length us, event | category | flops | bytes accessed | tf_op | source)
XLA Modules:
  0.0 151.1 jit_solution(7638372959078432559)
XLA Ops:
  0.0 3.7 %whiten.1 = (bf16[512,128]{1,0:T(8,128)(2,1)}, bf16[512,128]{1,0:T(8,128)(2,1)}) custom-call(s32[4]{0:T(128)} %flags_ref.1, bf16[256,512]{1,0:T(8,128)(2,1)} %bitcast.17, bf16[3,512,512]{2,1,0:T(8,128)(2,1)} %constant.6.clone.dft_ref, f32[256,256]{1,0:T(8,128)} %constant.7.clone.near_ref), custom_call_target="tpu_custom_call" | custom-call | tf_op jit(solution)/shard_map/whiten/pallas_call | solution.py:92
  3.7 2.6 %collective-permute-start = (bf16[512,128]{1,0:T(8,128)(2,1)}, bf16[512,128]{1,0:T(8,128)(2,1)S(1)}, u32[]{:S(2)}, u32[]{:S(2)}) collective-permute-start(bf16[512,128]{1,0:T(8,128)(2,1)} %get-tuple-element.10), channel_id=1, source_target_pairs={{0,16},{1,17},{2,18},{3,19},{4,20},{5,21},{6,22},{7,23},{8,24},{9,... | collective-permute-start | bytes 393224 | tf_op jit(solution)/shard_map/ppermute | solution.py:274
  8.1 1.8 %merge.1 = bf16[1024,128]{1,0:T(8,128)(2,1)} custom-call(bf16[512,128]{1,0:T(8,128)(2,1)} %get-tuple-element.9.keep_ref, bf16[512,128]{1,0:T(8,128)(2,1)} %copy-done.18), custom_call_target="tpu_custom_call" | custom-call | tf_op jit(solution)/shard_map/merge/pallas_call | solution.py:117
  9.9 3.3 %collective-permute-start.11 = (bf16[128,8,128]{2,1,0:T(8,128)(2,1)}, bf16[128,8,128]{2,1,0:T(8,128)(2,1)S(1)}, u32[]{:S(2)}, u32[]{:S(2)}) collective-permute-start(bf16[128,8,128]{2,1,0:T(8,128)(2,1)} %bitcast.11), channel_id=1, source_target_pairs={{0,64},{1,65},{2,66},{3,67},{4,68},{5,69},{6,70},{7,71},{8,72},{9,... | collective-permute-start | bytes 786440 | tf_op jit(solution)/shard_map/ppermute | solution.py:274
  13.2 9.7 %collective-permute-start.10 = (bf16[128,8,128]{2,1,0:T(8,128)(2,1)}, bf16[128,8,128]{2,1,0:T(8,128)(2,1)S(1)}, u32[]{:S(2)}, u32[]{:S(2)}) collective-permute-start(bf16[128,8,128]{2,1,0:T(8,128)(2,1)} %bitcast.12), channel_id=1, source_target_pairs={{0,32},{1,33},{2,34},{3,35},{4,36},{5,37},{6,38},{7,39},{8,40},{9,... | collective-permute-start | bytes 786440 | tf_op jit(solution)/shard_map/ppermute | solution.py:274
  23.0 3.1 %collective-permute-start.1 = (bf16[128,8,128]{2,1,0:T(8,128)(2,1)}, bf16[128,8,128]{2,1,0:T(8,128)(2,1)S(1)}, u32[]{:S(2)}, u32[]{:S(2)}) collective-permute-start(bf16[128,8,128]{2,1,0:T(8,128)(2,1)} %bitcast.13), channel_id=1, source_target_pairs={{0,1},{1,2},{2,3},{3,0},{4,5},{5,6},{6,7},{7,4},{8,9},{9,10},{10,1... | collective-permute-start | bytes 786440 | tf_op jit(solution)/shard_map/ppermute | solution.py:274
  26.1 9.7 %collective-permute-done.10 = bf16[128,8,128]{2,1,0:T(8,128)(2,1)S(1)} collective-permute-done((bf16[128,8,128]{2,1,0:T(8,128)(2,1)}, bf16[128,8,128]{2,1,0:T(8,128)(2,1)S(1)}, u32[]{:S(2)}, u32[]{:S(2)}) %collective-permute-start.10) | collective-permute-done | bytes 262176 | tf_op jit(solution)/shard_map/ppermute | solution.py:274
  35.8 4.7 %collective-permute-done.1 = bf16[128,8,128]{2,1,0:T(8,128)(2,1)S(1)} collective-permute-done((bf16[128,8,128]{2,1,0:T(8,128)(2,1)}, bf16[128,8,128]{2,1,0:T(8,128)(2,1)S(1)}, u32[]{:S(2)}, u32[]{:S(2)}) %collective-permute-start.1) | collective-permute-done | bytes 262176 | tf_op jit(solution)/shard_map/ppermute | solution.py:274
  41.6 4.1 %collective-permute-start.15 = (bf16[2,128,8,128]{3,2,1,0:T(8,128)(2,1)S(1)}, bf16[2,128,8,128]{3,2,1,0:T(8,128)(2,1)S(1)}, u32[]{:S(2)}, u32[]{:S(2)}) collective-permute-start(bf16[2,128,8,128]{3,2,1,0:T(8,128)(2,1)S(1)} %get-tuple-element.14.refs_8_), channel_id=1, source_target_pairs={{0,448},{1,449},{2,450},{3,451},{4,452},{5,453},{6,454},{7,455},{8... | collective-permute-start | bytes 1572872 | tf_op jit(solution)/shard_map/ppermute | solution.py:274
  45.7 1.9 %collective-permute-start.12 = (bf16[2,128,8,128]{3,2,1,0:T(8,128)(2,1)S(1)}, bf16[2,128,8,128]{3,2,1,0:T(8,128)(2,1)S(1)}, u32[]{:S(2)}, u32[]{:S(2)}) collective-permute-start(bf16[2,128,8,128]{3,2,1,0:T(8,128)(2,1)S(1)} %get-tuple-element.13), channel_id=1, source_target_pairs={{0,64},{1,65},{2,66},{3,67},{4,68},{5,69},{6,70},{7,71},{8,72},{9,... | collective-permute-start | bytes 1572872 | tf_op jit(solution)/shard_map/ppermute | solution.py:274
  47.6 8.2 %collective-permute-done.15.refs_13_ = bf16[2,128,8,128]{3,2,1,0:T(8,128)(2,1)S(1)} collective-permute-done((bf16[2,128,8,128]{3,2,1,0:T(8,128)(2,1)S(1)}, bf16[2,128,8,128]{3,2,1,0:T(8,128)(2,1)S(1)}, u32[]{:S(2)}, u32[]{:S(2)}) %collective-permute-start.15) | collective-permute-done | bytes 524320 | tf_op jit(solution)/shard_map/ppermute | solution.py:274
  55.8 5.3 %collective-permute-start.16 = (bf16[2,128,8,128]{3,2,1,0:T(8,128)(2,1)S(1)}, bf16[2,128,8,128]{3,2,1,0:T(8,128)(2,1)S(1)}, u32[]{:S(2)}, u32[]{:S(2)}) collective-permute-start(bf16[2,128,8,128]{3,2,1,0:T(8,128)(2,1)S(1)} %collective-permute-done.15.refs_13_), channel_id=1, source_target_pairs={{0,448},{1,449},{2,450},{3,451},{4,452},{5,453},{6,454},{7,455},{8... | collective-permute-start | bytes 1572872 | tf_op jit(solution)/shard_map/ppermute | solution.py:274
  61.1 5.3 %collective-permute-start.3 = (bf16[128,8,128]{2,1,0:T(8,128)(2,1)S(1)}, bf16[128,8,128]{2,1,0:T(8,128)(2,1)S(1)}, u32[]{:S(2)}, u32[]{:S(2)}) collective-permute-start(bf16[128,8,128]{2,1,0:T(8,128)(2,1)S(1)} %bitcast.15), channel_id=1, source_target_pairs={{0,2},{1,3},{2,0},{3,1},{4,6},{5,7},{6,4},{7,5},{8,10},{9,11},{10,... | collective-permute-start | bytes 786440 | tf_op jit(solution)/shard_map/ppermute | solution.py:274
  66.4 2.2 %collective-permute-start.2 = (bf16[128,8,128]{2,1,0:T(8,128)(2,1)S(1)}, bf16[128,8,128]{2,1,0:T(8,128)(2,1)S(1)}, u32[]{:S(2)}, u32[]{:S(2)}) collective-permute-start(bf16[128,8,128]{2,1,0:T(8,128)(2,1)S(1)} %bitcast.16), channel_id=1, source_target_pairs={{0,3},{1,0},{2,1},{3,2},{4,7},{5,4},{6,5},{7,6},{8,11},{9,8},{10,9... | collective-permute-start | bytes 786440 | tf_op jit(solution)/shard_map/ppermute | solution.py:274
  68.6 15.0 %collective-permute-done.3 = bf16[128,8,128]{2,1,0:T(8,128)(2,1)S(1)} collective-permute-done((bf16[128,8,128]{2,1,0:T(8,128)(2,1)S(1)}, bf16[128,8,128]{2,1,0:T(8,128)(2,1)S(1)}, u32[]{:S(2)}, u32[]{:S(2)}) %collective-permute-start.3) | collective-permute-done | bytes 262176 | tf_op jit(solution)/shard_map/ppermute | solution.py:274
  83.7 2.5 %collective-permute-start.7 = (bf16[2,128,8,128]{3,2,1,0:T(8,128)(2,1)S(1)}, bf16[2,128,8,128]{3,2,1,0:T(8,128)(2,1)S(1)}, u32[]{:S(2)}, u32[]{:S(2)}) collective-permute-start(bf16[2,128,8,128]{3,2,1,0:T(8,128)(2,1)S(1)} %pad_maximum_fusion.3.refs_1_), channel_id=1, source_target_pairs={{0,12},{1,13},{2,14},{3,15},{4,0},{5,1},{6,2},{7,3},{8,4},{9,5},{1... | collective-permute-start | bytes 1572872 | tf_op jit(solution)/shard_map/ppermute | solution.py:274
  86.2 4.0 %collective-permute-start.4 = (bf16[2,128,8,128]{3,2,1,0:T(8,128)(2,1)S(1)}, bf16[2,128,8,128]{3,2,1,0:T(8,128)(2,1)S(1)}, u32[]{:S(2)}, u32[]{:S(2)}) collective-permute-start(bf16[2,128,8,128]{3,2,1,0:T(8,128)(2,1)S(1)} %get-tuple-element.15.refs_0_), channel_id=1, source_target_pairs={{0,4},{1,5},{2,6},{3,7},{4,8},{5,9},{6,10},{7,11},{8,12},{9,13},{1... | collective-permute-start | bytes 1572872 | tf_op jit(solution)/shard_map/ppermute | solution.py:274
  90.2 1.9 %collective-permute-start.13 = (bf16[2,128,8,128]{3,2,1,0:T(8,128)(2,1)S(1)}, bf16[2,128,8,128]{3,2,1,0:T(8,128)(2,1)S(1)}, u32[]{:S(2)}, u32[]{:S(2)}) collective-permute-start(bf16[2,128,8,128]{3,2,1,0:T(8,128)(2,1)S(1)} %collective-permute-done.12.refs_10_), channel_id=1, source_target_pairs={{0,64},{1,65},{2,66},{3,67},{4,68},{5,69},{6,70},{7,71},{8,72},{9,... | collective-permute-start | bytes 1572872 | tf_op jit(solution)/shard_map/ppermute | solution.py:274
  92.2 4.6 %collective-permute-start.17 = (bf16[2,128,8,128]{3,2,1,0:T(8,128)(2,1)S(1)}, bf16[2,128,8,128]{3,2,1,0:T(8,128)(2,1)S(1)}, u32[]{:S(2)}, u32[]{:S(2)}) collective-permute-start(bf16[2,128,8,128]{3,2,1,0:T(8,128)(2,1)S(1)} %collective-permute-done.16.refs_14_), channel_id=1, source_target_pairs={{0,448},{1,449},{2,450},{3,451},{4,452},{5,453},{6,454},{7,455},{8... | collective-permute-start | bytes 1572872 | tf_op jit(solution)/shard_map/ppermute | solution.py:274
  96.8 1.9 %collective-permute-start.5 = (bf16[2,128,8,128]{3,2,1,0:T(8,128)(2,1)S(1)}, bf16[2,128,8,128]{3,2,1,0:T(8,128)(2,1)S(1)}, u32[]{:S(2)}, u32[]{:S(2)}) collective-permute-start(bf16[2,128,8,128]{3,2,1,0:T(8,128)(2,1)S(1)} %pad_maximum_fusion.3.refs_1_), channel_id=1, source_target_pairs={{0,4},{1,5},{2,6},{3,7},{4,8},{5,9},{6,10},{7,11},{8,12},{9,13},{1... | collective-permute-start | bytes 1572872 | tf_op jit(solution)/shard_map/ppermute | solution.py:274
  99.8 2.3 %collective-permute-start.6 = (bf16[2,128,8,128]{3,2,1,0:T(8,128)(2,1)S(1)}, bf16[2,128,8,128]{3,2,1,0:T(8,128)(2,1)S(1)}, u32[]{:S(2)}, u32[]{:S(2)}) collective-permute-start(bf16[2,128,8,128]{3,2,1,0:T(8,128)(2,1)S(1)} %get-tuple-element.15.refs_0_), channel_id=1, source_target_pairs={{0,12},{1,13},{2,14},{3,15},{4,0},{5,1},{6,2},{7,3},{8,4},{9,5},{1... | collective-permute-start | bytes 1572872 | tf_op jit(solution)/shard_map/ppermute | solution.py:274
  102.1 1.9 %collective-permute-start.9 = (bf16[2,128,8,128]{3,2,1,0:T(8,128)(2,1)S(1)}, bf16[2,128,8,128]{3,2,1,0:T(8,128)(2,1)S(1)}, u32[]{:S(2)}, u32[]{:S(2)}) collective-permute-start(bf16[2,128,8,128]{3,2,1,0:T(8,128)(2,1)S(1)} %collective-permute-done.7.refs_5_), channel_id=1, source_target_pairs={{0,12},{1,13},{2,14},{3,15},{4,0},{5,1},{6,2},{7,3},{8,4},{9,5},{1... | collective-permute-start | bytes 1572872 | tf_op jit(solution)/shard_map/ppermute | solution.py:274
  104.0 1.7 %collective-permute-done.13.refs_11_ = bf16[2,128,8,128]{3,2,1,0:T(8,128)(2,1)S(1)} collective-permute-done((bf16[2,128,8,128]{3,2,1,0:T(8,128)(2,1)S(1)}, bf16[2,128,8,128]{3,2,1,0:T(8,128)(2,1)S(1)}, u32[]{:S(2)}, u32[]{:S(2)}) %collective-permute-start.13) | collective-permute-done | bytes 524320 | tf_op jit(solution)/shard_map/ppermute | solution.py:274
  105.8 2.9 %collective-permute-start.8 = (bf16[2,128,8,128]{3,2,1,0:T(8,128)(2,1)S(1)}, bf16[2,128,8,128]{3,2,1,0:T(8,128)(2,1)S(1)}, u32[]{:S(2)}, u32[]{:S(2)}) collective-permute-start(bf16[2,128,8,128]{3,2,1,0:T(8,128)(2,1)S(1)} %collective-permute-done.4.refs_2_), channel_id=1, source_target_pairs={{0,4},{1,5},{2,6},{3,7},{4,8},{5,9},{6,10},{7,11},{8,12},{9,13},{1... | collective-permute-start | bytes 1572872 | tf_op jit(solution)/shard_map/ppermute | solution.py:274
  108.6 1.9 %collective-permute-start.14 = (bf16[2,128,8,128]{3,2,1,0:T(8,128)(2,1)S(1)}, bf16[2,128,8,128]{3,2,1,0:T(8,128)(2,1)S(1)}, u32[]{:S(2)}, u32[]{:S(2)}) collective-permute-start(bf16[2,128,8,128]{3,2,1,0:T(8,128)(2,1)S(1)} %collective-permute-done.13.refs_11_), channel_id=1, source_target_pairs={{0,64},{1,65},{2,66},{3,67},{4,68},{5,69},{6,70},{7,71},{8,72},{9,... | collective-permute-start | bytes 1572872 | tf_op jit(solution)/shard_map/ppermute | solution.py:274
  110.6 1.3 collective-permute-done.5.refs_3_
  111.9 3.3 %collective-permute-start.18 = (bf16[128,8,128]{2,1,0:T(8,128)(2,1)S(1)}, bf16[128,8,128]{2,1,0:T(8,128)(2,1)S(1)}, u32[]{:S(2)}, u32[]{:S(2)}) collective-permute-start(bf16[128,8,128]{2,1,0:T(8,128)(2,1)S(1)} %slice_bitcast_fusion), channel_id=1, source_target_pairs={{0,448},{1,449},{2,450},{3,451},{4,452},{5,453},{6,454},{7,455},{8... | collective-permute-start | bytes 786440 | tf_op jit(solution)/shard_map/ppermute | solution.py:274
  115.2 11.0 %collective-permute-done.9.refs_7_ = bf16[2,128,8,128]{3,2,1,0:T(8,128)(2,1)S(1)} collective-permute-done((bf16[2,128,8,128]{3,2,1,0:T(8,128)(2,1)S(1)}, bf16[2,128,8,128]{3,2,1,0:T(8,128)(2,1)S(1)}, u32[]{:S(2)}, u32[]{:S(2)}) %collective-permute-start.9) | collective-permute-done | bytes 524320 | tf_op jit(solution)/shard_map/ppermute | solution.py:274
  128.8 12.4 %cross.1 = (bf16[64,128,128]{2,1,0:T(8,128)(2,1)S(1)}, f32[64,128,128]{2,1,0:T(8,128)S(1)}) custom-call(bf16[2,128,8,128]{3,2,1,0:T(8,128)(2,1)} %copy-done.1, bf16[2,128,8,128]{3,2,1,0:T(8,128)(2,1)} %copy-done.2, bf16[2,128,8,128]{3,2,1,0:T(8,128)(2,1)} %copy-done.10, bf16[2,128,8,128]{3,2,1,0:T(8,128)(2,1)} %copy-done.12, ...), custom_call_target="tpu_custom_call" | custom-call | tf_op jit(solution)/shard_map/cross/pallas_call | solution.py:233
  141.2 4.1 %collective-permute-start.19 = (bf16[64,128,128]{2,1,0:T(8,128)(2,1)S(1)}, bf16[64,128,128]{2,1,0:T(8,128)(2,1)S(1)}, u32[]{:S(2)}, u32[]{:S(2)}) collective-permute-start(bf16[64,128,128]{2,1,0:T(8,128)(2,1)S(1)} %get-tuple-element.12), channel_id=1, source_target_pairs={{0,16},{1,17},{2,18},{3,19},{4,20},{5,21},{6,22},{7,23},{8,24},{9,... | collective-permute-start | bytes 6291464 | tf_op jit(solution)/shard_map/ppermute | solution.py:274
  145.3 3.8 %collective-permute-done.19 = bf16[64,128,128]{2,1,0:T(8,128)(2,1)S(1)} collective-permute-done((bf16[64,128,128]{2,1,0:T(8,128)(2,1)S(1)}, bf16[64,128,128]{2,1,0:T(8,128)(2,1)S(1)}, u32[]{:S(2)}, u32[]{:S(2)}) %collective-permute-start.19) | collective-permute-done | bytes 2097184 | tf_op jit(solution)/shard_map/ppermute | solution.py:274
  149.1 2.0 %add_convert_fusion = bf16[64,128,128]{2,1,0:T(8,128)(2,1)} fusion(f32[64,128,128]{2,1,0:T(8,128)S(1)} %get-tuple-element.11, bf16[64,128,128]{2,1,0:T(8,128)(2,1)S(1)} %collective-permute-done.19), kind=kLoop, calls=%fused_computation | loop fusion | flops 3145728 | bytes 8388608 | tf_op jit(solution)/shard_map/convert_element_type | solution.py:303
  (53 shorter events, 6.6 us)
Async XLA Ops:
  3.7 3.8 %collective-permute-start = (bf16[512,128]{1,0:T(8,128)(2,1)}, bf16[512,128]{1,0:T(8,128)(2,1)S(1)}, u32[]{:S(2)}, u32[]{:S(2)}) collective-permute-start(bf16[512,128]{1,0:T(8,128)(2,1)} %get-tuple-element.10), channel_id=1, source_target_pairs={{0,16},{1,17},{2,18},{3,19},{4,20},{5,21},{6,22},{7,23},{8,24},{9,... | collective-permute-start | bytes 393224 | tf_op jit(solution)/shard_map/ppermute | solution.py:274
  9.9 51.2 %copy-start.5 = (bf16[1024,128]{1,0:T(8,128)(2,1)S(1)}, bf16[1024,128]{1,0:T(8,128)(2,1)}, u32[]{:S(2)}) copy-start(bf16[1024,128]{1,0:T(8,128)(2,1)} %merge.1) | copy-start | bytes 786436
  9.9 16.2 %collective-permute-start.11 = (bf16[128,8,128]{2,1,0:T(8,128)(2,1)}, bf16[128,8,128]{2,1,0:T(8,128)(2,1)S(1)}, u32[]{:S(2)}, u32[]{:S(2)}) collective-permute-start(bf16[128,8,128]{2,1,0:T(8,128)(2,1)} %bitcast.11), channel_id=1, source_target_pairs={{0,64},{1,65},{2,66},{3,67},{4,68},{5,69},{6,70},{7,71},{8,72},{9,... | collective-permute-start | bytes 786440 | tf_op jit(solution)/shard_map/ppermute | solution.py:274
  13.2 22.6 %collective-permute-start.10 = (bf16[128,8,128]{2,1,0:T(8,128)(2,1)}, bf16[128,8,128]{2,1,0:T(8,128)(2,1)S(1)}, u32[]{:S(2)}, u32[]{:S(2)}) collective-permute-start(bf16[128,8,128]{2,1,0:T(8,128)(2,1)} %bitcast.12), channel_id=1, source_target_pairs={{0,32},{1,33},{2,34},{3,35},{4,36},{5,37},{6,38},{7,39},{8,40},{9,... | collective-permute-start | bytes 786440 | tf_op jit(solution)/shard_map/ppermute | solution.py:274
  23.0 17.5 %collective-permute-start.1 = (bf16[128,8,128]{2,1,0:T(8,128)(2,1)}, bf16[128,8,128]{2,1,0:T(8,128)(2,1)S(1)}, u32[]{:S(2)}, u32[]{:S(2)}) collective-permute-start(bf16[128,8,128]{2,1,0:T(8,128)(2,1)} %bitcast.13), channel_id=1, source_target_pairs={{0,1},{1,2},{2,3},{3,0},{4,5},{5,6},{6,7},{7,4},{8,9},{9,10},{10,1... | collective-permute-start | bytes 786440 | tf_op jit(solution)/shard_map/ppermute | solution.py:274
  26.1 84.5 %copy-start.4 = (bf16[128,8,128]{2,1,0:T(8,128)(2,1)}, bf16[128,8,128]{2,1,0:T(8,128)(2,1)S(1)}, u32[]{:S(2)}) copy-start(bf16[128,8,128]{2,1,0:T(8,128)(2,1)S(1)} %collective-permute-done.11.refs_9_) | copy-start | bytes 786436
  41.5 86.5 %copy-start = (bf16[2,128,8,128]{3,2,1,0:T(8,128)(2,1)}, bf16[2,128,8,128]{3,2,1,0:T(8,128)(2,1)S(1)}, u32[]{:S(2)}) copy-start(bf16[2,128,8,128]{3,2,1,0:T(8,128)(2,1)S(1)} %get-tuple-element.14.refs_8_) | copy-start | bytes 1572868
  41.5 86.5 %copy-start.1 = (bf16[2,128,8,128]{3,2,1,0:T(8,128)(2,1)}, bf16[2,128,8,128]{3,2,1,0:T(8,128)(2,1)S(1)}, u32[]{:S(2)}) copy-start(bf16[2,128,8,128]{3,2,1,0:T(8,128)(2,1)S(1)} %get-tuple-element.15.refs_0_) | copy-start | bytes 1572868
  41.6 14.2 %collective-permute-start.15 = (bf16[2,128,8,128]{3,2,1,0:T(8,128)(2,1)S(1)}, bf16[2,128,8,128]{3,2,1,0:T(8,128)(2,1)S(1)}, u32[]{:S(2)}, u32[]{:S(2)}) collective-permute-start(bf16[2,128,8,128]{3,2,1,0:T(8,128)(2,1)S(1)} %get-tuple-element.14.refs_8_), channel_id=1, source_target_pairs={{0,448},{1,449},{2,450},{3,451},{4,452},{5,453},{6,454},{7,455},{8... | collective-permute-start | bytes 1572872 | tf_op jit(solution)/shard_map/ppermute | solution.py:274
  45.7 44.5 %collective-permute-start.12 = (bf16[2,128,8,128]{3,2,1,0:T(8,128)(2,1)S(1)}, bf16[2,128,8,128]{3,2,1,0:T(8,128)(2,1)S(1)}, u32[]{:S(2)}, u32[]{:S(2)}) collective-permute-start(bf16[2,128,8,128]{3,2,1,0:T(8,128)(2,1)S(1)} %get-tuple-element.13), channel_id=1, source_target_pairs={{0,64},{1,65},{2,66},{3,67},{4,68},{5,69},{6,70},{7,71},{8,72},{9,... | collective-permute-start | bytes 1572872 | tf_op jit(solution)/shard_map/ppermute | solution.py:274
  55.8 70.5 %copy-start.6 = (bf16[2,128,8,128]{3,2,1,0:T(8,128)(2,1)}, bf16[2,128,8,128]{3,2,1,0:T(8,128)(2,1)S(1)}, u32[]{:S(2)}) copy-start(bf16[2,128,8,128]{3,2,1,0:T(8,128)(2,1)S(1)} %collective-permute-done.15.refs_13_) | copy-start | bytes 1572868
  55.8 36.3 %collective-permute-start.16 = (bf16[2,128,8,128]{3,2,1,0:T(8,128)(2,1)S(1)}, bf16[2,128,8,128]{3,2,1,0:T(8,128)(2,1)S(1)}, u32[]{:S(2)}, u32[]{:S(2)}) collective-permute-start(bf16[2,128,8,128]{3,2,1,0:T(8,128)(2,1)S(1)} %collective-permute-done.15.refs_13_), channel_id=1, source_target_pairs={{0,448},{1,449},{2,450},{3,451},{4,452},{5,453},{6,454},{7,455},{8... | collective-permute-start | bytes 1572872 | tf_op jit(solution)/shard_map/ppermute | solution.py:274
  61.1 22.5 %collective-permute-start.3 = (bf16[128,8,128]{2,1,0:T(8,128)(2,1)S(1)}, bf16[128,8,128]{2,1,0:T(8,128)(2,1)S(1)}, u32[]{:S(2)}, u32[]{:S(2)}) collective-permute-start(bf16[128,8,128]{2,1,0:T(8,128)(2,1)S(1)} %bitcast.15), channel_id=1, source_target_pairs={{0,2},{1,3},{2,0},{3,1},{4,6},{5,7},{6,4},{7,5},{8,10},{9,11},{10,... | collective-permute-start | bytes 786440 | tf_op jit(solution)/shard_map/ppermute | solution.py:274
  66.4 17.2 %collective-permute-start.2 = (bf16[128,8,128]{2,1,0:T(8,128)(2,1)S(1)}, bf16[128,8,128]{2,1,0:T(8,128)(2,1)S(1)}, u32[]{:S(2)}, u32[]{:S(2)}) collective-permute-start(bf16[128,8,128]{2,1,0:T(8,128)(2,1)S(1)} %bitcast.16), channel_id=1, source_target_pairs={{0,3},{1,0},{2,1},{3,2},{4,7},{5,4},{6,5},{7,6},{8,11},{9,8},{10,9... | collective-permute-start | bytes 786440 | tf_op jit(solution)/shard_map/ppermute | solution.py:274
  83.7 44.4 %copy-start.2 = (bf16[2,128,8,128]{3,2,1,0:T(8,128)(2,1)}, bf16[2,128,8,128]{3,2,1,0:T(8,128)(2,1)S(1)}, u32[]{:S(2)}) copy-start(bf16[2,128,8,128]{3,2,1,0:T(8,128)(2,1)S(1)} %pad_maximum_fusion.3.refs_1_) | copy-start | bytes 1572868
  83.7 16.1 %collective-permute-start.7 = (bf16[2,128,8,128]{3,2,1,0:T(8,128)(2,1)S(1)}, bf16[2,128,8,128]{3,2,1,0:T(8,128)(2,1)S(1)}, u32[]{:S(2)}, u32[]{:S(2)}) collective-permute-start(bf16[2,128,8,128]{3,2,1,0:T(8,128)(2,1)S(1)} %pad_maximum_fusion.3.refs_1_), channel_id=1, source_target_pairs={{0,12},{1,13},{2,14},{3,15},{4,0},{5,1},{6,2},{7,3},{8,4},{9,5},{1... | collective-permute-start | bytes 1572872 | tf_op jit(solution)/shard_map/ppermute | solution.py:274
  86.2 15.9 %collective-permute-start.4 = (bf16[2,128,8,128]{3,2,1,0:T(8,128)(2,1)S(1)}, bf16[2,128,8,128]{3,2,1,0:T(8,128)(2,1)S(1)}, u32[]{:S(2)}, u32[]{:S(2)}) collective-permute-start(bf16[2,128,8,128]{3,2,1,0:T(8,128)(2,1)S(1)} %get-tuple-element.15.refs_0_), channel_id=1, source_target_pairs={{0,4},{1,5},{2,6},{3,7},{4,8},{5,9},{6,10},{7,11},{8,12},{9,13},{1... | collective-permute-start | bytes 1572872 | tf_op jit(solution)/shard_map/ppermute | solution.py:274
  90.2 36.1 %copy-start.7 = (bf16[2,128,8,128]{3,2,1,0:T(8,128)(2,1)}, bf16[2,128,8,128]{3,2,1,0:T(8,128)(2,1)S(1)}, u32[]{:S(2)}) copy-start(bf16[2,128,8,128]{3,2,1,0:T(8,128)(2,1)S(1)} %collective-permute-done.12.refs_10_) | copy-start | bytes 1572868
  90.2 15.5 %collective-permute-start.13 = (bf16[2,128,8,128]{3,2,1,0:T(8,128)(2,1)S(1)}, bf16[2,128,8,128]{3,2,1,0:T(8,128)(2,1)S(1)}, u32[]{:S(2)}, u32[]{:S(2)}) collective-permute-start(bf16[2,128,8,128]{3,2,1,0:T(8,128)(2,1)S(1)} %collective-permute-done.12.refs_10_), channel_id=1, source_target_pairs={{0,64},{1,65},{2,66},{3,67},{4,68},{5,69},{6,70},{7,71},{8,72},{9,... | collective-permute-start | bytes 1572872 | tf_op jit(solution)/shard_map/ppermute | solution.py:274
  92.2 34.1 %copy-start.8 = (bf16[2,128,8,128]{3,2,1,0:T(8,128)(2,1)}, bf16[2,128,8,128]{3,2,1,0:T(8,128)(2,1)S(1)}, u32[]{:S(2)}) copy-start(bf16[2,128,8,128]{3,2,1,0:T(8,128)(2,1)S(1)} %collective-permute-done.16.refs_14_) | copy-start | bytes 1572868
  92.2 16.5 %collective-permute-start.17 = (bf16[2,128,8,128]{3,2,1,0:T(8,128)(2,1)S(1)}, bf16[2,128,8,128]{3,2,1,0:T(8,128)(2,1)S(1)}, u32[]{:S(2)}, u32[]{:S(2)}) collective-permute-start(bf16[2,128,8,128]{3,2,1,0:T(8,128)(2,1)S(1)} %collective-permute-done.16.refs_14_), channel_id=1, source_target_pairs={{0,448},{1,449},{2,450},{3,451},{4,452},{5,453},{6,454},{7,455},{8... | collective-permute-start | bytes 1572872 | tf_op jit(solution)/shard_map/ppermute | solution.py:274
  96.8 15.2 %collective-permute-start.5 = (bf16[2,128,8,128]{3,2,1,0:T(8,128)(2,1)S(1)}, bf16[2,128,8,128]{3,2,1,0:T(8,128)(2,1)S(1)}, u32[]{:S(2)}, u32[]{:S(2)}) collective-permute-start(bf16[2,128,8,128]{3,2,1,0:T(8,128)(2,1)S(1)} %pad_maximum_fusion.3.refs_1_), channel_id=1, source_target_pairs={{0,4},{1,5},{2,6},{3,7},{4,8},{5,9},{6,10},{7,11},{8,12},{9,13},{1... | collective-permute-start | bytes 1572872 | tf_op jit(solution)/shard_map/ppermute | solution.py:274
  99.8 26.5 %copy-start.9 = (bf16[2,128,8,128]{3,2,1,0:T(8,128)(2,1)}, bf16[2,128,8,128]{3,2,1,0:T(8,128)(2,1)S(1)}, u32[]{:S(2)}) copy-start(bf16[2,128,8,128]{3,2,1,0:T(8,128)(2,1)S(1)} %collective-permute-done.7.refs_5_) | copy-start | bytes 1572868
  99.8 15.4 %collective-permute-start.6 = (bf16[2,128,8,128]{3,2,1,0:T(8,128)(2,1)S(1)}, bf16[2,128,8,128]{3,2,1,0:T(8,128)(2,1)S(1)}, u32[]{:S(2)}, u32[]{:S(2)}) collective-permute-start(bf16[2,128,8,128]{3,2,1,0:T(8,128)(2,1)S(1)} %get-tuple-element.15.refs_0_), channel_id=1, source_target_pairs={{0,12},{1,13},{2,14},{3,15},{4,0},{5,1},{6,2},{7,3},{8,4},{9,5},{1... | collective-permute-start | bytes 1572872 | tf_op jit(solution)/shard_map/ppermute | solution.py:274
  102.1 24.2 %copy-start.10 = (bf16[2,128,8,128]{3,2,1,0:T(8,128)(2,1)}, bf16[2,128,8,128]{3,2,1,0:T(8,128)(2,1)S(1)}, u32[]{:S(2)}) copy-start(bf16[2,128,8,128]{3,2,1,0:T(8,128)(2,1)S(1)} %collective-permute-done.4.refs_2_) | copy-start | bytes 1572868
  102.1 24.2 %collective-permute-start.9 = (bf16[2,128,8,128]{3,2,1,0:T(8,128)(2,1)S(1)}, bf16[2,128,8,128]{3,2,1,0:T(8,128)(2,1)S(1)}, u32[]{:S(2)}, u32[]{:S(2)}) collective-permute-start(bf16[2,128,8,128]{3,2,1,0:T(8,128)(2,1)S(1)} %collective-permute-done.7.refs_5_), channel_id=1, source_target_pairs={{0,12},{1,13},{2,14},{3,15},{4,0},{5,1},{6,2},{7,3},{8,4},{9,5},{1... | collective-permute-start | bytes 1572872 | tf_op jit(solution)/shard_map/ppermute | solution.py:274
  105.8 20.6 %copy-start.11 = (bf16[2,128,8,128]{3,2,1,0:T(8,128)(2,1)}, bf16[2,128,8,128]{3,2,1,0:T(8,128)(2,1)S(1)}, u32[]{:S(2)}) copy-start(bf16[2,128,8,128]{3,2,1,0:T(8,128)(2,1)S(1)} %collective-permute-done.13.refs_11_) | copy-start | bytes 1572868
  105.8 20.5 %collective-permute-start.8 = (bf16[2,128,8,128]{3,2,1,0:T(8,128)(2,1)S(1)}, bf16[2,128,8,128]{3,2,1,0:T(8,128)(2,1)S(1)}, u32[]{:S(2)}, u32[]{:S(2)}) collective-permute-start(bf16[2,128,8,128]{3,2,1,0:T(8,128)(2,1)S(1)} %collective-permute-done.4.refs_2_), channel_id=1, source_target_pairs={{0,4},{1,5},{2,6},{3,7},{4,8},{5,9},{6,10},{7,11},{8,12},{9,13},{1... | collective-permute-start | bytes 1572872 | tf_op jit(solution)/shard_map/ppermute | solution.py:274
  108.6 17.7 %copy-start.3 = (bf16[2,128,8,128]{3,2,1,0:T(8,128)(2,1)}, bf16[2,128,8,128]{3,2,1,0:T(8,128)(2,1)S(1)}, u32[]{:S(2)}) copy-start(bf16[2,128,8,128]{3,2,1,0:T(8,128)(2,1)S(1)} %collective-permute-done.17.refs_15_) | copy-start | bytes 1572868
  108.6 17.6 %collective-permute-start.14 = (bf16[2,128,8,128]{3,2,1,0:T(8,128)(2,1)S(1)}, bf16[2,128,8,128]{3,2,1,0:T(8,128)(2,1)S(1)}, u32[]{:S(2)}, u32[]{:S(2)}) collective-permute-start(bf16[2,128,8,128]{3,2,1,0:T(8,128)(2,1)S(1)} %collective-permute-done.13.refs_11_), channel_id=1, source_target_pairs={{0,64},{1,65},{2,66},{3,67},{4,68},{5,69},{6,70},{7,71},{8,72},{9,... | collective-permute-start | bytes 1572872 | tf_op jit(solution)/shard_map/ppermute | solution.py:274
  111.9 16.1 %collective-permute-start.18 = (bf16[128,8,128]{2,1,0:T(8,128)(2,1)S(1)}, bf16[128,8,128]{2,1,0:T(8,128)(2,1)S(1)}, u32[]{:S(2)}, u32[]{:S(2)}) collective-permute-start(bf16[128,8,128]{2,1,0:T(8,128)(2,1)S(1)} %slice_bitcast_fusion), channel_id=1, source_target_pairs={{0,448},{1,449},{2,450},{3,451},{4,452},{5,453},{6,454},{7,455},{8... | collective-permute-start | bytes 786440 | tf_op jit(solution)/shard_map/ppermute | solution.py:274
  141.2 7.9 %collective-permute-start.19 = (bf16[64,128,128]{2,1,0:T(8,128)(2,1)S(1)}, bf16[64,128,128]{2,1,0:T(8,128)(2,1)S(1)}, u32[]{:S(2)}, u32[]{:S(2)}) collective-permute-start(bf16[64,128,128]{2,1,0:T(8,128)(2,1)S(1)} %get-tuple-element.12), channel_id=1, source_target_pairs={{0,16},{1,17},{2,18},{3,19},{4,20},{5,21},{6,22},{7,23},{8,24},{9,... | collective-permute-start | bytes 6291464 | tf_op jit(solution)/shard_map/ppermute | solution.py:274
  (7 other events, 29.5 us)

commit v2 on v1

--- a/solution.py
+++ b/solution.py
@@ -88,7 +88,7 @@
 def whiten(traces, live_flags, dft, near):
     vmem = pl.BlockSpec(memory_space=pltpu.VMEM)
     smem = pl.BlockSpec(memory_space=pltpu.SMEM)
-    shape = jax.ShapeDtypeStruct((HALF * 4, 2 * NW), jnp.bfloat16)
+    shape = pltpu.VMEM((HALF * 4, 2 * NW), jnp.bfloat16)
     return pl.pallas_call(
         whiten_kernel,
         out_shape=(shape, shape),
@@ -116,11 +116,11 @@
     vmem = pl.BlockSpec(memory_space=pltpu.VMEM)
     return pl.pallas_call(
         merge_kernel,
-        out_shape=jax.ShapeDtypeStruct((PIECE, 2 * NW), jnp.bfloat16),
+        out_shape=pltpu.VMEM((PIECE, 2 * NW), jnp.bfloat16),
         in_specs=[vmem, vmem],
         out_specs=vmem,
         name="merge",
-    )(keep, got)
+    )(in_vmem(keep), in_vmem(got))
 
 
 N_CHUNK = 4
@@ -136,12 +136,10 @@
     for d in (0, -1, 1, 2):
         firsts += [(x + d) % N_X * N_L + (l + q) % N_L for q in (0, 3, 1, 2)]
     spot = lambda d, mine: (y + d) % N_Y * N_H + (h if mine else 1 - h)
-    seconds = [spot(0, True), spot(0, False), spot(-1, True)]
-    for d in (1, 2, 3):
-        seconds += [spot(-d - 1, True), spot(-d, False)]
-    for d in (1, 2, 3):
-        seconds += [spot(d, True), spot(d, False)]
-    seconds += [spot(4, False)]
+    seconds = [spot(0, True), spot(0, False), spot(-1, True), spot(1, True)]
+    for d in (1, 2):
+        seconds += [spot(-d - 1, True), spot(-d, False), spot(d + 1, True), spot(d, False)]
+    seconds += [spot(-4, True), spot(-3, False), spot(3, False), spot(4, False)]
     return row, col, firsts + seconds
 
 
@@ -227,7 +225,6 @@
     n_first = tuple(count(x) for x in firsts)
     n_second = tuple(count(x) for x in seconds)
     kernel = lambda *refs: cross_kernel(n_first, n_second, *refs)
-    anywhere = pl.BlockSpec(memory_space=pl.ANY)
     vmem = pl.BlockSpec(memory_space=pltpu.VMEM)
     n_in = len(firsts) + len(seconds)
     return pl.pallas_call(
@@ -236,7 +233,7 @@
             pltpu.VMEM((64, 128, LAGS), jnp.bfloat16),
             pltpu.VMEM((64, 128, LAGS), jnp.float32),
         ),
-        in_specs=[anywhere] * n_in + [vmem],
+        in_specs=[vmem] * (n_in + 1),
         out_specs=(vmem, vmem),
         scratch_shapes=[
             pltpu.VMEM((HALF, 128, 2 * NW), jnp.bfloat16),
@@ -244,9 +241,9 @@
             pltpu.VMEM((128 * PITCH, 128), jnp.float32),
             pltpu.SemaphoreType.DMA((N_CHUNK, 32)),
         ],
-        compiler_params=pltpu.CompilerParams(vmem_limit_bytes=56 * 1024 * 1024),
+        compiler_params=pltpu.CompilerParams(vmem_limit_bytes=32 * 1024 * 1024),
         name="cross",
-    )(*firsts, *seconds, inverse)
+    )(*[in_vmem(value) for value in (*firsts, *seconds)], inverse)
 
 
 def permutation(move):
@@ -270,6 +267,10 @@
 X_DOWN = permutation(lambda y, h, c, x, l: (y, h, c, x - 1, l))
 
 
+def in_vmem(value):
+    return pltpu.with_memory_space_constraint(value, pltpu.VMEM)
+
+
 def move(value, pairs):
     return lax.ppermute(value, AXES, pairs)
 
@@ -280,24 +281,24 @@
     piece = merge(keep, move(send, SWAP_CORE)).reshape(HALF, 8, 2 * NW)
 
     other = move(piece, SWAP_H)
-    up1 = move(piece, Y_UP)
+    up1, down1 = move(piece, Y_UP), move(piece, Y_DOWN)
     l1, l3 = move(piece, STEP_L[1]), move(piece, STEP_L[3])
     up2 = move(jnp.stack([up1, other]), Y_UP)
-    down0 = jnp.stack([piece, other])
-    down1 = move(down0, Y_DOWN)
+    down2 = move(jnp.stack([down1, other]), Y_DOWN)
     l2 = move(piece, STEP_L[2])
     x1 = jnp.stack([piece, l1])
     x1_up, x1_down = move(x1, X_UP), move(x1, X_DOWN)
-    up3, down2 = move(up2, Y_UP), move(down1, Y_DOWN)
+    up3, down3 = move(up2, Y_UP), move(down2, Y_DOWN)
     x2 = jnp.stack([l3, l2])
     x2_up, x2_down = move(x2, X_UP), move(x2, X_DOWN)
     x1_far = move(x1_up, X_UP)
-    up4, down3 = move(up3, Y_UP), move(down2, Y_DOWN)
+    up4 = move(up3, Y_UP)
+    down4 = move(down3[1], Y_DOWN)
     x2_far = move(x2_down, X_DOWN)
-    down4 = move(down3[1], Y_DOWN)
+    down5 = move(down4, Y_DOWN)
 
     firsts = (x1, x2, x1_up, x2_up, x1_down, x2_down, x1_far, x2_far)
-    seconds = (down0, up1, up2, up3, up4, down1, down2, down3, down4)
+    seconds = (piece, other, up1, down1, up2, down2, up3, down3, up4, down4, down5)
     sent, own = cross(firsts, seconds, jnp.asarray(inverse))
     got = move(sent, SWAP_CORE)
     return (own + got.astype(jnp.float32)).astype(jnp.bfloat16)

time: 152 us -> 134 us (0.88)
  the two profiles are of different devices: /device:TPU:71 before, /device:TPU:131 now
where the time goes in v2:
time: 134 us
  starting transfers between devices  73.7 us (55%)
  waiting for transfers between devices  41.7 us (31%)
  Pallas kernels  15.7 us (12%)
  other arithmetic  2.19 us (2%)
    ppermute x21, starting transfers between devices, move(): return lax.ppermute(value, AXES, pairs)  73.7 us
    ppermute x21, waiting for transfers between devices, move(): return lax.ppermute(value, AXES, pairs)  41.7 us
    pallas_call x1, Pallas kernels, cross(): pl.pallas_call(kernel, out_shape=(pltpu.VMEM((64, 128, LAGS), jnp.bfloat1...  12.5 us
    pallas_call x1, Pallas kernels, whiten(): pl.pallas_call(whiten_kernel, out_shape=(shape, shape), in_specs=[smem, v...  3.02 us
  transfers between devices with their start and end apart: 21, of which 10 were waited for; matrix products, arithmetic and copies ran while one was open for 0% of the time, Pallas kernels for 0%

profile of v2, /device:TPU:131, one launch (start us, length us, event | category | flops | bytes accessed | tf_op | source)
XLA Modules:
  0.0 133.6 jit_solution(14139317252504197428)
XLA Ops:
  0.0 3.0 %whiten.1 = (bf16[512,128]{1,0:T(8,128)(2,1)S(1)}, bf16[512,128]{1,0:T(8,128)(2,1)S(1)}) custom-call(s32[4]{0:T(128)} %flags_ref.1, bf16[256,512]{1,0:T(8,128)(2,1)} %bitcast.22, bf16[3,512,512]{2,1,0:T(8,128)(2,1)} %constant.6.clone.dft_ref, f32[256,256]{1,0:T(8,128)} %constant.7.clone.near_ref), custom_call_target="tpu_custom_call" | custom-call | tf_op jit(solution)/shard_map/whiten/pallas_call | solution.py:92
  3.0 2.6 %collective-permute-start = (bf16[512,128]{1,0:T(8,128)(2,1)S(1)}, bf16[512,128]{1,0:T(8,128)(2,1)S(1)}, u32[]{:S(2)}, u32[]{:S(2)}) collective-permute-start(bf16[512,128]{1,0:T(8,128)(2,1)S(1)} %get-tuple-element.10), channel_id=1, source_target_pairs={{0,16},{1,17},{2,18},{3,19},{4,20},{5,21},{6,22},{7,23},{8,24},{9,... | collective-permute-start | bytes 393224 | tf_op jit(solution)/shard_map/ppermute | solution.py:275
  6.7 5.1 %collective-permute-start.12 = (bf16[128,8,128]{2,1,0:T(8,128)(2,1)S(1)}, bf16[128,8,128]{2,1,0:T(8,128)(2,1)S(1)}, u32[]{:S(2)}, u32[]{:S(2)}) collective-permute-start(bf16[128,8,128]{2,1,0:T(8,128)(2,1)S(1)} %bitcast.11), channel_id=1, source_target_pairs={{0,448},{1,449},{2,450},{3,451},{4,452},{5,453},{6,454},{7,455},{8... | collective-permute-start | bytes 786440 | tf_op jit(solution)/shard_map/ppermute | solution.py:275
  11.8 1.9 %collective-permute-start.11 = (bf16[128,8,128]{2,1,0:T(8,128)(2,1)S(1)}, bf16[128,8,128]{2,1,0:T(8,128)(2,1)S(1)}, u32[]{:S(2)}, u32[]{:S(2)}) collective-permute-start(bf16[128,8,128]{2,1,0:T(8,128)(2,1)S(1)} %bitcast.12), channel_id=1, source_target_pairs={{0,64},{1,65},{2,66},{3,67},{4,68},{5,69},{6,70},{7,71},{8,72},{9,... | collective-permute-start | bytes 786440 | tf_op jit(solution)/shard_map/ppermute | solution.py:275
  13.7 8.8 %collective-permute-start.10 = (bf16[128,8,128]{2,1,0:T(8,128)(2,1)S(1)}, bf16[128,8,128]{2,1,0:T(8,128)(2,1)S(1)}, u32[]{:S(2)}, u32[]{:S(2)}) collective-permute-start(bf16[128,8,128]{2,1,0:T(8,128)(2,1)S(1)} %bitcast.13), channel_id=1, source_target_pairs={{0,32},{1,33},{2,34},{3,35},{4,36},{5,37},{6,38},{7,39},{8,40},{9,... | collective-permute-start | bytes 786440 | tf_op jit(solution)/shard_map/ppermute | solution.py:275
  22.6 12.3 %collective-permute-done.10.refs_9_ = bf16[128,8,128]{2,1,0:T(8,128)(2,1)S(1)} collective-permute-done((bf16[128,8,128]{2,1,0:T(8,128)(2,1)S(1)}, bf16[128,8,128]{2,1,0:T(8,128)(2,1)S(1)}, u32[]{:S(2)}, u32[]{:S(2)}) %collective-permute-start.10) | collective-permute-done | bytes 262176 | tf_op jit(solution)/shard_map/ppermute | solution.py:275
  35.0 4.6 %collective-permute-start.14 = (bf16[2,128,8,128]{3,2,1,0:T(8,128)(2,1)S(1)}, bf16[2,128,8,128]{3,2,1,0:T(8,128)(2,1)S(1)}, u32[]{:S(2)}, u32[]{:S(2)}) collective-permute-start(bf16[2,128,8,128]{3,2,1,0:T(8,128)(2,1)S(1)} %get-tuple-element.13), channel_id=1, source_target_pairs={{0,448},{1,449},{2,450},{3,451},{4,452},{5,453},{6,454},{7,455},{8... | collective-permute-start | bytes 1572872 | tf_op jit(solution)/shard_map/ppermute | solution.py:275
  39.6 1.9 %collective-permute-start.1 = (bf16[128,8,128]{2,1,0:T(8,128)(2,1)S(1)}, bf16[128,8,128]{2,1,0:T(8,128)(2,1)S(1)}, u32[]{:S(2)}, u32[]{:S(2)}) collective-permute-start(bf16[128,8,128]{2,1,0:T(8,128)(2,1)S(1)} %bitcast.14), channel_id=1, source_target_pairs={{0,1},{1,2},{2,3},{3,0},{4,5},{5,6},{6,7},{7,4},{8,9},{9,10},{10,1... | collective-permute-start | bytes 786440 | tf_op jit(solution)/shard_map/ppermute | solution.py:275
  41.5 2.4 %collective-permute-start.3 = (bf16[128,8,128]{2,1,0:T(8,128)(2,1)S(1)}, bf16[128,8,128]{2,1,0:T(8,128)(2,1)S(1)}, u32[]{:S(2)}, u32[]{:S(2)}) collective-permute-start(bf16[128,8,128]{2,1,0:T(8,128)(2,1)S(1)} %bitcast.15), channel_id=1, source_target_pairs={{0,2},{1,3},{2,0},{3,1},{4,6},{5,7},{6,4},{7,5},{8,10},{9,11},{10,... | collective-permute-start | bytes 786440 | tf_op jit(solution)/shard_map/ppermute | solution.py:275
  43.9 2.9 %collective-permute-start.2 = (bf16[128,8,128]{2,1,0:T(8,128)(2,1)S(1)}, bf16[128,8,128]{2,1,0:T(8,128)(2,1)S(1)}, u32[]{:S(2)}, u32[]{:S(2)}) collective-permute-start(bf16[128,8,128]{2,1,0:T(8,128)(2,1)S(1)} %bitcast.16), channel_id=1, source_target_pairs={{0,3},{1,0},{2,1},{3,2},{4,7},{5,4},{6,5},{7,6},{8,11},{9,8},{10,9... | collective-permute-start | bytes 786440 | tf_op jit(solution)/shard_map/ppermute | solution.py:275
  46.8 1.9 %collective-permute-start.13 = (bf16[2,128,8,128]{3,2,1,0:T(8,128)(2,1)S(1)}, bf16[2,128,8,128]{3,2,1,0:T(8,128)(2,1)S(1)}, u32[]{:S(2)}, u32[]{:S(2)}) collective-permute-start(bf16[2,128,8,128]{3,2,1,0:T(8,128)(2,1)S(1)} %get-tuple-element.14), channel_id=1, source_target_pairs={{0,64},{1,65},{2,66},{3,67},{4,68},{5,69},{6,70},{7,71},{8,72},{9,... | collective-permute-start | bytes 1572872 | tf_op jit(solution)/shard_map/ppermute | solution.py:275
  50.2 3.1 %collective-permute-start.4 = (bf16[2,128,8,128]{3,2,1,0:T(8,128)(2,1)S(1)}, bf16[2,128,8,128]{3,2,1,0:T(8,128)(2,1)S(1)}, u32[]{:S(2)}, u32[]{:S(2)}) collective-permute-start(bf16[2,128,8,128]{3,2,1,0:T(8,128)(2,1)S(1)} %pad_maximum_fusion.2.refs_0_), channel_id=1, source_target_pairs={{0,4},{1,5},{2,6},{3,7},{4,8},{5,9},{6,10},{7,11},{8,12},{9,13},{1... | collective-permute-start | bytes 1572872 | tf_op jit(solution)/shard_map/ppermute | solution.py:275
  53.3 4.4 %collective-permute-done.3 = bf16[128,8,128]{2,1,0:T(8,128)(2,1)S(1)} collective-permute-done((bf16[128,8,128]{2,1,0:T(8,128)(2,1)S(1)}, bf16[128,8,128]{2,1,0:T(8,128)(2,1)S(1)}, u32[]{:S(2)}, u32[]{:S(2)}) %collective-permute-start.3) | collective-permute-done | bytes 262176 | tf_op jit(solution)/shard_map/ppermute | solution.py:275
  57.7 5.6 %collective-permute-done.2 = bf16[128,8,128]{2,1,0:T(8,128)(2,1)S(1)} collective-permute-done((bf16[128,8,128]{2,1,0:T(8,128)(2,1)S(1)}, bf16[128,8,128]{2,1,0:T(8,128)(2,1)S(1)}, u32[]{:S(2)}, u32[]{:S(2)}) %collective-permute-start.2) | collective-permute-done | bytes 262176 | tf_op jit(solution)/shard_map/ppermute | solution.py:275
  63.3 2.2 %collective-permute-start.7 = (bf16[2,128,8,128]{3,2,1,0:T(8,128)(2,1)S(1)}, bf16[2,128,8,128]{3,2,1,0:T(8,128)(2,1)S(1)}, u32[]{:S(2)}, u32[]{:S(2)}) collective-permute-start(bf16[2,128,8,128]{3,2,1,0:T(8,128)(2,1)S(1)} %pad_maximum_fusion.3.refs_1_), channel_id=1, source_target_pairs={{0,12},{1,13},{2,14},{3,15},{4,0},{5,1},{6,2},{7,3},{8,4},{9,5},{1... | collective-permute-start | bytes 1572872 | tf_op jit(solution)/shard_map/ppermute | solution.py:275
  65.5 1.9 %collective-permute-start.16 = (bf16[2,128,8,128]{3,2,1,0:T(8,128)(2,1)S(1)}, bf16[2,128,8,128]{3,2,1,0:T(8,128)(2,1)S(1)}, u32[]{:S(2)}, u32[]{:S(2)}) collective-permute-start(bf16[2,128,8,128]{3,2,1,0:T(8,128)(2,1)S(1)} %collective-permute-done.14.refs_13_), channel_id=1, source_target_pairs={{0,448},{1,449},{2,450},{3,451},{4,452},{5,453},{6,454},{7,455},{8... | collective-permute-start | bytes 1572872 | tf_op jit(solution)/shard_map/ppermute | solution.py:275
  67.4 4.4 %collective-permute-start.6 = (bf16[2,128,8,128]{3,2,1,0:T(8,128)(2,1)S(1)}, bf16[2,128,8,128]{3,2,1,0:T(8,128)(2,1)S(1)}, u32[]{:S(2)}, u32[]{:S(2)}) collective-permute-start(bf16[2,128,8,128]{3,2,1,0:T(8,128)(2,1)S(1)} %pad_maximum_fusion.2.refs_0_), channel_id=1, source_target_pairs={{0,12},{1,13},{2,14},{3,15},{4,0},{5,1},{6,2},{7,3},{8,4},{9,5},{1... | collective-permute-start | bytes 1572872 | tf_op jit(solution)/shard_map/ppermute | solution.py:275
  71.9 3.4 %collective-permute-start.15 = (bf16[2,128,8,128]{3,2,1,0:T(8,128)(2,1)S(1)}, bf16[2,128,8,128]{3,2,1,0:T(8,128)(2,1)S(1)}, u32[]{:S(2)}, u32[]{:S(2)}) collective-permute-start(bf16[2,128,8,128]{3,2,1,0:T(8,128)(2,1)S(1)} %collective-permute-done.13.refs_12_), channel_id=1, source_target_pairs={{0,64},{1,65},{2,66},{3,67},{4,68},{5,69},{6,70},{7,71},{8,72},{9,... | collective-permute-start | bytes 1572872 | tf_op jit(solution)/shard_map/ppermute | solution.py:275
  75.2 1.9 %collective-permute-start.5 = (bf16[2,128,8,128]{3,2,1,0:T(8,128)(2,1)S(1)}, bf16[2,128,8,128]{3,2,1,0:T(8,128)(2,1)S(1)}, u32[]{:S(2)}, u32[]{:S(2)}) collective-permute-start(bf16[2,128,8,128]{3,2,1,0:T(8,128)(2,1)S(1)} %pad_maximum_fusion.3.refs_1_), channel_id=1, source_target_pairs={{0,4},{1,5},{2,6},{3,7},{4,8},{5,9},{6,10},{7,11},{8,12},{9,13},{1... | collective-permute-start | bytes 1572872 | tf_op jit(solution)/shard_map/ppermute | solution.py:275
  77.2 2.1 %collective-permute-start.8 = (bf16[2,128,8,128]{3,2,1,0:T(8,128)(2,1)S(1)}, bf16[2,128,8,128]{3,2,1,0:T(8,128)(2,1)S(1)}, u32[]{:S(2)}, u32[]{:S(2)}) collective-permute-start(bf16[2,128,8,128]{3,2,1,0:T(8,128)(2,1)S(1)} %collective-permute-done.4.refs_2_), channel_id=1, source_target_pairs={{0,4},{1,5},{2,6},{3,7},{4,8},{5,9},{6,10},{7,11},{8,12},{9,13},{1... | collective-permute-start | bytes 1572872 | tf_op jit(solution)/shard_map/ppermute | solution.py:275
  79.3 3.8 %collective-permute-start.9 = (bf16[2,128,8,128]{3,2,1,0:T(8,128)(2,1)S(1)}, bf16[2,128,8,128]{3,2,1,0:T(8,128)(2,1)S(1)}, u32[]{:S(2)}, u32[]{:S(2)}) collective-permute-start(bf16[2,128,8,128]{3,2,1,0:T(8,128)(2,1)S(1)} %collective-permute-done.7.refs_5_), channel_id=1, source_target_pairs={{0,12},{1,13},{2,14},{3,15},{4,0},{5,1},{6,2},{7,3},{8,4},{9,5},{1... | collective-permute-start | bytes 1572872 | tf_op jit(solution)/shard_map/ppermute | solution.py:275
  83.1 3.9 %collective-permute-done.6.refs_4_ = bf16[2,128,8,128]{3,2,1,0:T(8,128)(2,1)S(1)} collective-permute-done((bf16[2,128,8,128]{3,2,1,0:T(8,128)(2,1)S(1)}, bf16[2,128,8,128]{3,2,1,0:T(8,128)(2,1)S(1)}, u32[]{:S(2)}, u32[]{:S(2)}) %collective-permute-start.6) | collective-permute-done | bytes 524320 | tf_op jit(solution)/shard_map/ppermute | solution.py:275
  87.1 1.9 %collective-permute-start.18 = (bf16[128,8,128]{2,1,0:T(8,128)(2,1)S(1)}, bf16[128,8,128]{2,1,0:T(8,128)(2,1)S(1)}, u32[]{:S(2)}, u32[]{:S(2)}) collective-permute-start(bf16[128,8,128]{2,1,0:T(8,128)(2,1)S(1)} %slice_bitcast_fusion), channel_id=1, source_target_pairs={{0,448},{1,449},{2,450},{3,451},{4,452},{5,453},{6,454},{7,455},{8... | collective-permute-start | bytes 786440 | tf_op jit(solution)/shard_map/ppermute | solution.py:275
  89.0 3.4 %collective-permute-start.17 = (bf16[2,128,8,128]{3,2,1,0:T(8,128)(2,1)S(1)}, bf16[2,128,8,128]{3,2,1,0:T(8,128)(2,1)S(1)}, u32[]{:S(2)}, u32[]{:S(2)}) collective-permute-start(bf16[2,128,8,128]{3,2,1,0:T(8,128)(2,1)S(1)} %collective-permute-done.15.refs_14_), channel_id=1, source_target_pairs={{0,64},{1,65},{2,66},{3,67},{4,68},{5,69},{6,70},{7,71},{8,72},{9,... | collective-permute-start | bytes 1572872 | tf_op jit(solution)/shard_map/ppermute | solution.py:275
  92.4 2.1 %collective-permute-done.18.refs_17_ = bf16[128,8,128]{2,1,0:T(8,128)(2,1)S(1)} collective-permute-done((bf16[128,8,128]{2,1,0:T(8,128)(2,1)S(1)}, bf16[128,8,128]{2,1,0:T(8,128)(2,1)S(1)}, u32[]{:S(2)}, u32[]{:S(2)}) %collective-permute-start.18) | collective-permute-done | bytes 262176 | tf_op jit(solution)/shard_map/ppermute | solution.py:275
  94.5 2.8 %collective-permute-start.19 = (bf16[128,8,128]{2,1,0:T(8,128)(2,1)S(1)}, bf16[128,8,128]{2,1,0:T(8,128)(2,1)S(1)}, u32[]{:S(2)}, u32[]{:S(2)}) collective-permute-start(bf16[128,8,128]{2,1,0:T(8,128)(2,1)S(1)} %collective-permute-done.18.refs_17_), channel_id=1, source_target_pairs={{0,448},{1,449},{2,450},{3,451},{4,452},{5,453},{6,454},{7,455},{8... | collective-permute-start | bytes 786440 | tf_op jit(solution)/shard_map/ppermute | solution.py:275
  97.3 1.5 %collective-permute-done.8.refs_6_ = bf16[2,128,8,128]{3,2,1,0:T(8,128)(2,1)S(1)} collective-permute-done((bf16[2,128,8,128]{3,2,1,0:T(8,128)(2,1)S(1)}, bf16[2,128,8,128]{3,2,1,0:T(8,128)(2,1)S(1)}, u32[]{:S(2)}, u32[]{:S(2)}) %collective-permute-start.8) | collective-permute-done | bytes 524320 | tf_op jit(solution)/shard_map/ppermute | solution.py:275
  98.9 5.7 %collective-permute-done.19.refs_18_ = bf16[128,8,128]{2,1,0:T(8,128)(2,1)S(1)} collective-permute-done((bf16[128,8,128]{2,1,0:T(8,128)(2,1)S(1)}, bf16[128,8,128]{2,1,0:T(8,128)(2,1)S(1)}, u32[]{:S(2)}, u32[]{:S(2)}) %collective-permute-start.19) | collective-permute-done | bytes 262176 | tf_op jit(solution)/shard_map/ppermute | solution.py:275
  104.5 12.5 %cross.1 = (bf16[64,128,128]{2,1,0:T(8,128)(2,1)S(1)}, f32[64,128,128]{2,1,0:T(8,128)S(1)}) custom-call(bf16[2,128,8,128]{3,2,1,0:T(8,128)(2,1)S(1)} %pad_maximum_fusion.2.refs_0_, bf16[2,128,8,128]{3,2,1,0:T(8,128)(2,1)S(1)} %pad_maximum_fusion.3.refs_1_, bf16[2,128,8,128]{3,2,1,0:T(8,128)(2,1)S(1)} %collective-permute-done.4.refs_2_, ...), custom_call_target="tpu_custom_call" | custom-call | tf_op jit(solution)/shard_map/cross/pallas_call | solution.py:230
  117.1 10.7 %collective-permute-start.20 = (bf16[64,128,128]{2,1,0:T(8,128)(2,1)S(1)}, bf16[64,128,128]{2,1,0:T(8,128)(2,1)S(1)}, u32[]{:S(2)}, u32[]{:S(2)}) collective-permute-start(bf16[64,128,128]{2,1,0:T(8,128)(2,1)S(1)} %get-tuple-element.12), channel_id=1, source_target_pairs={{0,16},{1,17},{2,18},{3,19},{4,20},{5,21},{6,22},{7,23},{8,24},{9,... | collective-permute-start | bytes 6291464 | tf_op jit(solution)/shard_map/ppermute | solution.py:275
  127.8 3.8 %collective-permute-done.20 = bf16[64,128,128]{2,1,0:T(8,128)(2,1)S(1)} collective-permute-done((bf16[64,128,128]{2,1,0:T(8,128)(2,1)S(1)}, bf16[64,128,128]{2,1,0:T(8,128)(2,1)S(1)}, u32[]{:S(2)}, u32[]{:S(2)}) %collective-permute-start.20) | collective-permute-done | bytes 2097184 | tf_op jit(solution)/shard_map/ppermute | solution.py:275
  131.6 2.0 %add_convert_fusion = bf16[64,128,128]{2,1,0:T(8,128)(2,1)} fusion(f32[64,128,128]{2,1,0:T(8,128)S(1)} %get-tuple-element.11, bf16[64,128,128]{2,1,0:T(8,128)(2,1)S(1)} %collective-permute-done.20), kind=kLoop, calls=%fused_computation | loop fusion | flops 3145728 | bytes 8388608 | tf_op jit(solution)/shard_map/convert_element_type | solution.py:304
  (20 shorter events, 2.7 us)
Async XLA Ops:
  3.0 3.6 %collective-permute-start = (bf16[512,128]{1,0:T(8,128)(2,1)S(1)}, bf16[512,128]{1,0:T(8,128)(2,1)S(1)}, u32[]{:S(2)}, u32[]{:S(2)}) collective-permute-start(bf16[512,128]{1,0:T(8,128)(2,1)S(1)} %get-tuple-element.10), channel_id=1, source_target_pairs={{0,16},{1,17},{2,18},{3,19},{4,20},{5,21},{6,22},{7,23},{8,24},{9,... | collective-permute-start | bytes 393224 | tf_op jit(solution)/shard_map/ppermute | solution.py:275
  6.7 15.9 %collective-permute-start.12 = (bf16[128,8,128]{2,1,0:T(8,128)(2,1)S(1)}, bf16[128,8,128]{2,1,0:T(8,128)(2,1)S(1)}, u32[]{:S(2)}, u32[]{:S(2)}) collective-permute-start(bf16[128,8,128]{2,1,0:T(8,128)(2,1)S(1)} %bitcast.11), channel_id=1, source_target_pairs={{0,448},{1,449},{2,450},{3,451},{4,452},{5,453},{6,454},{7,455},{8... | collective-permute-start | bytes 786440 | tf_op jit(solution)/shard_map/ppermute | solution.py:275
  11.8 10.8 %collective-permute-start.11 = (bf16[128,8,128]{2,1,0:T(8,128)(2,1)S(1)}, bf16[128,8,128]{2,1,0:T(8,128)(2,1)S(1)}, u32[]{:S(2)}, u32[]{:S(2)}) collective-permute-start(bf16[128,8,128]{2,1,0:T(8,128)(2,1)S(1)} %bitcast.12), channel_id=1, source_target_pairs={{0,64},{1,65},{2,66},{3,67},{4,68},{5,69},{6,70},{7,71},{8,72},{9,... | collective-permute-start | bytes 786440 | tf_op jit(solution)/shard_map/ppermute | solution.py:275
  13.7 21.2 %collective-permute-start.10 = (bf16[128,8,128]{2,1,0:T(8,128)(2,1)S(1)}, bf16[128,8,128]{2,1,0:T(8,128)(2,1)S(1)}, u32[]{:S(2)}, u32[]{:S(2)}) collective-permute-start(bf16[128,8,128]{2,1,0:T(8,128)(2,1)S(1)} %bitcast.13), channel_id=1, source_target_pairs={{0,32},{1,33},{2,34},{3,35},{4,36},{5,37},{6,38},{7,39},{8,40},{9,... | collective-permute-start | bytes 786440 | tf_op jit(solution)/shard_map/ppermute | solution.py:275
  35.0 69.6 %copy-start = (bf16[2,128,256]{2,1,0:T(8,128)(2,1)S(1)}, bf16[2,128,256]{2,1,0:T(8,128)(2,1)}, u32[]{:S(2)}) copy-start(bf16[2,128,256]{2,1,0:T(8,128)(2,1)} %constant.8.clone.refs_19_) | copy-start | bytes 393220
  35.0 30.5 %collective-permute-start.14 = (bf16[2,128,8,128]{3,2,1,0:T(8,128)(2,1)S(1)}, bf16[2,128,8,128]{3,2,1,0:T(8,128)(2,1)S(1)}, u32[]{:S(2)}, u32[]{:S(2)}) collective-permute-start(bf16[2,128,8,128]{3,2,1,0:T(8,128)(2,1)S(1)} %get-tuple-element.13), channel_id=1, source_target_pairs={{0,448},{1,449},{2,450},{3,451},{4,452},{5,453},{6,454},{7,455},{8... | collective-permute-start | bytes 1572872 | tf_op jit(solution)/shard_map/ppermute | solution.py:275
  39.6 10.5 %collective-permute-start.1 = (bf16[128,8,128]{2,1,0:T(8,128)(2,1)S(1)}, bf16[128,8,128]{2,1,0:T(8,128)(2,1)S(1)}, u32[]{:S(2)}, u32[]{:S(2)}) collective-permute-start(bf16[128,8,128]{2,1,0:T(8,128)(2,1)S(1)} %bitcast.14), channel_id=1, source_target_pairs={{0,1},{1,2},{2,3},{3,0},{4,5},{5,6},{6,7},{7,4},{8,9},{9,10},{10,1... | collective-permute-start | bytes 786440 | tf_op jit(solution)/shard_map/ppermute | solution.py:275
  41.5 16.1 %collective-permute-start.3 = (bf16[128,8,128]{2,1,0:T(8,128)(2,1)S(1)}, bf16[128,8,128]{2,1,0:T(8,128)(2,1)S(1)}, u32[]{:S(2)}, u32[]{:S(2)}) collective-permute-start(bf16[128,8,128]{2,1,0:T(8,128)(2,1)S(1)} %bitcast.15), channel_id=1, source_target_pairs={{0,2},{1,3},{2,0},{3,1},{4,6},{5,7},{6,4},{7,5},{8,10},{9,11},{10,... | collective-permute-start | bytes 786440 | tf_op jit(solution)/shard_map/ppermute | solution.py:275
  43.9 19.4 %collective-permute-start.2 = (bf16[128,8,128]{2,1,0:T(8,128)(2,1)S(1)}, bf16[128,8,128]{2,1,0:T(8,128)(2,1)S(1)}, u32[]{:S(2)}, u32[]{:S(2)}) collective-permute-start(bf16[128,8,128]{2,1,0:T(8,128)(2,1)S(1)} %bitcast.16), channel_id=1, source_target_pairs={{0,3},{1,0},{2,1},{3,2},{4,7},{5,4},{6,5},{7,6},{8,11},{9,8},{10,9... | collective-permute-start | bytes 786440 | tf_op jit(solution)/shard_map/ppermute | solution.py:275
  46.8 25.0 %collective-permute-start.13 = (bf16[2,128,8,128]{3,2,1,0:T(8,128)(2,1)S(1)}, bf16[2,128,8,128]{3,2,1,0:T(8,128)(2,1)S(1)}, u32[]{:S(2)}, u32[]{:S(2)}) collective-permute-start(bf16[2,128,8,128]{3,2,1,0:T(8,128)(2,1)S(1)} %get-tuple-element.14), channel_id=1, source_target_pairs={{0,64},{1,65},{2,66},{3,67},{4,68},{5,69},{6,70},{7,71},{8,72},{9,... | collective-permute-start | bytes 1572872 | tf_op jit(solution)/shard_map/ppermute | solution.py:275
  50.2 25.0 %collective-permute-start.4 = (bf16[2,128,8,128]{3,2,1,0:T(8,128)(2,1)S(1)}, bf16[2,128,8,128]{3,2,1,0:T(8,128)(2,1)S(1)}, u32[]{:S(2)}, u32[]{:S(2)}) collective-permute-start(bf16[2,128,8,128]{3,2,1,0:T(8,128)(2,1)S(1)} %pad_maximum_fusion.2.refs_0_), channel_id=1, source_target_pairs={{0,4},{1,5},{2,6},{3,7},{4,8},{5,9},{6,10},{7,11},{8,12},{9,13},{1... | collective-permute-start | bytes 1572872 | tf_op jit(solution)/shard_map/ppermute | solution.py:275
  63.3 13.8 %collective-permute-start.7 = (bf16[2,128,8,128]{3,2,1,0:T(8,128)(2,1)S(1)}, bf16[2,128,8,128]{3,2,1,0:T(8,128)(2,1)S(1)}, u32[]{:S(2)}, u32[]{:S(2)}) collective-permute-start(bf16[2,128,8,128]{3,2,1,0:T(8,128)(2,1)S(1)} %pad_maximum_fusion.3.refs_1_), channel_id=1, source_target_pairs={{0,12},{1,13},{2,14},{3,15},{4,0},{5,1},{6,2},{7,3},{8,4},{9,5},{1... | collective-permute-start | bytes 1572872 | tf_op jit(solution)/shard_map/ppermute | solution.py:275
  65.5 13.8 %collective-permute-start.16 = (bf16[2,128,8,128]{3,2,1,0:T(8,128)(2,1)S(1)}, bf16[2,128,8,128]{3,2,1,0:T(8,128)(2,1)S(1)}, u32[]{:S(2)}, u32[]{:S(2)}) collective-permute-start(bf16[2,128,8,128]{3,2,1,0:T(8,128)(2,1)S(1)} %collective-permute-done.14.refs_13_), channel_id=1, source_target_pairs={{0,448},{1,449},{2,450},{3,451},{4,452},{5,453},{6,454},{7,455},{8... | collective-permute-start | bytes 1572872 | tf_op jit(solution)/shard_map/ppermute | solution.py:275
  67.4 19.6 %collective-permute-start.6 = (bf16[2,128,8,128]{3,2,1,0:T(8,128)(2,1)S(1)}, bf16[2,128,8,128]{3,2,1,0:T(8,128)(2,1)S(1)}, u32[]{:S(2)}, u32[]{:S(2)}) collective-permute-start(bf16[2,128,8,128]{3,2,1,0:T(8,128)(2,1)S(1)} %pad_maximum_fusion.2.refs_0_), channel_id=1, source_target_pairs={{0,12},{1,13},{2,14},{3,15},{4,0},{5,1},{6,2},{7,3},{8,4},{9,5},{1... | collective-permute-start | bytes 1572872 | tf_op jit(solution)/shard_map/ppermute | solution.py:275
  71.9 17.1 %collective-permute-start.15 = (bf16[2,128,8,128]{3,2,1,0:T(8,128)(2,1)S(1)}, bf16[2,128,8,128]{3,2,1,0:T(8,128)(2,1)S(1)}, u32[]{:S(2)}, u32[]{:S(2)}) collective-permute-start(bf16[2,128,8,128]{3,2,1,0:T(8,128)(2,1)S(1)} %collective-permute-done.13.refs_12_), channel_id=1, source_target_pairs={{0,64},{1,65},{2,66},{3,67},{4,68},{5,69},{6,70},{7,71},{8,72},{9,... | collective-permute-start | bytes 1572872 | tf_op jit(solution)/shard_map/ppermute | solution.py:275
  75.2 22.1 %collective-permute-start.5 = (bf16[2,128,8,128]{3,2,1,0:T(8,128)(2,1)S(1)}, bf16[2,128,8,128]{3,2,1,0:T(8,128)(2,1)S(1)}, u32[]{:S(2)}, u32[]{:S(2)}) collective-permute-start(bf16[2,128,8,128]{3,2,1,0:T(8,128)(2,1)S(1)} %pad_maximum_fusion.3.refs_1_), channel_id=1, source_target_pairs={{0,4},{1,5},{2,6},{3,7},{4,8},{5,9},{6,10},{7,11},{8,12},{9,13},{1... | collective-permute-start | bytes 1572872 | tf_op jit(solution)/shard_map/ppermute | solution.py:275
  77.2 21.7 %collective-permute-start.8 = (bf16[2,128,8,128]{3,2,1,0:T(8,128)(2,1)S(1)}, bf16[2,128,8,128]{3,2,1,0:T(8,128)(2,1)S(1)}, u32[]{:S(2)}, u32[]{:S(2)}) collective-permute-start(bf16[2,128,8,128]{3,2,1,0:T(8,128)(2,1)S(1)} %collective-permute-done.4.refs_2_), channel_id=1, source_target_pairs={{0,4},{1,5},{2,6},{3,7},{4,8},{5,9},{6,10},{7,11},{8,12},{9,13},{1... | collective-permute-start | bytes 1572872 | tf_op jit(solution)/shard_map/ppermute | solution.py:275
  79.3 19.6 %collective-permute-start.9 = (bf16[2,128,8,128]{3,2,1,0:T(8,128)(2,1)S(1)}, bf16[2,128,8,128]{3,2,1,0:T(8,128)(2,1)S(1)}, u32[]{:S(2)}, u32[]{:S(2)}) collective-permute-start(bf16[2,128,8,128]{3,2,1,0:T(8,128)(2,1)S(1)} %collective-permute-done.7.refs_5_), channel_id=1, source_target_pairs={{0,12},{1,13},{2,14},{3,15},{4,0},{5,1},{6,2},{7,3},{8,4},{9,5},{1... | collective-permute-start | bytes 1572872 | tf_op jit(solution)/shard_map/ppermute | solution.py:275
  87.1 7.4 %collective-permute-start.18 = (bf16[128,8,128]{2,1,0:T(8,128)(2,1)S(1)}, bf16[128,8,128]{2,1,0:T(8,128)(2,1)S(1)}, u32[]{:S(2)}, u32[]{:S(2)}) collective-permute-start(bf16[128,8,128]{2,1,0:T(8,128)(2,1)S(1)} %slice_bitcast_fusion), channel_id=1, source_target_pairs={{0,448},{1,449},{2,450},{3,451},{4,452},{5,453},{6,454},{7,455},{8... | collective-permute-start | bytes 786440 | tf_op jit(solution)/shard_map/ppermute | solution.py:275
  89.0 15.5 %collective-permute-start.17 = (bf16[2,128,8,128]{3,2,1,0:T(8,128)(2,1)S(1)}, bf16[2,128,8,128]{3,2,1,0:T(8,128)(2,1)S(1)}, u32[]{:S(2)}, u32[]{:S(2)}) collective-permute-start(bf16[2,128,8,128]{3,2,1,0:T(8,128)(2,1)S(1)} %collective-permute-done.15.refs_14_), channel_id=1, source_target_pairs={{0,64},{1,65},{2,66},{3,67},{4,68},{5,69},{6,70},{7,71},{8,72},{9,... | collective-permute-start | bytes 1572872 | tf_op jit(solution)/shard_map/ppermute | solution.py:275
  94.5 10.1 %collective-permute-start.19 = (bf16[128,8,128]{2,1,0:T(8,128)(2,1)S(1)}, bf16[128,8,128]{2,1,0:T(8,128)(2,1)S(1)}, u32[]{:S(2)}, u32[]{:S(2)}) collective-permute-start(bf16[128,8,128]{2,1,0:T(8,128)(2,1)S(1)} %collective-permute-done.18.refs_17_), channel_id=1, source_target_pairs={{0,448},{1,449},{2,450},{3,451},{4,452},{5,453},{6,454},{7,455},{8... | collective-permute-start | bytes 786440 | tf_op jit(solution)/shard_map/ppermute | solution.py:275
  117.1 14.5 %collective-permute-start.20 = (bf16[64,128,128]{2,1,0:T(8,128)(2,1)S(1)}, bf16[64,128,128]{2,1,0:T(8,128)(2,1)S(1)}, u32[]{:S(2)}, u32[]{:S(2)}) collective-permute-start(bf16[64,128,128]{2,1,0:T(8,128)(2,1)S(1)} %get-tuple-element.12), channel_id=1, source_target_pairs={{0,16},{1,17},{2,18},{3,19},{4,20},{5,21},{6,22},{7,23},{8,24},{9,... | collective-permute-start | bytes 6291464 | tf_op jit(solution)/shard_map/ppermute | solution.py:275

commit v3 on v2

--- a/solution.py
+++ b/solution.py
@@ -123,9 +123,7 @@
     )(in_vmem(keep), in_vmem(got))
 
 
-N_CHUNK = 4
 PITCH = 2 * HALF + 8
-CHUNK = HALF // N_CHUNK
 
 
 def placements():
@@ -143,38 +141,27 @@
     return row, col, firsts + seconds
 
 
-def cross_kernel(n_first, n_second, *refs):
-    row, col, where = placements()
+def cross_kernel(n_first, *refs):
+    firsts, seconds = refs[:n_first], refs[n_first:-5]
+    inv_ref, send_ref, own_ref, s_ref, place_ref = refs[-5:]
+    row, _, where = placements()
     core = row % N_C
-    n_in = len(n_first) + len(n_second)
-    inputs = refs[:n_in]
-    inv_ref, send_ref, own_ref, a_ref, b_ref, s_ref, sem = refs[n_in:]
-    copies = []
-    for chunk in range(N_CHUNK):
-        started = []
-        slot = 0
-        for index, ref in enumerate(inputs):
-            count = (n_first + n_second)[index]
-            dst = a_ref if index < len(n_first) else b_ref
-            for piece in range(count):
-                src = ref.at[piece] if count > 1 else ref
-                place = pl.multiple_of(where[slot] * 8, 8)
-                bins = pl.ds(chunk * CHUNK, CHUNK)
-                copy = pltpu.make_async_copy(
-                    src.at[bins], dst.at[bins, pl.ds(place, 8), :], sem.at[chunk, slot]
-                )
-                copy.start()
-                started.append(copy)
-                slot += 1
-        copies.append(started)
+    for slot in range(16):
+        place_ref[slot] = where[slot]
     sign = jnp.where(
         lax.broadcasted_iota(jnp.int32, (128, 2 * NW), 1) < NW, 1.0, -1.0
     ).astype(jnp.bfloat16)
     contract = (((1,), (1,)), ((), ()))
 
+    def gather(blocks, f):
+        parts = []
+        for ref in blocks:
+            parts += [ref[f]] if len(ref.shape) == 3 else [ref[n, f] for n in range(ref.shape[0])]
+        return jnp.concatenate(parts, axis=0)
+
     def one_bin(f, carry):
-        a = a_ref[f]
-        b = b_ref[f]
+        a = gather(firsts, f)
+        b = gather(seconds, f)
         turned = jnp.concatenate([a[:, NW:], a[:, :NW]], axis=1) * sign
         both = jnp.concatenate([a, turned], axis=0)
         terms = lax.dot_general(both, b, contract, preferred_element_type=jnp.float32)
@@ -182,31 +169,26 @@
         s_ref[pl.ds(f + HALF, 128, stride=PITCH), :] = terms[128:]
         return carry
 
-    for chunk in range(N_CHUNK):
-        for copy in copies[chunk]:
-            copy.wait()
-        lax.fori_loop(chunk * CHUNK, (chunk + 1) * CHUNK, one_bin, 0, unroll=16)
+    lax.fori_loop(0, HALF, one_bin, 0, unroll=UNROLL)
 
     lane = lax.broadcasted_iota(jnp.int32, (2 * HALF, 128), 1)
-    for side in range(N_C):
-        for ch in range(4):
-            start = pl.multiple_of((col * 8 + side * 4 + ch) * PITCH, 8)
-            same = lane == (row - core + side) * 4 + ch
-            stacked = s_ref[pl.ds(start, 2 * HALF), :]
-            s_ref[pl.ds(start, 2 * HALF), :] = jnp.where(same, 0.0, stacked)
+    for slot in range(8):
+        rows = pl.ds(slot * PITCH, 2 * HALF)
+        s_ref[rows, :] = jnp.where(lane == slot, 0.0, s_ref[rows, :])
     table = inv_ref[core]
+    spots = [pl.ds(pl.multiple_of(place * 8, 8), 8) for place in where[16:]]
 
     def lag_pair(step, which, out_ref):
         piece, half = step // 2, step % 2
-        row = piece * 8 + which * 4 + half * 2
-        start = pl.multiple_of(row * PITCH, 8)
+        start = pl.multiple_of((piece * 8 + which * 4 + half * 2) * PITCH, 8)
         w0 = s_ref[pl.ds(start, 2 * HALF), :].astype(jnp.bfloat16)
         w1 = s_ref[pl.ds(pl.multiple_of(start + PITCH, 8), 2 * HALF), :].astype(jnp.bfloat16)
-        both = jnp.concatenate([w0, w1], axis=1)
-        lagged = jnp.dot(table, both, preferred_element_type=jnp.float32)
-        i = piece * 4 + half * 2
-        out_ref[i] = lagged[:, :128].T.astype(out_ref.dtype)
-        out_ref[i + 1] = lagged[:, 128:].T.astype(out_ref.dtype)
+        lagged = jnp.dot(table, jnp.concatenate([w0, w1], axis=1), preferred_element_type=jnp.float32)
+        i = place_ref[piece] * 4 + half * 2
+        for n in range(2):
+            block = lagged[:, n * 128 : (n + 1) * 128].T
+            for slot in range(16):
+                out_ref[i + n, spots[slot], :] = block[slot * 8 : slot * 8 + 8].astype(out_ref.dtype)
 
     def send_step(step, carry):
         lag_pair(step, 1 - core, send_ref)
@@ -216,30 +198,27 @@
         lag_pair(step, core, own_ref)
         return carry
 
-    lax.fori_loop(0, 32, send_step, 0, unroll=8)
-    lax.fori_loop(0, 32, own_step, 0, unroll=8)
+    lax.fori_loop(0, 32, send_step, 0, unroll=16)
+    lax.fori_loop(0, 32, own_step, 0, unroll=16)
+
+
+UNROLL = 16
 
 
 def cross(firsts, seconds, inverse):
-    count = lambda x: 1 if x.ndim == 3 else x.shape[0]
-    n_first = tuple(count(x) for x in firsts)
-    n_second = tuple(count(x) for x in seconds)
-    kernel = lambda *refs: cross_kernel(n_first, n_second, *refs)
+    kernel = lambda *refs: cross_kernel(len(firsts), *refs)
     vmem = pl.BlockSpec(memory_space=pltpu.VMEM)
-    n_in = len(firsts) + len(seconds)
     return pl.pallas_call(
         kernel,
         out_shape=(
             pltpu.VMEM((64, 128, LAGS), jnp.bfloat16),
             pltpu.VMEM((64, 128, LAGS), jnp.float32),
         ),
-        in_specs=[vmem] * (n_in + 1),
+        in_specs=[vmem] * (len(firsts) + len(seconds) + 1),
         out_specs=(vmem, vmem),
         scratch_shapes=[
-            pltpu.VMEM((HALF, 128, 2 * NW), jnp.bfloat16),
-            pltpu.VMEM((HALF, 128, 2 * NW), jnp.bfloat16),
             pltpu.VMEM((128 * PITCH, 128), jnp.float32),
-            pltpu.SemaphoreType.DMA((N_CHUNK, 32)),
+            pltpu.SMEM((16,), jnp.int32),
         ],
         compiler_params=pltpu.CompilerParams(vmem_limit_bytes=32 * 1024 * 1024),
         name="cross",

time: 134 us -> 129 us (0.963)
  Pallas kernels: 15.7 us -> 10.8 us
    pallas_call x1, Pallas kernels: 12.5 us -> 7.62 us  [cross(): pl.pallas_call(kernel, out_shape=(pltpu.VMEM((64, 128, LAGS), jnp.bfloat1...]
where the time goes in v3:
time: 129 us
  starting transfers between devices  73.7 us (57%)
  waiting for transfers between devices  41.7 us (32%)
  Pallas kernels  10.8 us (8%)
  other arithmetic  2.19 us (2%)
    ppermute x21, starting transfers between devices, move(): return lax.ppermute(value, AXES, pairs)  73.7 us
    ppermute x21, waiting for transfers between devices, move(): return lax.ppermute(value, AXES, pairs)  41.7 us
    pallas_call x1, Pallas kernels, cross(): pl.pallas_call(kernel, out_shape=(pltpu.VMEM((64, 128, LAGS), jnp.bfloat1...  7.62 us
    pallas_call x1, Pallas kernels, whiten(): pl.pallas_call(whiten_kernel, out_shape=(shape, shape), in_specs=[smem, v...  3.02 us
  transfers between devices with their start and end apart: 21, of which 10 were waited for; matrix products, arithmetic and copies ran while one was open for 0% of the time, Pallas kernels for 0%

profile of v3, /device:TPU:131, one launch (start us, length us, event | category | flops | bytes accessed | tf_op | source)
XLA Modules:
  0.0 128.6 jit_solution(1941688220943898820)
XLA Ops:
  0.0 3.0 %whiten.1 = (bf16[512,128]{1,0:T(8,128)(2,1)S(1)}, bf16[512,128]{1,0:T(8,128)(2,1)S(1)}) custom-call(s32[4]{0:T(128)} %flags_ref.1, bf16[256,512]{1,0:T(8,128)(2,1)} %bitcast.22, bf16[3,512,512]{2,1,0:T(8,128)(2,1)} %constant.6.clone.dft_ref, f32[256,256]{1,0:T(8,128)} %constant.7.clone.near_ref), custom_call_target="tpu_custom_call" | custom-call | tf_op jit(solution)/shard_map/whiten/pallas_call | solution.py:92
  3.0 2.6 %collective-permute-start = (bf16[512,128]{1,0:T(8,128)(2,1)S(1)}, bf16[512,128]{1,0:T(8,128)(2,1)S(1)}, u32[]{:S(2)}, u32[]{:S(2)}) collective-permute-start(bf16[512,128]{1,0:T(8,128)(2,1)S(1)} %get-tuple-element.10), channel_id=1, source_target_pairs={{0,16},{1,17},{2,18},{3,19},{4,20},{5,21},{6,22},{7,23},{8,24},{9,... | collective-permute-start | bytes 393224 | tf_op jit(solution)/shard_map/ppermute | solution.py:254
  6.7 5.1 %collective-permute-start.12 = (bf16[128,8,128]{2,1,0:T(8,128)(2,1)S(1)}, bf16[128,8,128]{2,1,0:T(8,128)(2,1)S(1)}, u32[]{:S(2)}, u32[]{:S(2)}) collective-permute-start(bf16[128,8,128]{2,1,0:T(8,128)(2,1)S(1)} %bitcast.11), channel_id=1, source_target_pairs={{0,448},{1,449},{2,450},{3,451},{4,452},{5,453},{6,454},{7,455},{8... | collective-permute-start | bytes 786440 | tf_op jit(solution)/shard_map/ppermute | solution.py:254
  11.8 1.9 %collective-permute-start.11 = (bf16[128,8,128]{2,1,0:T(8,128)(2,1)S(1)}, bf16[128,8,128]{2,1,0:T(8,128)(2,1)S(1)}, u32[]{:S(2)}, u32[]{:S(2)}) collective-permute-start(bf16[128,8,128]{2,1,0:T(8,128)(2,1)S(1)} %bitcast.12), channel_id=1, source_target_pairs={{0,64},{1,65},{2,66},{3,67},{4,68},{5,69},{6,70},{7,71},{8,72},{9,... | collective-permute-start | bytes 786440 | tf_op jit(solution)/shard_map/ppermute | solution.py:254
  13.7 8.8 %collective-permute-start.10 = (bf16[128,8,128]{2,1,0:T(8,128)(2,1)S(1)}, bf16[128,8,128]{2,1,0:T(8,128)(2,1)S(1)}, u32[]{:S(2)}, u32[]{:S(2)}) collective-permute-start(bf16[128,8,128]{2,1,0:T(8,128)(2,1)S(1)} %bitcast.13), channel_id=1, source_target_pairs={{0,32},{1,33},{2,34},{3,35},{4,36},{5,37},{6,38},{7,39},{8,40},{9,... | collective-permute-start | bytes 786440 | tf_op jit(solution)/shard_map/ppermute | solution.py:254
  22.6 12.3 %collective-permute-done.10.refs_9_ = bf16[128,8,128]{2,1,0:T(8,128)(2,1)S(1)} collective-permute-done((bf16[128,8,128]{2,1,0:T(8,128)(2,1)S(1)}, bf16[128,8,128]{2,1,0:T(8,128)(2,1)S(1)}, u32[]{:S(2)}, u32[]{:S(2)}) %collective-permute-start.10) | collective-permute-done | bytes 262176 | tf_op jit(solution)/shard_map/ppermute | solution.py:254
  35.0 4.6 %collective-permute-start.14 = (bf16[2,128,8,128]{3,2,1,0:T(8,128)(2,1)S(1)}, bf16[2,128,8,128]{3,2,1,0:T(8,128)(2,1)S(1)}, u32[]{:S(2)}, u32[]{:S(2)}) collective-permute-start(bf16[2,128,8,128]{3,2,1,0:T(8,128)(2,1)S(1)} %get-tuple-element.13), channel_id=1, source_target_pairs={{0,448},{1,449},{2,450},{3,451},{4,452},{5,453},{6,454},{7,455},{8... | collective-permute-start | bytes 1572872 | tf_op jit(solution)/shard_map/ppermute | solution.py:254
  39.6 1.9 %collective-permute-start.1 = (bf16[128,8,128]{2,1,0:T(8,128)(2,1)S(1)}, bf16[128,8,128]{2,1,0:T(8,128)(2,1)S(1)}, u32[]{:S(2)}, u32[]{:S(2)}) collective-permute-start(bf16[128,8,128]{2,1,0:T(8,128)(2,1)S(1)} %bitcast.14), channel_id=1, source_target_pairs={{0,1},{1,2},{2,3},{3,0},{4,5},{5,6},{6,7},{7,4},{8,9},{9,10},{10,1... | collective-permute-start | bytes 786440 | tf_op jit(solution)/shard_map/ppermute | solution.py:254
  41.5 2.4 %collective-permute-start.3 = (bf16[128,8,128]{2,1,0:T(8,128)(2,1)S(1)}, bf16[128,8,128]{2,1,0:T(8,128)(2,1)S(1)}, u32[]{:S(2)}, u32[]{:S(2)}) collective-permute-start(bf16[128,8,128]{2,1,0:T(8,128)(2,1)S(1)} %bitcast.15), channel_id=1, source_target_pairs={{0,2},{1,3},{2,0},{3,1},{4,6},{5,7},{6,4},{7,5},{8,10},{9,11},{10,... | collective-permute-start | bytes 786440 | tf_op jit(solution)/shard_map/ppermute | solution.py:254
  43.9 2.9 %collective-permute-start.2 = (bf16[128,8,128]{2,1,0:T(8,128)(2,1)S(1)}, bf16[128,8,128]{2,1,0:T(8,128)(2,1)S(1)}, u32[]{:S(2)}, u32[]{:S(2)}) collective-permute-start(bf16[128,8,128]{2,1,0:T(8,128)(2,1)S(1)} %bitcast.16), channel_id=1, source_target_pairs={{0,3},{1,0},{2,1},{3,2},{4,7},{5,4},{6,5},{7,6},{8,11},{9,8},{10,9... | collective-permute-start | bytes 786440 | tf_op jit(solution)/shard_map/ppermute | solution.py:254
  46.8 1.9 %collective-permute-start.13 = (bf16[2,128,8,128]{3,2,1,0:T(8,128)(2,1)S(1)}, bf16[2,128,8,128]{3,2,1,0:T(8,128)(2,1)S(1)}, u32[]{:S(2)}, u32[]{:S(2)}) collective-permute-start(bf16[2,128,8,128]{3,2,1,0:T(8,128)(2,1)S(1)} %get-tuple-element.14), channel_id=1, source_target_pairs={{0,64},{1,65},{2,66},{3,67},{4,68},{5,69},{6,70},{7,71},{8,72},{9,... | collective-permute-start | bytes 1572872 | tf_op jit(solution)/shard_map/ppermute | solution.py:254
  50.2 3.1 %collective-permute-start.4 = (bf16[2,128,8,128]{3,2,1,0:T(8,128)(2,1)S(1)}, bf16[2,128,8,128]{3,2,1,0:T(8,128)(2,1)S(1)}, u32[]{:S(2)}, u32[]{:S(2)}) collective-permute-start(bf16[2,128,8,128]{3,2,1,0:T(8,128)(2,1)S(1)} %pad_maximum_fusion.2.refs_0_), channel_id=1, source_target_pairs={{0,4},{1,5},{2,6},{3,7},{4,8},{5,9},{6,10},{7,11},{8,12},{9,13},{1... | collective-permute-start | bytes 1572872 | tf_op jit(solution)/shard_map/ppermute | solution.py:254
  53.3 4.4 %collective-permute-done.3 = bf16[128,8,128]{2,1,0:T(8,128)(2,1)S(1)} collective-permute-done((bf16[128,8,128]{2,1,0:T(8,128)(2,1)S(1)}, bf16[128,8,128]{2,1,0:T(8,128)(2,1)S(1)}, u32[]{:S(2)}, u32[]{:S(2)}) %collective-permute-start.3) | collective-permute-done | bytes 262176 | tf_op jit(solution)/shard_map/ppermute | solution.py:254
  57.7 5.6 %collective-permute-done.2 = bf16[128,8,128]{2,1,0:T(8,128)(2,1)S(1)} collective-permute-done((bf16[128,8,128]{2,1,0:T(8,128)(2,1)S(1)}, bf16[128,8,128]{2,1,0:T(8,128)(2,1)S(1)}, u32[]{:S(2)}, u32[]{:S(2)}) %collective-permute-start.2) | collective-permute-done | bytes 262176 | tf_op jit(solution)/shard_map/ppermute | solution.py:254
  63.3 2.2 %collective-permute-start.7 = (bf16[2,128,8,128]{3,2,1,0:T(8,128)(2,1)S(1)}, bf16[2,128,8,128]{3,2,1,0:T(8,128)(2,1)S(1)}, u32[]{:S(2)}, u32[]{:S(2)}) collective-permute-start(bf16[2,128,8,128]{3,2,1,0:T(8,128)(2,1)S(1)} %pad_maximum_fusion.3.refs_1_), channel_id=1, source_target_pairs={{0,12},{1,13},{2,14},{3,15},{4,0},{5,1},{6,2},{7,3},{8,4},{9,5},{1... | collective-permute-start | bytes 1572872 | tf_op jit(solution)/shard_map/ppermute | solution.py:254
  65.5 1.9 %collective-permute-start.16 = (bf16[2,128,8,128]{3,2,1,0:T(8,128)(2,1)S(1)}, bf16[2,128,8,128]{3,2,1,0:T(8,128)(2,1)S(1)}, u32[]{:S(2)}, u32[]{:S(2)}) collective-permute-start(bf16[2,128,8,128]{3,2,1,0:T(8,128)(2,1)S(1)} %collective-permute-done.14.refs_13_), channel_id=1, source_target_pairs={{0,448},{1,449},{2,450},{3,451},{4,452},{5,453},{6,454},{7,455},{8... | collective-permute-start | bytes 1572872 | tf_op jit(solution)/shard_map/ppermute | solution.py:254
  67.4 4.4 %collective-permute-start.6 = (bf16[2,128,8,128]{3,2,1,0:T(8,128)(2,1)S(1)}, bf16[2,128,8,128]{3,2,1,0:T(8,128)(2,1)S(1)}, u32[]{:S(2)}, u32[]{:S(2)}) collective-permute-start(bf16[2,128,8,128]{3,2,1,0:T(8,128)(2,1)S(1)} %pad_maximum_fusion.2.refs_0_), channel_id=1, source_target_pairs={{0,12},{1,13},{2,14},{3,15},{4,0},{5,1},{6,2},{7,3},{8,4},{9,5},{1... | collective-permute-start | bytes 1572872 | tf_op jit(solution)/shard_map/ppermute | solution.py:254
  71.9 3.4 %collective-permute-start.15 = (bf16[2,128,8,128]{3,2,1,0:T(8,128)(2,1)S(1)}, bf16[2,128,8,128]{3,2,1,0:T(8,128)(2,1)S(1)}, u32[]{:S(2)}, u32[]{:S(2)}) collective-permute-start(bf16[2,128,8,128]{3,2,1,0:T(8,128)(2,1)S(1)} %collective-permute-done.13.refs_12_), channel_id=1, source_target_pairs={{0,64},{1,65},{2,66},{3,67},{4,68},{5,69},{6,70},{7,71},{8,72},{9,... | collective-permute-start | bytes 1572872 | tf_op jit(solution)/shard_map/ppermute | solution.py:254
  75.2 1.9 %collective-permute-start.5 = (bf16[2,128,8,128]{3,2,1,0:T(8,128)(2,1)S(1)}, bf16[2,128,8,128]{3,2,1,0:T(8,128)(2,1)S(1)}, u32[]{:S(2)}, u32[]{:S(2)}) collective-permute-start(bf16[2,128,8,128]{3,2,1,0:T(8,128)(2,1)S(1)} %pad_maximum_fusion.3.refs_1_), channel_id=1, source_target_pairs={{0,4},{1,5},{2,6},{3,7},{4,8},{5,9},{6,10},{7,11},{8,12},{9,13},{1... | collective-permute-start | bytes 1572872 | tf_op jit(solution)/shard_map/ppermute | solution.py:254
  77.2 2.1 %collective-permute-start.8 = (bf16[2,128,8,128]{3,2,1,0:T(8,128)(2,1)S(1)}, bf16[2,128,8,128]{3,2,1,0:T(8,128)(2,1)S(1)}, u32[]{:S(2)}, u32[]{:S(2)}) collective-permute-start(bf16[2,128,8,128]{3,2,1,0:T(8,128)(2,1)S(1)} %collective-permute-done.4.refs_2_), channel_id=1, source_target_pairs={{0,4},{1,5},{2,6},{3,7},{4,8},{5,9},{6,10},{7,11},{8,12},{9,13},{1... | collective-permute-start | bytes 1572872 | tf_op jit(solution)/shard_map/ppermute | solution.py:254
  79.3 3.8 %collective-permute-start.9 = (bf16[2,128,8,128]{3,2,1,0:T(8,128)(2,1)S(1)}, bf16[2,128,8,128]{3,2,1,0:T(8,128)(2,1)S(1)}, u32[]{:S(2)}, u32[]{:S(2)}) collective-permute-start(bf16[2,128,8,128]{3,2,1,0:T(8,128)(2,1)S(1)} %collective-permute-done.7.refs_5_), channel_id=1, source_target_pairs={{0,12},{1,13},{2,14},{3,15},{4,0},{5,1},{6,2},{7,3},{8,4},{9,5},{1... | collective-permute-start | bytes 1572872 | tf_op jit(solution)/shard_map/ppermute | solution.py:254
  83.1 3.9 %collective-permute-done.6.refs_4_ = bf16[2,128,8,128]{3,2,1,0:T(8,128)(2,1)S(1)} collective-permute-done((bf16[2,128,8,128]{3,2,1,0:T(8,128)(2,1)S(1)}, bf16[2,128,8,128]{3,2,1,0:T(8,128)(2,1)S(1)}, u32[]{:S(2)}, u32[]{:S(2)}) %collective-permute-start.6) | collective-permute-done | bytes 524320 | tf_op jit(solution)/shard_map/ppermute | solution.py:254
  87.1 1.9 %collective-permute-start.18 = (bf16[128,8,128]{2,1,0:T(8,128)(2,1)S(1)}, bf16[128,8,128]{2,1,0:T(8,128)(2,1)S(1)}, u32[]{:S(2)}, u32[]{:S(2)}) collective-permute-start(bf16[128,8,128]{2,1,0:T(8,128)(2,1)S(1)} %slice_bitcast_fusion), channel_id=1, source_target_pairs={{0,448},{1,449},{2,450},{3,451},{4,452},{5,453},{6,454},{7,455},{8... | collective-permute-start | bytes 786440 | tf_op jit(solution)/shard_map/ppermute | solution.py:254
  89.0 3.4 %collective-permute-start.17 = (bf16[2,128,8,128]{3,2,1,0:T(8,128)(2,1)S(1)}, bf16[2,128,8,128]{3,2,1,0:T(8,128)(2,1)S(1)}, u32[]{:S(2)}, u32[]{:S(2)}) collective-permute-start(bf16[2,128,8,128]{3,2,1,0:T(8,128)(2,1)S(1)} %collective-permute-done.15.refs_14_), channel_id=1, source_target_pairs={{0,64},{1,65},{2,66},{3,67},{4,68},{5,69},{6,70},{7,71},{8,72},{9,... | collective-permute-start | bytes 1572872 | tf_op jit(solution)/shard_map/ppermute | solution.py:254
  92.4 2.1 %collective-permute-done.18.refs_17_ = bf16[128,8,128]{2,1,0:T(8,128)(2,1)S(1)} collective-permute-done((bf16[128,8,128]{2,1,0:T(8,128)(2,1)S(1)}, bf16[128,8,128]{2,1,0:T(8,128)(2,1)S(1)}, u32[]{:S(2)}, u32[]{:S(2)}) %collective-permute-start.18) | collective-permute-done | bytes 262176 | tf_op jit(solution)/shard_map/ppermute | solution.py:254
  94.5 2.8 %collective-permute-start.19 = (bf16[128,8,128]{2,1,0:T(8,128)(2,1)S(1)}, bf16[128,8,128]{2,1,0:T(8,128)(2,1)S(1)}, u32[]{:S(2)}, u32[]{:S(2)}) collective-permute-start(bf16[128,8,128]{2,1,0:T(8,128)(2,1)S(1)} %collective-permute-done.18.refs_17_), channel_id=1, source_target_pairs={{0,448},{1,449},{2,450},{3,451},{4,452},{5,453},{6,454},{7,455},{8... | collective-permute-start | bytes 786440 | tf_op jit(solution)/shard_map/ppermute | solution.py:254
  97.3 1.5 %collective-permute-done.8.refs_6_ = bf16[2,128,8,128]{3,2,1,0:T(8,128)(2,1)S(1)} collective-permute-done((bf16[2,128,8,128]{3,2,1,0:T(8,128)(2,1)S(1)}, bf16[2,128,8,128]{3,2,1,0:T(8,128)(2,1)S(1)}, u32[]{:S(2)}, u32[]{:S(2)}) %collective-permute-start.8) | collective-permute-done | bytes 524320 | tf_op jit(solution)/shard_map/ppermute | solution.py:254
  98.9 5.7 %collective-permute-done.19.refs_18_ = bf16[128,8,128]{2,1,0:T(8,128)(2,1)S(1)} collective-permute-done((bf16[128,8,128]{2,1,0:T(8,128)(2,1)S(1)}, bf16[128,8,128]{2,1,0:T(8,128)(2,1)S(1)}, u32[]{:S(2)}, u32[]{:S(2)}) %collective-permute-start.19) | collective-permute-done | bytes 262176 | tf_op jit(solution)/shard_map/ppermute | solution.py:254
  104.5 7.6 %cross.1 = (bf16[64,128,128]{2,1,0:T(8,128)(2,1)S(1)}, f32[64,128,128]{2,1,0:T(8,128)S(1)}) custom-call(bf16[2,128,8,128]{3,2,1,0:T(8,128)(2,1)S(1)} %pad_maximum_fusion.2.refs_0_, bf16[2,128,8,128]{3,2,1,0:T(8,128)(2,1)S(1)} %pad_maximum_fusion.3.refs_1_, bf16[2,128,8,128]{3,2,1,0:T(8,128)(2,1)S(1)} %collective-permute-done.4.refs_2_, ...), custom_call_target="tpu_custom_call" | custom-call | tf_op jit(solution)/shard_map/cross/pallas_call | solution.py:211
  112.2 10.7 %collective-permute-start.20 = (bf16[64,128,128]{2,1,0:T(8,128)(2,1)S(1)}, bf16[64,128,128]{2,1,0:T(8,128)(2,1)S(1)}, u32[]{:S(2)}, u32[]{:S(2)}) collective-permute-start(bf16[64,128,128]{2,1,0:T(8,128)(2,1)S(1)} %get-tuple-element.12), channel_id=1, source_target_pairs={{0,16},{1,17},{2,18},{3,19},{4,20},{5,21},{6,22},{7,23},{8,24},{9,... | collective-permute-start | bytes 6291464 | tf_op jit(solution)/shard_map/ppermute | solution.py:254
  122.9 3.8 %collective-permute-done.20 = bf16[64,128,128]{2,1,0:T(8,128)(2,1)S(1)} collective-permute-done((bf16[64,128,128]{2,1,0:T(8,128)(2,1)S(1)}, bf16[64,128,128]{2,1,0:T(8,128)(2,1)S(1)}, u32[]{:S(2)}, u32[]{:S(2)}) %collective-permute-start.20) | collective-permute-done | bytes 2097184 | tf_op jit(solution)/shard_map/ppermute | solution.py:254
  126.6 2.0 %add_convert_fusion = bf16[64,128,128]{2,1,0:T(8,128)(2,1)} fusion(f32[64,128,128]{2,1,0:T(8,128)S(1)} %get-tuple-element.11, bf16[64,128,128]{2,1,0:T(8,128)(2,1)S(1)} %collective-permute-done.20), kind=kLoop, calls=%fused_computation | loop fusion | flops 3145728 | bytes 8388608 | tf_op jit(solution)/shard_map/convert_element_type | solution.py:283
  (20 shorter events, 2.7 us)
Async XLA Ops:
  3.0 3.6 %collective-permute-start = (bf16[512,128]{1,0:T(8,128)(2,1)S(1)}, bf16[512,128]{1,0:T(8,128)(2,1)S(1)}, u32[]{:S(2)}, u32[]{:S(2)}) collective-permute-start(bf16[512,128]{1,0:T(8,128)(2,1)S(1)} %get-tuple-element.10), channel_id=1, source_target_pairs={{0,16},{1,17},{2,18},{3,19},{4,20},{5,21},{6,22},{7,23},{8,24},{9,... | collective-permute-start | bytes 393224 | tf_op jit(solution)/shard_map/ppermute | solution.py:254
  6.7 15.9 %collective-permute-start.12 = (bf16[128,8,128]{2,1,0:T(8,128)(2,1)S(1)}, bf16[128,8,128]{2,1,0:T(8,128)(2,1)S(1)}, u32[]{:S(2)}, u32[]{:S(2)}) collective-permute-start(bf16[128,8,128]{2,1,0:T(8,128)(2,1)S(1)} %bitcast.11), channel_id=1, source_target_pairs={{0,448},{1,449},{2,450},{3,451},{4,452},{5,453},{6,454},{7,455},{8... | collective-permute-start | bytes 786440 | tf_op jit(solution)/shard_map/ppermute | solution.py:254
  11.8 10.8 %collective-permute-start.11 = (bf16[128,8,128]{2,1,0:T(8,128)(2,1)S(1)}, bf16[128,8,128]{2,1,0:T(8,128)(2,1)S(1)}, u32[]{:S(2)}, u32[]{:S(2)}) collective-permute-start(bf16[128,8,128]{2,1,0:T(8,128)(2,1)S(1)} %bitcast.12), channel_id=1, source_target_pairs={{0,64},{1,65},{2,66},{3,67},{4,68},{5,69},{6,70},{7,71},{8,72},{9,... | collective-permute-start | bytes 786440 | tf_op jit(solution)/shard_map/ppermute | solution.py:254
  13.7 21.2 %collective-permute-start.10 = (bf16[128,8,128]{2,1,0:T(8,128)(2,1)S(1)}, bf16[128,8,128]{2,1,0:T(8,128)(2,1)S(1)}, u32[]{:S(2)}, u32[]{:S(2)}) collective-permute-start(bf16[128,8,128]{2,1,0:T(8,128)(2,1)S(1)} %bitcast.13), channel_id=1, source_target_pairs={{0,32},{1,33},{2,34},{3,35},{4,36},{5,37},{6,38},{7,39},{8,40},{9,... | collective-permute-start | bytes 786440 | tf_op jit(solution)/shard_map/ppermute | solution.py:254
  35.0 69.6 %copy-start = (bf16[2,128,256]{2,1,0:T(8,128)(2,1)S(1)}, bf16[2,128,256]{2,1,0:T(8,128)(2,1)}, u32[]{:S(2)}) copy-start(bf16[2,128,256]{2,1,0:T(8,128)(2,1)} %constant.8.clone.refs_19_) | copy-start | bytes 393220
  35.0 30.5 %collective-permute-start.14 = (bf16[2,128,8,128]{3,2,1,0:T(8,128)(2,1)S(1)}, bf16[2,128,8,128]{3,2,1,0:T(8,128)(2,1)S(1)}, u32[]{:S(2)}, u32[]{:S(2)}) collective-permute-start(bf16[2,128,8,128]{3,2,1,0:T(8,128)(2,1)S(1)} %get-tuple-element.13), channel_id=1, source_target_pairs={{0,448},{1,449},{2,450},{3,451},{4,452},{5,453},{6,454},{7,455},{8... | collective-permute-start | bytes 1572872 | tf_op jit(solution)/shard_map/ppermute | solution.py:254
  39.6 10.5 %collective-permute-start.1 = (bf16[128,8,128]{2,1,0:T(8,128)(2,1)S(1)}, bf16[128,8,128]{2,1,0:T(8,128)(2,1)S(1)}, u32[]{:S(2)}, u32[]{:S(2)}) collective-permute-start(bf16[128,8,128]{2,1,0:T(8,128)(2,1)S(1)} %bitcast.14), channel_id=1, source_target_pairs={{0,1},{1,2},{2,3},{3,0},{4,5},{5,6},{6,7},{7,4},{8,9},{9,10},{10,1... | collective-permute-start | bytes 786440 | tf_op jit(solution)/shard_map/ppermute | solution.py:254
  41.5 16.1 %collective-permute-start.3 = (bf16[128,8,128]{2,1,0:T(8,128)(2,1)S(1)}, bf16[128,8,128]{2,1,0:T(8,128)(2,1)S(1)}, u32[]{:S(2)}, u32[]{:S(2)}) collective-permute-start(bf16[128,8,128]{2,1,0:T(8,128)(2,1)S(1)} %bitcast.15), channel_id=1, source_target_pairs={{0,2},{1,3},{2,0},{3,1},{4,6},{5,7},{6,4},{7,5},{8,10},{9,11},{10,... | collective-permute-start | bytes 786440 | tf_op jit(solution)/shard_map/ppermute | solution.py:254
  43.9 19.4 %collective-permute-start.2 = (bf16[128,8,128]{2,1,0:T(8,128)(2,1)S(1)}, bf16[128,8,128]{2,1,0:T(8,128)(2,1)S(1)}, u32[]{:S(2)}, u32[]{:S(2)}) collective-permute-start(bf16[128,8,128]{2,1,0:T(8,128)(2,1)S(1)} %bitcast.16), channel_id=1, source_target_pairs={{0,3},{1,0},{2,1},{3,2},{4,7},{5,4},{6,5},{7,6},{8,11},{9,8},{10,9... | collective-permute-start | bytes 786440 | tf_op jit(solution)/shard_map/ppermute | solution.py:254
  46.8 25.0 %collective-permute-start.13 = (bf16[2,128,8,128]{3,2,1,0:T(8,128)(2,1)S(1)}, bf16[2,128,8,128]{3,2,1,0:T(8,128)(2,1)S(1)}, u32[]{:S(2)}, u32[]{:S(2)}) collective-permute-start(bf16[2,128,8,128]{3,2,1,0:T(8,128)(2,1)S(1)} %get-tuple-element.14), channel_id=1, source_target_pairs={{0,64},{1,65},{2,66},{3,67},{4,68},{5,69},{6,70},{7,71},{8,72},{9,... | collective-permute-start | bytes 1572872 | tf_op jit(solution)/shard_map/ppermute | solution.py:254
  50.2 25.0 %collective-permute-start.4 = (bf16[2,128,8,128]{3,2,1,0:T(8,128)(2,1)S(1)}, bf16[2,128,8,128]{3,2,1,0:T(8,128)(2,1)S(1)}, u32[]{:S(2)}, u32[]{:S(2)}) collective-permute-start(bf16[2,128,8,128]{3,2,1,0:T(8,128)(2,1)S(1)} %pad_maximum_fusion.2.refs_0_), channel_id=1, source_target_pairs={{0,4},{1,5},{2,6},{3,7},{4,8},{5,9},{6,10},{7,11},{8,12},{9,13},{1... | collective-permute-start | bytes 1572872 | tf_op jit(solution)/shard_map/ppermute | solution.py:254
  63.3 13.8 %collective-permute-start.7 = (bf16[2,128,8,128]{3,2,1,0:T(8,128)(2,1)S(1)}, bf16[2,128,8,128]{3,2,1,0:T(8,128)(2,1)S(1)}, u32[]{:S(2)}, u32[]{:S(2)}) collective-permute-start(bf16[2,128,8,128]{3,2,1,0:T(8,128)(2,1)S(1)} %pad_maximum_fusion.3.refs_1_), channel_id=1, source_target_pairs={{0,12},{1,13},{2,14},{3,15},{4,0},{5,1},{6,2},{7,3},{8,4},{9,5},{1... | collective-permute-start | bytes 1572872 | tf_op jit(solution)/shard_map/ppermute | solution.py:254
  65.5 13.8 %collective-permute-start.16 = (bf16[2,128,8,128]{3,2,1,0:T(8,128)(2,1)S(1)}, bf16[2,128,8,128]{3,2,1,0:T(8,128)(2,1)S(1)}, u32[]{:S(2)}, u32[]{:S(2)}) collective-permute-start(bf16[2,128,8,128]{3,2,1,0:T(8,128)(2,1)S(1)} %collective-permute-done.14.refs_13_), channel_id=1, source_target_pairs={{0,448},{1,449},{2,450},{3,451},{4,452},{5,453},{6,454},{7,455},{8... | collective-permute-start | bytes 1572872 | tf_op jit(solution)/shard_map/ppermute | solution.py:254
  67.4 19.6 %collective-permute-start.6 = (bf16[2,128,8,128]{3,2,1,0:T(8,128)(2,1)S(1)}, bf16[2,128,8,128]{3,2,1,0:T(8,128)(2,1)S(1)}, u32[]{:S(2)}, u32[]{:S(2)}) collective-permute-start(bf16[2,128,8,128]{3,2,1,0:T(8,128)(2,1)S(1)} %pad_maximum_fusion.2.refs_0_), channel_id=1, source_target_pairs={{0,12},{1,13},{2,14},{3,15},{4,0},{5,1},{6,2},{7,3},{8,4},{9,5},{1... | collective-permute-start | bytes 1572872 | tf_op jit(solution)/shard_map/ppermute | solution.py:254
  71.9 17.1 %collective-permute-start.15 = (bf16[2,128,8,128]{3,2,1,0:T(8,128)(2,1)S(1)}, bf16[2,128,8,128]{3,2,1,0:T(8,128)(2,1)S(1)}, u32[]{:S(2)}, u32[]{:S(2)}) collective-permute-start(bf16[2,128,8,128]{3,2,1,0:T(8,128)(2,1)S(1)} %collective-permute-done.13.refs_12_), channel_id=1, source_target_pairs={{0,64},{1,65},{2,66},{3,67},{4,68},{5,69},{6,70},{7,71},{8,72},{9,... | collective-permute-start | bytes 1572872 | tf_op jit(solution)/shard_map/ppermute | solution.py:254
  75.2 22.1 %collective-permute-start.5 = (bf16[2,128,8,128]{3,2,1,0:T(8,128)(2,1)S(1)}, bf16[2,128,8,128]{3,2,1,0:T(8,128)(2,1)S(1)}, u32[]{:S(2)}, u32[]{:S(2)}) collective-permute-start(bf16[2,128,8,128]{3,2,1,0:T(8,128)(2,1)S(1)} %pad_maximum_fusion.3.refs_1_), channel_id=1, source_target_pairs={{0,4},{1,5},{2,6},{3,7},{4,8},{5,9},{6,10},{7,11},{8,12},{9,13},{1... | collective-permute-start | bytes 1572872 | tf_op jit(solution)/shard_map/ppermute | solution.py:254
  77.2 21.7 %collective-permute-start.8 = (bf16[2,128,8,128]{3,2,1,0:T(8,128)(2,1)S(1)}, bf16[2,128,8,128]{3,2,1,0:T(8,128)(2,1)S(1)}, u32[]{:S(2)}, u32[]{:S(2)}) collective-permute-start(bf16[2,128,8,128]{3,2,1,0:T(8,128)(2,1)S(1)} %collective-permute-done.4.refs_2_), channel_id=1, source_target_pairs={{0,4},{1,5},{2,6},{3,7},{4,8},{5,9},{6,10},{7,11},{8,12},{9,13},{1... | collective-permute-start | bytes 1572872 | tf_op jit(solution)/shard_map/ppermute | solution.py:254
  79.3 19.6 %collective-permute-start.9 = (bf16[2,128,8,128]{3,2,1,0:T(8,128)(2,1)S(1)}, bf16[2,128,8,128]{3,2,1,0:T(8,128)(2,1)S(1)}, u32[]{:S(2)}, u32[]{:S(2)}) collective-permute-start(bf16[2,128,8,128]{3,2,1,0:T(8,128)(2,1)S(1)} %collective-permute-done.7.refs_5_), channel_id=1, source_target_pairs={{0,12},{1,13},{2,14},{3,15},{4,0},{5,1},{6,2},{7,3},{8,4},{9,5},{1... | collective-permute-start | bytes 1572872 | tf_op jit(solution)/shard_map/ppermute | solution.py:254
  87.1 7.4 %collective-permute-start.18 = (bf16[128,8,128]{2,1,0:T(8,128)(2,1)S(1)}, bf16[128,8,128]{2,1,0:T(8,128)(2,1)S(1)}, u32[]{:S(2)}, u32[]{:S(2)}) collective-permute-start(bf16[128,8,128]{2,1,0:T(8,128)(2,1)S(1)} %slice_bitcast_fusion), channel_id=1, source_target_pairs={{0,448},{1,449},{2,450},{3,451},{4,452},{5,453},{6,454},{7,455},{8... | collective-permute-start | bytes 786440 | tf_op jit(solution)/shard_map/ppermute | solution.py:254
  89.0 15.5 %collective-permute-start.17 = (bf16[2,128,8,128]{3,2,1,0:T(8,128)(2,1)S(1)}, bf16[2,128,8,128]{3,2,1,0:T(8,128)(2,1)S(1)}, u32[]{:S(2)}, u32[]{:S(2)}) collective-permute-start(bf16[2,128,8,128]{3,2,1,0:T(8,128)(2,1)S(1)} %collective-permute-done.15.refs_14_), channel_id=1, source_target_pairs={{0,64},{1,65},{2,66},{3,67},{4,68},{5,69},{6,70},{7,71},{8,72},{9,... | collective-permute-start | bytes 1572872 | tf_op jit(solution)/shard_map/ppermute | solution.py:254
  94.5 10.1 %collective-permute-start.19 = (bf16[128,8,128]{2,1,0:T(8,128)(2,1)S(1)}, bf16[128,8,128]{2,1,0:T(8,128)(2,1)S(1)}, u32[]{:S(2)}, u32[]{:S(2)}) collective-permute-start(bf16[128,8,128]{2,1,0:T(8,128)(2,1)S(1)} %collective-permute-done.18.refs_17_), channel_id=1, source_target_pairs={{0,448},{1,449},{2,450},{3,451},{4,452},{5,453},{6,454},{7,455},{8... | collective-permute-start | bytes 786440 | tf_op jit(solution)/shard_map/ppermute | solution.py:254
  112.2 14.5 %collective-permute-start.20 = (bf16[64,128,128]{2,1,0:T(8,128)(2,1)S(1)}, bf16[64,128,128]{2,1,0:T(8,128)(2,1)S(1)}, u32[]{:S(2)}, u32[]{:S(2)}) collective-permute-start(bf16[64,128,128]{2,1,0:T(8,128)(2,1)S(1)} %get-tuple-element.12), channel_id=1, source_target_pairs={{0,16},{1,17},{2,18},{3,19},{4,20},{5,21},{6,22},{7,23},{8,24},{9,... | collective-permute-start | bytes 6291464 | tf_op jit(solution)/shard_map/ppermute | solution.py:254

commit v4 on v3

--- a/solution.py
+++ b/solution.py
@@ -176,30 +176,81 @@
         rows = pl.ds(slot * PITCH, 2 * HALF)
         s_ref[rows, :] = jnp.where(lane == slot, 0.0, s_ref[rows, :])
     table = inv_ref[core]
-    spots = [pl.ds(pl.multiple_of(place * 8, 8), 8) for place in where[16:]]
-
-    def lag_pair(step, which, out_ref):
+    spots = row_spots(where)
+
+    def send_step(step, carry):
         piece, half = step // 2, step % 2
-        start = pl.multiple_of((piece * 8 + which * 4 + half * 2) * PITCH, 8)
+        start = pl.multiple_of((piece * 8 + (1 - core) * 4 + half * 2) * PITCH, 8)
         w0 = s_ref[pl.ds(start, 2 * HALF), :].astype(jnp.bfloat16)
         w1 = s_ref[pl.ds(pl.multiple_of(start + PITCH, 8), 2 * HALF), :].astype(jnp.bfloat16)
-        lagged = jnp.dot(table, jnp.concatenate([w0, w1], axis=1), preferred_element_type=jnp.float32)
-        i = place_ref[piece] * 4 + half * 2
-        for n in range(2):
-            block = lagged[:, n * 128 : (n + 1) * 128].T
-            for slot in range(16):
-                out_ref[i + n, spots[slot], :] = block[slot * 8 : slot * 8 + 8].astype(out_ref.dtype)
-
-    def send_step(step, carry):
-        lag_pair(step, 1 - core, send_ref)
+        store_lags(table, w0, w1, place_ref[piece] * 4 + half * 2, spots, send_ref)
+        own = pl.multiple_of((piece * 8 + core * 4 + half * 2) * PITCH, 8)
+        at = place_ref[piece] * 4 + half * 2
+        own_ref[at] = s_ref[pl.ds(own, 2 * HALF), :].astype(jnp.bfloat16)
+        own_ref[at + 1] = s_ref[pl.ds(pl.multiple_of(own + PITCH, 8), 2 * HALF), :].astype(jnp.bfloat16)
         return carry
 
-    def own_step(step, carry):
-        lag_pair(step, core, own_ref)
+    lax.fori_loop(0, 32, send_step, 0, unroll=16)
+
+
+def row_spots(where):
+    return [pl.ds(pl.multiple_of(place * 8, 8), 8) for place in where[16:]]
+
+
+def store_lags(table, w0, w1, i, spots, out_ref):
+    lagged = jnp.dot(table, jnp.concatenate([w0, w1], axis=1), preferred_element_type=jnp.float32)
+    for n in range(2):
+        block = lagged[:, n * 128 : (n + 1) * 128].T
+        for slot in range(16):
+            out_ref[i + n, spots[slot], :] = block[slot * 8 : slot * 8 + 8].astype(out_ref.dtype)
+
+
+def lag_kernel(stacked_ref, inv_ref, out_ref):
+    row, _, where = placements()
+    table = inv_ref[row % N_C]
+    spots = row_spots(where)
+
+    def step(pair, carry):
+        i = 2 * pair
+        store_lags(table, stacked_ref[i], stacked_ref[i + 1], i, spots, out_ref)
         return carry
 
-    lax.fori_loop(0, 32, send_step, 0, unroll=16)
-    lax.fori_loop(0, 32, own_step, 0, unroll=16)
+    lax.fori_loop(0, 32, step, 0, unroll=16)
+
+
+def lag_own(stacked, inverse):
+    vmem = pl.BlockSpec(memory_space=pltpu.VMEM)
+    return pl.pallas_call(
+        lag_kernel,
+        out_shape=pltpu.VMEM((64, 128, LAGS), jnp.float32),
+        in_specs=[vmem, vmem],
+        out_specs=vmem,
+        compiler_params=pltpu.CompilerParams(vmem_limit_bytes=16 * 1024 * 1024),
+        cost_estimate=pl.CostEstimate(
+            flops=2 * 64 * 128 * LAGS * 2 * HALF, bytes_accessed=1 << 23, transcendentals=0
+        ),
+        name="lag_own",
+    )(in_vmem(stacked), inverse)
+
+
+def finish_kernel(own_ref, got_ref, out_ref):
+    step = out_ref.shape[0]
+    rows = pl.ds(pl.multiple_of(pl.program_id(0) * step, step), step)
+    out_ref[...] = (own_ref[rows] + got_ref[rows].astype(jnp.float32)).astype(jnp.bfloat16)
+
+
+def finish(own, got):
+    step = 8
+    vmem = pl.BlockSpec(memory_space=pltpu.VMEM)
+    return pl.pallas_call(
+        finish_kernel,
+        out_shape=jax.ShapeDtypeStruct((64, 128, LAGS), jnp.bfloat16),
+        grid=(64 // step,),
+        in_specs=[vmem, vmem],
+        out_specs=pl.BlockSpec((step, 128, LAGS), lambda n: (n, 0, 0)),
+        compiler_params=pltpu.CompilerParams(vmem_limit_bytes=16 * 1024 * 1024),
+        name="finish",
+    )(in_vmem(own), in_vmem(got))
 
 
 UNROLL = 16
@@ -212,7 +263,7 @@
         kernel,
         out_shape=(
             pltpu.VMEM((64, 128, LAGS), jnp.bfloat16),
-            pltpu.VMEM((64, 128, LAGS), jnp.float32),
+            pltpu.VMEM((64, 2 * HALF, 128), jnp.bfloat16),
         ),
         in_specs=[vmem] * (len(firsts) + len(seconds) + 1),
         out_specs=(vmem, vmem),
@@ -278,9 +329,10 @@
 
     firsts = (x1, x2, x1_up, x2_up, x1_down, x2_down, x1_far, x2_far)
     seconds = (piece, other, up1, down1, up2, down2, up3, down3, up4, down4, down5)
-    sent, own = cross(firsts, seconds, jnp.asarray(inverse))
+    table = jnp.asarray(inverse)
+    sent, stacked = cross(firsts, seconds, table)
     got = move(sent, SWAP_CORE)
-    return (own + got.astype(jnp.float32)).astype(jnp.bfloat16)
+    return finish(lag_own(stacked, table), got)
 
 
 def solution(mesh):

time: 129 us -> 129 us (level)
  Pallas kernels: 10.8 us -> 14.1 us
  other arithmetic: 2.19 us -> 0.18 us
  waiting for transfers between devices: 41.7 us -> 40 us
    pallas_call x0 -> x2, Pallas kernels: none -> 4.72 us  [the longest x1 3.07 us: finish(): pl.pallas_call(finish_kernel, out_shape=jax.ShapeDtypeStruct((64, 128, LA...]
    convert_element_type x1 -> x0, other arithmetic: 2.01 us -> none  [correlate(): return (own + got.astype(jnp.float32)).astype(jnp.bfloat16)]
    ppermute x21, waiting for transfers between devices: 41.7 us -> 40 us  [move(): return lax.ppermute(value, AXES, pairs)]
    pallas_call x1, Pallas kernels: 7.62 us -> 6.25 us  [cross(): pl.pallas_call(kernel, out_shape=(pltpu.VMEM((64, 128, LAGS), jnp.bfloat1...]
  transfers between devices with their start and end apart: 21 -> 21, of which waited for: 10 -> 10; matrix products, arithmetic and copies ran while one was open for 0% -> 0% of each run, Pallas kernels for 0% -> 1%
where the time goes in v4:
time: 129 us; the launch traced here: 128 us
  starting transfers between devices  73.7 us (57%)
  waiting for transfers between devices  40 us (31%)
  Pallas kernels  14.1 us (11%)
    ppermute x21, starting transfers between devices, move(): return lax.ppermute(value, AXES, pairs)  73.7 us
    ppermute x21, waiting for transfers between devices, move(): return lax.ppermute(value, AXES, pairs)  40 us
    pallas_call x1, Pallas kernels, cross(): pl.pallas_call(kernel, out_shape=(pltpu.VMEM((64, 128, LAGS), jnp.bfloat1...  6.25 us
    pallas_call x1, Pallas kernels, finish(): pl.pallas_call(finish_kernel, out_shape=jax.ShapeDtypeStruct((64, 128, LA...  3.07 us
    pallas_call x1, Pallas kernels, whiten(): pl.pallas_call(whiten_kernel, out_shape=(shape, shape), in_specs=[smem, v...  3.02 us
  transfers between devices with their start and end apart: 21, of which 10 were waited for; matrix products, arithmetic and copies ran while one was open for 0% of the time, Pallas kernels for 1%

profile of v4, /device:TPU:131, one launch (start us, length us, event | category | flops | bytes accessed | tf_op | source)
XLA Modules:
  0.0 128.4 jit_solution(14351110029751815913)
XLA Ops:
  0.0 3.0 %whiten.1 = (bf16[512,128]{1,0:T(8,128)(2,1)S(1)}, bf16[512,128]{1,0:T(8,128)(2,1)S(1)}) custom-call(s32[4]{0:T(128)} %flags_ref.1, bf16[256,512]{1,0:T(8,128)(2,1)} %bitcast.22, bf16[3,512,512]{2,1,0:T(8,128)(2,1)} %constant.6.clone.dft_ref, f32[256,256]{1,0:T(8,128)} %constant.7.clone.near_ref), custom_call_target="tpu_custom_call" | custom-call | tf_op jit(solution)/shard_map/whiten/pallas_call | solution.py:92
  3.0 2.6 %collective-permute-start = (bf16[512,128]{1,0:T(8,128)(2,1)S(1)}, bf16[512,128]{1,0:T(8,128)(2,1)S(1)}, u32[]{:S(2)}, u32[]{:S(2)}) collective-permute-start(bf16[512,128]{1,0:T(8,128)(2,1)S(1)} %get-tuple-element.10), channel_id=1, source_target_pairs={{0,16},{1,17},{2,18},{3,19},{4,20},{5,21},{6,22},{7,23},{8,24},{9,... | collective-permute-start | bytes 393224 | tf_op jit(solution)/shard_map/ppermute | solution.py:305
  6.7 5.1 %collective-permute-start.12 = (bf16[128,8,128]{2,1,0:T(8,128)(2,1)S(1)}, bf16[128,8,128]{2,1,0:T(8,128)(2,1)S(1)}, u32[]{:S(2)}, u32[]{:S(2)}) collective-permute-start(bf16[128,8,128]{2,1,0:T(8,128)(2,1)S(1)} %bitcast.11), channel_id=1, source_target_pairs={{0,448},{1,449},{2,450},{3,451},{4,452},{5,453},{6,454},{7,455},{8... | collective-permute-start | bytes 786440 | tf_op jit(solution)/shard_map/ppermute | solution.py:305
  11.8 1.9 %collective-permute-start.11 = (bf16[128,8,128]{2,1,0:T(8,128)(2,1)S(1)}, bf16[128,8,128]{2,1,0:T(8,128)(2,1)S(1)}, u32[]{:S(2)}, u32[]{:S(2)}) collective-permute-start(bf16[128,8,128]{2,1,0:T(8,128)(2,1)S(1)} %bitcast.12), channel_id=1, source_target_pairs={{0,64},{1,65},{2,66},{3,67},{4,68},{5,69},{6,70},{7,71},{8,72},{9,... | collective-permute-start | bytes 786440 | tf_op jit(solution)/shard_map/ppermute | solution.py:305
  13.7 8.8 %collective-permute-start.10 = (bf16[128,8,128]{2,1,0:T(8,128)(2,1)S(1)}, bf16[128,8,128]{2,1,0:T(8,128)(2,1)S(1)}, u32[]{:S(2)}, u32[]{:S(2)}) collective-permute-start(bf16[128,8,128]{2,1,0:T(8,128)(2,1)S(1)} %bitcast.13), channel_id=1, source_target_pairs={{0,32},{1,33},{2,34},{3,35},{4,36},{5,37},{6,38},{7,39},{8,40},{9,... | collective-permute-start | bytes 786440 | tf_op jit(solution)/shard_map/ppermute | solution.py:305
  22.6 12.3 %collective-permute-done.10.refs_9_ = bf16[128,8,128]{2,1,0:T(8,128)(2,1)S(1)} collective-permute-done((bf16[128,8,128]{2,1,0:T(8,128)(2,1)S(1)}, bf16[128,8,128]{2,1,0:T(8,128)(2,1)S(1)}, u32[]{:S(2)}, u32[]{:S(2)}) %collective-permute-start.10) | collective-permute-done | bytes 262176 | tf_op jit(solution)/shard_map/ppermute | solution.py:305
  35.0 4.6 %collective-permute-start.14 = (bf16[2,128,8,128]{3,2,1,0:T(8,128)(2,1)S(1)}, bf16[2,128,8,128]{3,2,1,0:T(8,128)(2,1)S(1)}, u32[]{:S(2)}, u32[]{:S(2)}) collective-permute-start(bf16[2,128,8,128]{3,2,1,0:T(8,128)(2,1)S(1)} %get-tuple-element.13), channel_id=1, source_target_pairs={{0,448},{1,449},{2,450},{3,451},{4,452},{5,453},{6,454},{7,455},{8... | collective-permute-start | bytes 1572872 | tf_op jit(solution)/shard_map/ppermute | solution.py:305
  39.6 1.9 %collective-permute-start.1 = (bf16[128,8,128]{2,1,0:T(8,128)(2,1)S(1)}, bf16[128,8,128]{2,1,0:T(8,128)(2,1)S(1)}, u32[]{:S(2)}, u32[]{:S(2)}) collective-permute-start(bf16[128,8,128]{2,1,0:T(8,128)(2,1)S(1)} %bitcast.14), channel_id=1, source_target_pairs={{0,1},{1,2},{2,3},{3,0},{4,5},{5,6},{6,7},{7,4},{8,9},{9,10},{10,1... | collective-permute-start | bytes 786440 | tf_op jit(solution)/shard_map/ppermute | solution.py:305
  41.5 2.4 %collective-permute-start.3 = (bf16[128,8,128]{2,1,0:T(8,128)(2,1)S(1)}, bf16[128,8,128]{2,1,0:T(8,128)(2,1)S(1)}, u32[]{:S(2)}, u32[]{:S(2)}) collective-permute-start(bf16[128,8,128]{2,1,0:T(8,128)(2,1)S(1)} %bitcast.15), channel_id=1, source_target_pairs={{0,2},{1,3},{2,0},{3,1},{4,6},{5,7},{6,4},{7,5},{8,10},{9,11},{10,... | collective-permute-start | bytes 786440 | tf_op jit(solution)/shard_map/ppermute | solution.py:305
  43.9 2.9 %collective-permute-start.2 = (bf16[128,8,128]{2,1,0:T(8,128)(2,1)S(1)}, bf16[128,8,128]{2,1,0:T(8,128)(2,1)S(1)}, u32[]{:S(2)}, u32[]{:S(2)}) collective-permute-start(bf16[128,8,128]{2,1,0:T(8,128)(2,1)S(1)} %bitcast.16), channel_id=1, source_target_pairs={{0,3},{1,0},{2,1},{3,2},{4,7},{5,4},{6,5},{7,6},{8,11},{9,8},{10,9... | collective-permute-start | bytes 786440 | tf_op jit(solution)/shard_map/ppermute | solution.py:305
  46.8 1.9 %collective-permute-start.13 = (bf16[2,128,8,128]{3,2,1,0:T(8,128)(2,1)S(1)}, bf16[2,128,8,128]{3,2,1,0:T(8,128)(2,1)S(1)}, u32[]{:S(2)}, u32[]{:S(2)}) collective-permute-start(bf16[2,128,8,128]{3,2,1,0:T(8,128)(2,1)S(1)} %get-tuple-element.14), channel_id=1, source_target_pairs={{0,64},{1,65},{2,66},{3,67},{4,68},{5,69},{6,70},{7,71},{8,72},{9,... | collective-permute-start | bytes 1572872 | tf_op jit(solution)/shard_map/ppermute | solution.py:305
  50.2 3.1 %collective-permute-start.4 = (bf16[2,128,8,128]{3,2,1,0:T(8,128)(2,1)S(1)}, bf16[2,128,8,128]{3,2,1,0:T(8,128)(2,1)S(1)}, u32[]{:S(2)}, u32[]{:S(2)}) collective-permute-start(bf16[2,128,8,128]{3,2,1,0:T(8,128)(2,1)S(1)} %pad_maximum_fusion.2.refs_0_), channel_id=1, source_target_pairs={{0,4},{1,5},{2,6},{3,7},{4,8},{5,9},{6,10},{7,11},{8,12},{9,13},{1... | collective-permute-start | bytes 1572872 | tf_op jit(solution)/shard_map/ppermute | solution.py:305
  53.3 4.4 %collective-permute-done.3 = bf16[128,8,128]{2,1,0:T(8,128)(2,1)S(1)} collective-permute-done((bf16[128,8,128]{2,1,0:T(8,128)(2,1)S(1)}, bf16[128,8,128]{2,1,0:T(8,128)(2,1)S(1)}, u32[]{:S(2)}, u32[]{:S(2)}) %collective-permute-start.3) | collective-permute-done | bytes 262176 | tf_op jit(solution)/shard_map/ppermute | solution.py:305
  57.7 5.6 %collective-permute-done.2 = bf16[128,8,128]{2,1,0:T(8,128)(2,1)S(1)} collective-permute-done((bf16[128,8,128]{2,1,0:T(8,128)(2,1)S(1)}, bf16[128,8,128]{2,1,0:T(8,128)(2,1)S(1)}, u32[]{:S(2)}, u32[]{:S(2)}) %collective-permute-start.2) | collective-permute-done | bytes 262176 | tf_op jit(solution)/shard_map/ppermute | solution.py:305
  63.3 2.2 %collective-permute-start.7 = (bf16[2,128,8,128]{3,2,1,0:T(8,128)(2,1)S(1)}, bf16[2,128,8,128]{3,2,1,0:T(8,128)(2,1)S(1)}, u32[]{:S(2)}, u32[]{:S(2)}) collective-permute-start(bf16[2,128,8,128]{3,2,1,0:T(8,128)(2,1)S(1)} %pad_maximum_fusion.3.refs_1_), channel_id=1, source_target_pairs={{0,12},{1,13},{2,14},{3,15},{4,0},{5,1},{6,2},{7,3},{8,4},{9,5},{1... | collective-permute-start | bytes 1572872 | tf_op jit(solution)/shard_map/ppermute | solution.py:305
  65.5 1.9 %collective-permute-start.16 = (bf16[2,128,8,128]{3,2,1,0:T(8,128)(2,1)S(1)}, bf16[2,128,8,128]{3,2,1,0:T(8,128)(2,1)S(1)}, u32[]{:S(2)}, u32[]{:S(2)}) collective-permute-start(bf16[2,128,8,128]{3,2,1,0:T(8,128)(2,1)S(1)} %collective-permute-done.14.refs_13_), channel_id=1, source_target_pairs={{0,448},{1,449},{2,450},{3,451},{4,452},{5,453},{6,454},{7,455},{8... | collective-permute-start | bytes 1572872 | tf_op jit(solution)/shard_map/ppermute | solution.py:305
  67.4 4.4 %collective-permute-start.6 = (bf16[2,128,8,128]{3,2,1,0:T(8,128)(2,1)S(1)}, bf16[2,128,8,128]{3,2,1,0:T(8,128)(2,1)S(1)}, u32[]{:S(2)}, u32[]{:S(2)}) collective-permute-start(bf16[2,128,8,128]{3,2,1,0:T(8,128)(2,1)S(1)} %pad_maximum_fusion.2.refs_0_), channel_id=1, source_target_pairs={{0,12},{1,13},{2,14},{3,15},{4,0},{5,1},{6,2},{7,3},{8,4},{9,5},{1... | collective-permute-start | bytes 1572872 | tf_op jit(solution)/shard_map/ppermute | solution.py:305
  71.9 3.4 %collective-permute-start.15 = (bf16[2,128,8,128]{3,2,1,0:T(8,128)(2,1)S(1)}, bf16[2,128,8,128]{3,2,1,0:T(8,128)(2,1)S(1)}, u32[]{:S(2)}, u32[]{:S(2)}) collective-permute-start(bf16[2,128,8,128]{3,2,1,0:T(8,128)(2,1)S(1)} %collective-permute-done.13.refs_12_), channel_id=1, source_target_pairs={{0,64},{1,65},{2,66},{3,67},{4,68},{5,69},{6,70},{7,71},{8,72},{9,... | collective-permute-start | bytes 1572872 | tf_op jit(solution)/shard_map/ppermute | solution.py:305
  75.2 1.9 %collective-permute-start.5 = (bf16[2,128,8,128]{3,2,1,0:T(8,128)(2,1)S(1)}, bf16[2,128,8,128]{3,2,1,0:T(8,128)(2,1)S(1)}, u32[]{:S(2)}, u32[]{:S(2)}) collective-permute-start(bf16[2,128,8,128]{3,2,1,0:T(8,128)(2,1)S(1)} %pad_maximum_fusion.3.refs_1_), channel_id=1, source_target_pairs={{0,4},{1,5},{2,6},{3,7},{4,8},{5,9},{6,10},{7,11},{8,12},{9,13},{1... | collective-permute-start | bytes 1572872 | tf_op jit(solution)/shard_map/ppermute | solution.py:305
  77.2 2.1 %collective-permute-start.8 = (bf16[2,128,8,128]{3,2,1,0:T(8,128)(2,1)S(1)}, bf16[2,128,8,128]{3,2,1,0:T(8,128)(2,1)S(1)}, u32[]{:S(2)}, u32[]{:S(2)}) collective-permute-start(bf16[2,128,8,128]{3,2,1,0:T(8,128)(2,1)S(1)} %collective-permute-done.4.refs_2_), channel_id=1, source_target_pairs={{0,4},{1,5},{2,6},{3,7},{4,8},{5,9},{6,10},{7,11},{8,12},{9,13},{1... | collective-permute-start | bytes 1572872 | tf_op jit(solution)/shard_map/ppermute | solution.py:305
  79.3 3.8 %collective-permute-start.9 = (bf16[2,128,8,128]{3,2,1,0:T(8,128)(2,1)S(1)}, bf16[2,128,8,128]{3,2,1,0:T(8,128)(2,1)S(1)}, u32[]{:S(2)}, u32[]{:S(2)}) collective-permute-start(bf16[2,128,8,128]{3,2,1,0:T(8,128)(2,1)S(1)} %collective-permute-done.7.refs_5_), channel_id=1, source_target_pairs={{0,12},{1,13},{2,14},{3,15},{4,0},{5,1},{6,2},{7,3},{8,4},{9,5},{1... | collective-permute-start | bytes 1572872 | tf_op jit(solution)/shard_map/ppermute | solution.py:305
  83.1 3.9 %collective-permute-done.6.refs_4_ = bf16[2,128,8,128]{3,2,1,0:T(8,128)(2,1)S(1)} collective-permute-done((bf16[2,128,8,128]{3,2,1,0:T(8,128)(2,1)S(1)}, bf16[2,128,8,128]{3,2,1,0:T(8,128)(2,1)S(1)}, u32[]{:S(2)}, u32[]{:S(2)}) %collective-permute-start.6) | collective-permute-done | bytes 524320 | tf_op jit(solution)/shard_map/ppermute | solution.py:305
  87.1 1.9 %collective-permute-start.18 = (bf16[128,8,128]{2,1,0:T(8,128)(2,1)S(1)}, bf16[128,8,128]{2,1,0:T(8,128)(2,1)S(1)}, u32[]{:S(2)}, u32[]{:S(2)}) collective-permute-start(bf16[128,8,128]{2,1,0:T(8,128)(2,1)S(1)} %slice_bitcast_fusion), channel_id=1, source_target_pairs={{0,448},{1,449},{2,450},{3,451},{4,452},{5,453},{6,454},{7,455},{8... | collective-permute-start | bytes 786440 | tf_op jit(solution)/shard_map/ppermute | solution.py:305
  89.0 3.4 %collective-permute-start.17 = (bf16[2,128,8,128]{3,2,1,0:T(8,128)(2,1)S(1)}, bf16[2,128,8,128]{3,2,1,0:T(8,128)(2,1)S(1)}, u32[]{:S(2)}, u32[]{:S(2)}) collective-permute-start(bf16[2,128,8,128]{3,2,1,0:T(8,128)(2,1)S(1)} %collective-permute-done.15.refs_14_), channel_id=1, source_target_pairs={{0,64},{1,65},{2,66},{3,67},{4,68},{5,69},{6,70},{7,71},{8,72},{9,... | collective-permute-start | bytes 1572872 | tf_op jit(solution)/shard_map/ppermute | solution.py:305
  92.4 2.1 %collective-permute-done.18.refs_17_ = bf16[128,8,128]{2,1,0:T(8,128)(2,1)S(1)} collective-permute-done((bf16[128,8,128]{2,1,0:T(8,128)(2,1)S(1)}, bf16[128,8,128]{2,1,0:T(8,128)(2,1)S(1)}, u32[]{:S(2)}, u32[]{:S(2)}) %collective-permute-start.18) | collective-permute-done | bytes 262176 | tf_op jit(solution)/shard_map/ppermute | solution.py:305
  94.5 2.8 %collective-permute-start.19 = (bf16[128,8,128]{2,1,0:T(8,128)(2,1)S(1)}, bf16[128,8,128]{2,1,0:T(8,128)(2,1)S(1)}, u32[]{:S(2)}, u32[]{:S(2)}) collective-permute-start(bf16[128,8,128]{2,1,0:T(8,128)(2,1)S(1)} %collective-permute-done.18.refs_17_), channel_id=1, source_target_pairs={{0,448},{1,449},{2,450},{3,451},{4,452},{5,453},{6,454},{7,455},{8... | collective-permute-start | bytes 786440 | tf_op jit(solution)/shard_map/ppermute | solution.py:305
  98.9 5.7 %collective-permute-done.19.refs_18_ = bf16[128,8,128]{2,1,0:T(8,128)(2,1)S(1)} collective-permute-done((bf16[128,8,128]{2,1,0:T(8,128)(2,1)S(1)}, bf16[128,8,128]{2,1,0:T(8,128)(2,1)S(1)}, u32[]{:S(2)}, u32[]{:S(2)}) %collective-permute-start.19) | collective-permute-done | bytes 262176 | tf_op jit(solution)/shard_map/ppermute | solution.py:305
  104.5 6.3 %cross.1 = (bf16[64,128,128]{2,1,0:T(8,128)(2,1)S(1)}, bf16[64,256,128]{2,1,0:T(8,128)(2,1)S(1)}) custom-call(bf16[2,128,8,128]{3,2,1,0:T(8,128)(2,1)S(1)} %pad_maximum_fusion.2.refs_0_, bf16[2,128,8,128]{3,2,1,0:T(8,128)(2,1)S(1)} %pad_maximum_fusion.3.refs_1_, bf16[2,128,8,128]{3,2,1,0:T(8,128)(2,1)S(1)} %collective-permute-done.4.refs_2_, ...), custom_call_target="tpu_custom_call" | custom-call | tf_op jit(solution)/shard_map/cross/pallas_call | solution.py:262
  110.8 10.7 %collective-permute-start.20 = (bf16[64,128,128]{2,1,0:T(8,128)(2,1)S(1)}, bf16[64,128,128]{2,1,0:T(8,128)(2,1)S(1)}, u32[]{:S(2)}, u32[]{:S(2)}) collective-permute-start(bf16[64,128,128]{2,1,0:T(8,128)(2,1)S(1)} %get-tuple-element.12), channel_id=1, source_target_pairs={{0,16},{1,17},{2,18},{3,19},{4,20},{5,21},{6,22},{7,23},{8,24},{9,... | collective-permute-start | bytes 6291464 | tf_op jit(solution)/shard_map/ppermute | solution.py:305
  121.5 1.6 %lag_own.1.own_ref = f32[64,128,128]{2,1,0:T(8,128)S(1)} custom-call(bf16[64,256,128]{2,1,0:T(8,128)(2,1)S(1)} %get-tuple-element.11.stacked_ref, bf16[2,128,256]{2,1,0:T(8,128)(2,1)S(1)} %copy-done), custom_call_target="tpu_custom_call" | custom-call | flops 536870912 | bytes 8388608 | tf_op jit(solution)/shard_map/lag_own/pallas_call | solution.py:223
  123.2 2.1 %collective-permute-done.20.got_ref = bf16[64,128,128]{2,1,0:T(8,128)(2,1)S(1)} collective-permute-done((bf16[64,128,128]{2,1,0:T(8,128)(2,1)S(1)}, bf16[64,128,128]{2,1,0:T(8,128)(2,1)S(1)}, u32[]{:S(2)}, u32[]{:S(2)}) %collective-permute-start.20) | collective-permute-done | bytes 2097184 | tf_op jit(solution)/shard_map/ppermute | solution.py:305
  125.3 3.1 %finish.1 = bf16[64,128,128]{2,1,0:T(8,128)(2,1)} custom-call(f32[64,128,128]{2,1,0:T(8,128)S(1)} %lag_own.1.own_ref, bf16[64,128,128]{2,1,0:T(8,128)(2,1)S(1)} %collective-permute-done.20.got_ref), custom_call_target="tpu_custom_call" | custom-call | tf_op jit(solution)/shard_map/finish/pallas_call | solution.py:245
  (21 shorter events, 4.2 us)
Async XLA Ops:
  3.0 3.6 %collective-permute-start = (bf16[512,128]{1,0:T(8,128)(2,1)S(1)}, bf16[512,128]{1,0:T(8,128)(2,1)S(1)}, u32[]{:S(2)}, u32[]{:S(2)}) collective-permute-start(bf16[512,128]{1,0:T(8,128)(2,1)S(1)} %get-tuple-element.10), channel_id=1, source_target_pairs={{0,16},{1,17},{2,18},{3,19},{4,20},{5,21},{6,22},{7,23},{8,24},{9,... | collective-permute-start | bytes 393224 | tf_op jit(solution)/shard_map/ppermute | solution.py:305
  6.7 15.9 %collective-permute-start.12 = (bf16[128,8,128]{2,1,0:T(8,128)(2,1)S(1)}, bf16[128,8,128]{2,1,0:T(8,128)(2,1)S(1)}, u32[]{:S(2)}, u32[]{:S(2)}) collective-permute-start(bf16[128,8,128]{2,1,0:T(8,128)(2,1)S(1)} %bitcast.11), channel_id=1, source_target_pairs={{0,448},{1,449},{2,450},{3,451},{4,452},{5,453},{6,454},{7,455},{8... | collective-permute-start | bytes 786440 | tf_op jit(solution)/shard_map/ppermute | solution.py:305
  11.8 10.8 %collective-permute-start.11 = (bf16[128,8,128]{2,1,0:T(8,128)(2,1)S(1)}, bf16[128,8,128]{2,1,0:T(8,128)(2,1)S(1)}, u32[]{:S(2)}, u32[]{:S(2)}) collective-permute-start(bf16[128,8,128]{2,1,0:T(8,128)(2,1)S(1)} %bitcast.12), channel_id=1, source_target_pairs={{0,64},{1,65},{2,66},{3,67},{4,68},{5,69},{6,70},{7,71},{8,72},{9,... | collective-permute-start | bytes 786440 | tf_op jit(solution)/shard_map/ppermute | solution.py:305
  13.7 21.2 %collective-permute-start.10 = (bf16[128,8,128]{2,1,0:T(8,128)(2,1)S(1)}, bf16[128,8,128]{2,1,0:T(8,128)(2,1)S(1)}, u32[]{:S(2)}, u32[]{:S(2)}) collective-permute-start(bf16[128,8,128]{2,1,0:T(8,128)(2,1)S(1)} %bitcast.13), channel_id=1, source_target_pairs={{0,32},{1,33},{2,34},{3,35},{4,36},{5,37},{6,38},{7,39},{8,40},{9,... | collective-permute-start | bytes 786440 | tf_op jit(solution)/shard_map/ppermute | solution.py:305
  35.0 69.6 %copy-start = (bf16[2,128,256]{2,1,0:T(8,128)(2,1)S(1)}, bf16[2,128,256]{2,1,0:T(8,128)(2,1)}, u32[]{:S(2)}) copy-start(bf16[2,128,256]{2,1,0:T(8,128)(2,1)} %constant.8.clone.refs_19_.inv_ref) | copy-start | bytes 393220
  35.0 30.5 %collective-permute-start.14 = (bf16[2,128,8,128]{3,2,1,0:T(8,128)(2,1)S(1)}, bf16[2,128,8,128]{3,2,1,0:T(8,128)(2,1)S(1)}, u32[]{:S(2)}, u32[]{:S(2)}) collective-permute-start(bf16[2,128,8,128]{3,2,1,0:T(8,128)(2,1)S(1)} %get-tuple-element.13), channel_id=1, source_target_pairs={{0,448},{1,449},{2,450},{3,451},{4,452},{5,453},{6,454},{7,455},{8... | collective-permute-start | bytes 1572872 | tf_op jit(solution)/shard_map/ppermute | solution.py:305
  39.6 10.5 %collective-permute-start.1 = (bf16[128,8,128]{2,1,0:T(8,128)(2,1)S(1)}, bf16[128,8,128]{2,1,0:T(8,128)(2,1)S(1)}, u32[]{:S(2)}, u32[]{:S(2)}) collective-permute-start(bf16[128,8,128]{2,1,0:T(8,128)(2,1)S(1)} %bitcast.14), channel_id=1, source_target_pairs={{0,1},{1,2},{2,3},{3,0},{4,5},{5,6},{6,7},{7,4},{8,9},{9,10},{10,1... | collective-permute-start | bytes 786440 | tf_op jit(solution)/shard_map/ppermute | solution.py:305
  41.5 16.1 %collective-permute-start.3 = (bf16[128,8,128]{2,1,0:T(8,128)(2,1)S(1)}, bf16[128,8,128]{2,1,0:T(8,128)(2,1)S(1)}, u32[]{:S(2)}, u32[]{:S(2)}) collective-permute-start(bf16[128,8,128]{2,1,0:T(8,128)(2,1)S(1)} %bitcast.15), channel_id=1, source_target_pairs={{0,2},{1,3},{2,0},{3,1},{4,6},{5,7},{6,4},{7,5},{8,10},{9,11},{10,... | collective-permute-start | bytes 786440 | tf_op jit(solution)/shard_map/ppermute | solution.py:305
  43.9 19.4 %collective-permute-start.2 = (bf16[128,8,128]{2,1,0:T(8,128)(2,1)S(1)}, bf16[128,8,128]{2,1,0:T(8,128)(2,1)S(1)}, u32[]{:S(2)}, u32[]{:S(2)}) collective-permute-start(bf16[128,8,128]{2,1,0:T(8,128)(2,1)S(1)} %bitcast.16), channel_id=1, source_target_pairs={{0,3},{1,0},{2,1},{3,2},{4,7},{5,4},{6,5},{7,6},{8,11},{9,8},{10,9... | collective-permute-start | bytes 786440 | tf_op jit(solution)/shard_map/ppermute | solution.py:305
  46.8 25.0 %collective-permute-start.13 = (bf16[2,128,8,128]{3,2,1,0:T(8,128)(2,1)S(1)}, bf16[2,128,8,128]{3,2,1,0:T(8,128)(2,1)S(1)}, u32[]{:S(2)}, u32[]{:S(2)}) collective-permute-start(bf16[2,128,8,128]{3,2,1,0:T(8,128)(2,1)S(1)} %get-tuple-element.14), channel_id=1, source_target_pairs={{0,64},{1,65},{2,66},{3,67},{4,68},{5,69},{6,70},{7,71},{8,72},{9,... | collective-permute-start | bytes 1572872 | tf_op jit(solution)/shard_map/ppermute | solution.py:305
  50.2 25.0 %collective-permute-start.4 = (bf16[2,128,8,128]{3,2,1,0:T(8,128)(2,1)S(1)}, bf16[2,128,8,128]{3,2,1,0:T(8,128)(2,1)S(1)}, u32[]{:S(2)}, u32[]{:S(2)}) collective-permute-start(bf16[2,128,8,128]{3,2,1,0:T(8,128)(2,1)S(1)} %pad_maximum_fusion.2.refs_0_), channel_id=1, source_target_pairs={{0,4},{1,5},{2,6},{3,7},{4,8},{5,9},{6,10},{7,11},{8,12},{9,13},{1... | collective-permute-start | bytes 1572872 | tf_op jit(solution)/shard_map/ppermute | solution.py:305
  63.3 13.8 %collective-permute-start.7 = (bf16[2,128,8,128]{3,2,1,0:T(8,128)(2,1)S(1)}, bf16[2,128,8,128]{3,2,1,0:T(8,128)(2,1)S(1)}, u32[]{:S(2)}, u32[]{:S(2)}) collective-permute-start(bf16[2,128,8,128]{3,2,1,0:T(8,128)(2,1)S(1)} %pad_maximum_fusion.3.refs_1_), channel_id=1, source_target_pairs={{0,12},{1,13},{2,14},{3,15},{4,0},{5,1},{6,2},{7,3},{8,4},{9,5},{1... | collective-permute-start | bytes 1572872 | tf_op jit(solution)/shard_map/ppermute | solution.py:305
  65.5 13.8 %collective-permute-start.16 = (bf16[2,128,8,128]{3,2,1,0:T(8,128)(2,1)S(1)}, bf16[2,128,8,128]{3,2,1,0:T(8,128)(2,1)S(1)}, u32[]{:S(2)}, u32[]{:S(2)}) collective-permute-start(bf16[2,128,8,128]{3,2,1,0:T(8,128)(2,1)S(1)} %collective-permute-done.14.refs_13_), channel_id=1, source_target_pairs={{0,448},{1,449},{2,450},{3,451},{4,452},{5,453},{6,454},{7,455},{8... | collective-permute-start | bytes 1572872 | tf_op jit(solution)/shard_map/ppermute | solution.py:305
  67.4 19.6 %collective-permute-start.6 = (bf16[2,128,8,128]{3,2,1,0:T(8,128)(2,1)S(1)}, bf16[2,128,8,128]{3,2,1,0:T(8,128)(2,1)S(1)}, u32[]{:S(2)}, u32[]{:S(2)}) collective-permute-start(bf16[2,128,8,128]{3,2,1,0:T(8,128)(2,1)S(1)} %pad_maximum_fusion.2.refs_0_), channel_id=1, source_target_pairs={{0,12},{1,13},{2,14},{3,15},{4,0},{5,1},{6,2},{7,3},{8,4},{9,5},{1... | collective-permute-start | bytes 1572872 | tf_op jit(solution)/shard_map/ppermute | solution.py:305
  71.9 17.1 %collective-permute-start.15 = (bf16[2,128,8,128]{3,2,1,0:T(8,128)(2,1)S(1)}, bf16[2,128,8,128]{3,2,1,0:T(8,128)(2,1)S(1)}, u32[]{:S(2)}, u32[]{:S(2)}) collective-permute-start(bf16[2,128,8,128]{3,2,1,0:T(8,128)(2,1)S(1)} %collective-permute-done.13.refs_12_), channel_id=1, source_target_pairs={{0,64},{1,65},{2,66},{3,67},{4,68},{5,69},{6,70},{7,71},{8,72},{9,... | collective-permute-start | bytes 1572872 | tf_op jit(solution)/shard_map/ppermute | solution.py:305
  75.2 22.1 %collective-permute-start.5 = (bf16[2,128,8,128]{3,2,1,0:T(8,128)(2,1)S(1)}, bf16[2,128,8,128]{3,2,1,0:T(8,128)(2,1)S(1)}, u32[]{:S(2)}, u32[]{:S(2)}) collective-permute-start(bf16[2,128,8,128]{3,2,1,0:T(8,128)(2,1)S(1)} %pad_maximum_fusion.3.refs_1_), channel_id=1, source_target_pairs={{0,4},{1,5},{2,6},{3,7},{4,8},{5,9},{6,10},{7,11},{8,12},{9,13},{1... | collective-permute-start | bytes 1572872 | tf_op jit(solution)/shard_map/ppermute | solution.py:305
  77.2 21.7 %collective-permute-start.8 = (bf16[2,128,8,128]{3,2,1,0:T(8,128)(2,1)S(1)}, bf16[2,128,8,128]{3,2,1,0:T(8,128)(2,1)S(1)}, u32[]{:S(2)}, u32[]{:S(2)}) collective-permute-start(bf16[2,128,8,128]{3,2,1,0:T(8,128)(2,1)S(1)} %collective-permute-done.4.refs_2_), channel_id=1, source_target_pairs={{0,4},{1,5},{2,6},{3,7},{4,8},{5,9},{6,10},{7,11},{8,12},{9,13},{1... | collective-permute-start | bytes 1572872 | tf_op jit(solution)/shard_map/ppermute | solution.py:305
  79.3 19.6 %collective-permute-start.9 = (bf16[2,128,8,128]{3,2,1,0:T(8,128)(2,1)S(1)}, bf16[2,128,8,128]{3,2,1,0:T(8,128)(2,1)S(1)}, u32[]{:S(2)}, u32[]{:S(2)}) collective-permute-start(bf16[2,128,8,128]{3,2,1,0:T(8,128)(2,1)S(1)} %collective-permute-done.7.refs_5_), channel_id=1, source_target_pairs={{0,12},{1,13},{2,14},{3,15},{4,0},{5,1},{6,2},{7,3},{8,4},{9,5},{1... | collective-permute-start | bytes 1572872 | tf_op jit(solution)/shard_map/ppermute | solution.py:305
  87.1 7.4 %collective-permute-start.18 = (bf16[128,8,128]{2,1,0:T(8,128)(2,1)S(1)}, bf16[128,8,128]{2,1,0:T(8,128)(2,1)S(1)}, u32[]{:S(2)}, u32[]{:S(2)}) collective-permute-start(bf16[128,8,128]{2,1,0:T(8,128)(2,1)S(1)} %slice_bitcast_fusion), channel_id=1, source_target_pairs={{0,448},{1,449},{2,450},{3,451},{4,452},{5,453},{6,454},{7,455},{8... | collective-permute-start | bytes 786440 | tf_op jit(solution)/shard_map/ppermute | solution.py:305
  89.0 15.5 %collective-permute-start.17 = (bf16[2,128,8,128]{3,2,1,0:T(8,128)(2,1)S(1)}, bf16[2,128,8,128]{3,2,1,0:T(8,128)(2,1)S(1)}, u32[]{:S(2)}, u32[]{:S(2)}) collective-permute-start(bf16[2,128,8,128]{3,2,1,0:T(8,128)(2,1)S(1)} %collective-permute-done.15.refs_14_), channel_id=1, source_target_pairs={{0,64},{1,65},{2,66},{3,67},{4,68},{5,69},{6,70},{7,71},{8,72},{9,... | collective-permute-start | bytes 1572872 | tf_op jit(solution)/shard_map/ppermute | solution.py:305
  94.5 10.1 %collective-permute-start.19 = (bf16[128,8,128]{2,1,0:T(8,128)(2,1)S(1)}, bf16[128,8,128]{2,1,0:T(8,128)(2,1)S(1)}, u32[]{:S(2)}, u32[]{:S(2)}) collective-permute-start(bf16[128,8,128]{2,1,0:T(8,128)(2,1)S(1)} %collective-permute-done.18.refs_17_), channel_id=1, source_target_pairs={{0,448},{1,449},{2,450},{3,451},{4,452},{5,453},{6,454},{7,455},{8... | collective-permute-start | bytes 786440 | tf_op jit(solution)/shard_map/ppermute | solution.py:305
  110.8 14.5 %collective-permute-start.20 = (bf16[64,128,128]{2,1,0:T(8,128)(2,1)S(1)}, bf16[64,128,128]{2,1,0:T(8,128)(2,1)S(1)}, u32[]{:S(2)}, u32[]{:S(2)}) collective-permute-start(bf16[64,128,128]{2,1,0:T(8,128)(2,1)S(1)} %get-tuple-element.12), channel_id=1, source_target_pairs={{0,16},{1,17},{2,18},{3,19},{4,20},{5,21},{6,22},{7,23},{8,24},{9,... | collective-permute-start | bytes 6291464 | tf_op jit(solution)/shard_map/ppermute | solution.py:305

commit v5 on v4

--- a/solution.py
+++ b/solution.py
@@ -35,7 +35,7 @@
     forward = np.concatenate([np.cos(angle), -np.sin(angle)], axis=0)
     taper = 0.5 - 0.5 * np.cos(2.0 * math.pi * samples / SAMP)
     dft = bf16_parts(forward * taper[None, :], 3)
-    near = (np.abs(bins[:, None] - bins[None, :]) <= 4).astype(np.float32)
+    near = (np.abs(bins[:, None] - bins[None, :]) <= 4).astype(jnp.bfloat16)
     lags = np.arange(LAGS) - LAGS // 2
     langle = 2.0 * math.pi * (bins[:, None] * lags[None, :] % SAMP) / SAMP
     shift = 1.0 / (math.sqrt(NW) * math.sqrt(F))
@@ -62,9 +62,18 @@
     power = re * re + im * im
     bins = lax.broadcasted_iota(jnp.int32, (F, 1), 0)
     counts = jnp.minimum(bins + 4, F - 1) - jnp.maximum(bins - 4, 0) + 1
-    smooth = jnp.dot(
-        near_ref[...], power, precision=lax.Precision.HIGHEST, preferred_element_type=jnp.float32
-    ) / counts.astype(jnp.float32)
+    high = power.astype(jnp.bfloat16)
+    rest = power - high.astype(jnp.float32)
+    middle = rest.astype(jnp.bfloat16)
+    tail = (rest - middle.astype(jnp.float32)).astype(jnp.bfloat16)
+    sums = jnp.dot(
+        near_ref[...],
+        jnp.concatenate([high, middle, tail], axis=1),
+        preferred_element_type=jnp.float32,
+    )
+    width = power.shape[1]
+    total = sums[:, 2 * width :] + sums[:, width : 2 * width] + sums[:, :width]
+    smooth = total / counts.astype(jnp.float32)
     level = jnp.mean(power, axis=0, keepdims=True)
     lane = lax.broadcasted_iota(jnp.int32, (1, 4 * NW), 1) // NW
     alive = jnp.zeros((1, 4 * NW), jnp.float32)
@@ -293,6 +302,7 @@
 STEP_L = [permutation(lambda y, h, c, x, l, d=d: (y, h, c, x, l + d)) for d in range(4)]
 Y_UP = permutation(lambda y, h, c, x, l: (y + 1, h, c, x, l))
 Y_DOWN = permutation(lambda y, h, c, x, l: (y - 1, h, c, x, l))
+Y_DOWN2 = permutation(lambda y, h, c, x, l: (y - 2, h, c, x, l))
 X_UP = permutation(lambda y, h, c, x, l: (y, h, c, x + 1, l))
 X_DOWN = permutation(lambda y, h, c, x, l: (y, h, c, x - 1, l))
 
@@ -323,9 +333,10 @@
     x2_up, x2_down = move(x2, X_UP), move(x2, X_DOWN)
     x1_far = move(x1_up, X_UP)
     up4 = move(up3, Y_UP)
-    down4 = move(down3[1], Y_DOWN)
+    far = down3[1]
+    down4 = move(far, Y_DOWN)
     x2_far = move(x2_down, X_DOWN)
-    down5 = move(down4, Y_DOWN)
+    down5 = move(far, Y_DOWN2)
 
     firsts = (x1, x2, x1_up, x2_up, x1_down, x2_down, x1_far, x2_far)
     seconds = (piece, other, up1, down1, up2, down2, up3, down3, up4, down4, down5)

time: 129 us -> 128 us (level)
  the two profiles are of different devices: /device:TPU:131 before, /device:TPU:71 now
where the time goes in v5:
time: 128 us; the launch traced here: 127 us
  starting transfers between devices  71.1 us (56%)
  waiting for transfers between devices  41.5 us (32%)
  Pallas kernels  13.8 us (11%)
    ppermute x21, starting transfers between devices, move(): return lax.ppermute(value, AXES, pairs)  71.1 us
    ppermute x21, waiting for transfers between devices, move(): return lax.ppermute(value, AXES, pairs)  41.5 us
    pallas_call x1, Pallas kernels, cross(): pl.pallas_call(kernel, out_shape=(pltpu.VMEM((64, 128, LAGS), jnp.bfloat1...  6.26 us
    pallas_call x1, Pallas kernels, finish(): pl.pallas_call(finish_kernel, out_shape=jax.ShapeDtypeStruct((64, 128, LA...  3.07 us
    pallas_call x1, Pallas kernels, whiten(): pl.pallas_call(whiten_kernel, out_shape=(shape, shape), in_specs=[smem, v...  2.69 us
  transfers between devices with their start and end apart: 21, of which 10 were waited for; matrix products, arithmetic and copies ran while one was open for 0% of the time, Pallas kernels for 1%

profile of v5, /device:TPU:71, one launch (start us, length us, event | category | flops | bytes accessed | tf_op | source)
XLA Modules:
  0.0 127.0 jit_solution(4472921336504804957)
XLA Ops:
  0.0 2.7 %whiten.1 = (bf16[512,128]{1,0:T(8,128)(2,1)S(1)}, bf16[512,128]{1,0:T(8,128)(2,1)S(1)}) custom-call(s32[4]{0:T(128)} %flags_ref.1, bf16[256,512]{1,0:T(8,128)(2,1)} %bitcast.22, bf16[3,512,512]{2,1,0:T(8,128)(2,1)} %constant.6.clone.dft_ref, bf16[256,256]{1,0:T(8,128)(2,1)} %constant.7.clone.near_ref), custom_call_target="tpu_custom_call" | custom-call | tf_op jit(solution)/shard_map/whiten/pallas_call | solution.py:101
  2.7 2.6 %collective-permute-start = (bf16[512,128]{1,0:T(8,128)(2,1)S(1)}, bf16[512,128]{1,0:T(8,128)(2,1)S(1)}, u32[]{:S(2)}, u32[]{:S(2)}) collective-permute-start(bf16[512,128]{1,0:T(8,128)(2,1)S(1)} %get-tuple-element.10), channel_id=1, source_target_pairs={{0,16},{1,17},{2,18},{3,19},{4,20},{5,21},{6,22},{7,23},{8,24},{9,... | collective-permute-start | bytes 393224 | tf_op jit(solution)/shard_map/ppermute | solution.py:315
  6.4 5.1 %collective-permute-start.12 = (bf16[128,8,128]{2,1,0:T(8,128)(2,1)S(1)}, bf16[128,8,128]{2,1,0:T(8,128)(2,1)S(1)}, u32[]{:S(2)}, u32[]{:S(2)}) collective-permute-start(bf16[128,8,128]{2,1,0:T(8,128)(2,1)S(1)} %bitcast.11), channel_id=1, source_target_pairs={{0,448},{1,449},{2,450},{3,451},{4,452},{5,453},{6,454},{7,455},{8... | collective-permute-start | bytes 786440 | tf_op jit(solution)/shard_map/ppermute | solution.py:315
  11.5 1.9 %collective-permute-start.11 = (bf16[128,8,128]{2,1,0:T(8,128)(2,1)S(1)}, bf16[128,8,128]{2,1,0:T(8,128)(2,1)S(1)}, u32[]{:S(2)}, u32[]{:S(2)}) collective-permute-start(bf16[128,8,128]{2,1,0:T(8,128)(2,1)S(1)} %bitcast.12), channel_id=1, source_target_pairs={{0,64},{1,65},{2,66},{3,67},{4,68},{5,69},{6,70},{7,71},{8,72},{9,... | collective-permute-start | bytes 786440 | tf_op jit(solution)/shard_map/ppermute | solution.py:315
  13.4 9.7 %collective-permute-start.10 = (bf16[128,8,128]{2,1,0:T(8,128)(2,1)S(1)}, bf16[128,8,128]{2,1,0:T(8,128)(2,1)S(1)}, u32[]{:S(2)}, u32[]{:S(2)}) collective-permute-start(bf16[128,8,128]{2,1,0:T(8,128)(2,1)S(1)} %bitcast.13), channel_id=1, source_target_pairs={{0,32},{1,33},{2,34},{3,35},{4,36},{5,37},{6,38},{7,39},{8,40},{9,... | collective-permute-start | bytes 786440 | tf_op jit(solution)/shard_map/ppermute | solution.py:315
  23.1 3.1 %collective-permute-start.1 = (bf16[128,8,128]{2,1,0:T(8,128)(2,1)S(1)}, bf16[128,8,128]{2,1,0:T(8,128)(2,1)S(1)}, u32[]{:S(2)}, u32[]{:S(2)}) collective-permute-start(bf16[128,8,128]{2,1,0:T(8,128)(2,1)S(1)} %bitcast.14), channel_id=1, source_target_pairs={{0,1},{1,2},{2,3},{3,0},{4,5},{5,6},{6,7},{7,4},{8,9},{9,10},{10,1... | collective-permute-start | bytes 786440 | tf_op jit(solution)/shard_map/ppermute | solution.py:315
  26.3 9.5 %collective-permute-done.10.refs_9_ = bf16[128,8,128]{2,1,0:T(8,128)(2,1)S(1)} collective-permute-done((bf16[128,8,128]{2,1,0:T(8,128)(2,1)S(1)}, bf16[128,8,128]{2,1,0:T(8,128)(2,1)S(1)}, u32[]{:S(2)}, u32[]{:S(2)}) %collective-permute-start.10) | collective-permute-done | bytes 262176 | tf_op jit(solution)/shard_map/ppermute | solution.py:315
  35.9 4.3 %collective-permute-start.14 = (bf16[2,128,8,128]{3,2,1,0:T(8,128)(2,1)S(1)}, bf16[2,128,8,128]{3,2,1,0:T(8,128)(2,1)S(1)}, u32[]{:S(2)}, u32[]{:S(2)}) collective-permute-start(bf16[2,128,8,128]{3,2,1,0:T(8,128)(2,1)S(1)} %get-tuple-element.13), channel_id=1, source_target_pairs={{0,448},{1,449},{2,450},{3,451},{4,452},{5,453},{6,454},{7,455},{8... | collective-permute-start | bytes 1572872 | tf_op jit(solution)/shard_map/ppermute | solution.py:315
  40.2 1.9 %collective-permute-start.13 = (bf16[2,128,8,128]{3,2,1,0:T(8,128)(2,1)S(1)}, bf16[2,128,8,128]{3,2,1,0:T(8,128)(2,1)S(1)}, u32[]{:S(2)}, u32[]{:S(2)}) collective-permute-start(bf16[2,128,8,128]{3,2,1,0:T(8,128)(2,1)S(1)} %get-tuple-element.14), channel_id=1, source_target_pairs={{0,64},{1,65},{2,66},{3,67},{4,68},{5,69},{6,70},{7,71},{8,72},{9,... | collective-permute-start | bytes 1572872 | tf_op jit(solution)/shard_map/ppermute | solution.py:315
  42.1 1.9 %collective-permute-start.3 = (bf16[128,8,128]{2,1,0:T(8,128)(2,1)S(1)}, bf16[128,8,128]{2,1,0:T(8,128)(2,1)S(1)}, u32[]{:S(2)}, u32[]{:S(2)}) collective-permute-start(bf16[128,8,128]{2,1,0:T(8,128)(2,1)S(1)} %bitcast.15), channel_id=1, source_target_pairs={{0,2},{1,3},{2,0},{3,1},{4,6},{5,7},{6,4},{7,5},{8,10},{9,11},{10,... | collective-permute-start | bytes 786440 | tf_op jit(solution)/shard_map/ppermute | solution.py:315
  44.0 4.3 %collective-permute-start.2 = (bf16[128,8,128]{2,1,0:T(8,128)(2,1)S(1)}, bf16[128,8,128]{2,1,0:T(8,128)(2,1)S(1)}, u32[]{:S(2)}, u32[]{:S(2)}) collective-permute-start(bf16[128,8,128]{2,1,0:T(8,128)(2,1)S(1)} %bitcast.16), channel_id=1, source_target_pairs={{0,3},{1,0},{2,1},{3,2},{4,7},{5,4},{6,5},{7,6},{8,11},{9,8},{10,9... | collective-permute-start | bytes 786440 | tf_op jit(solution)/shard_map/ppermute | solution.py:315
  48.4 2.1 %collective-permute-start.4 = (bf16[2,128,8,128]{3,2,1,0:T(8,128)(2,1)S(1)}, bf16[2,128,8,128]{3,2,1,0:T(8,128)(2,1)S(1)}, u32[]{:S(2)}, u32[]{:S(2)}) collective-permute-start(bf16[2,128,8,128]{3,2,1,0:T(8,128)(2,1)S(1)} %pad_maximum_fusion.2.refs_0_), channel_id=1, source_target_pairs={{0,4},{1,5},{2,6},{3,7},{4,8},{5,9},{6,10},{7,11},{8,12},{9,13},{1... | collective-permute-start | bytes 1572872 | tf_op jit(solution)/shard_map/ppermute | solution.py:315
  50.5 8.7 %collective-permute-done.3 = bf16[128,8,128]{2,1,0:T(8,128)(2,1)S(1)} collective-permute-done((bf16[128,8,128]{2,1,0:T(8,128)(2,1)S(1)}, bf16[128,8,128]{2,1,0:T(8,128)(2,1)S(1)}, u32[]{:S(2)}, u32[]{:S(2)}) %collective-permute-start.3) | collective-permute-done | bytes 262176 | tf_op jit(solution)/shard_map/ppermute | solution.py:315
  59.2 2.8 %collective-permute-done.2 = bf16[128,8,128]{2,1,0:T(8,128)(2,1)S(1)} collective-permute-done((bf16[128,8,128]{2,1,0:T(8,128)(2,1)S(1)}, bf16[128,8,128]{2,1,0:T(8,128)(2,1)S(1)}, u32[]{:S(2)}, u32[]{:S(2)}) %collective-permute-start.2) | collective-permute-done | bytes 262176 | tf_op jit(solution)/shard_map/ppermute | solution.py:315
  62.1 2.5 %collective-permute-start.7 = (bf16[2,128,8,128]{3,2,1,0:T(8,128)(2,1)S(1)}, bf16[2,128,8,128]{3,2,1,0:T(8,128)(2,1)S(1)}, u32[]{:S(2)}, u32[]{:S(2)}) collective-permute-start(bf16[2,128,8,128]{3,2,1,0:T(8,128)(2,1)S(1)} %pad_maximum_fusion.3.refs_1_), channel_id=1, source_target_pairs={{0,12},{1,13},{2,14},{3,15},{4,0},{5,1},{6,2},{7,3},{8,4},{9,5},{1... | collective-permute-start | bytes 1572872 | tf_op jit(solution)/shard_map/ppermute | solution.py:315
  64.6 4.6 %collective-permute-start.16 = (bf16[2,128,8,128]{3,2,1,0:T(8,128)(2,1)S(1)}, bf16[2,128,8,128]{3,2,1,0:T(8,128)(2,1)S(1)}, u32[]{:S(2)}, u32[]{:S(2)}) collective-permute-start(bf16[2,128,8,128]{3,2,1,0:T(8,128)(2,1)S(1)} %collective-permute-done.14.refs_13_), channel_id=1, source_target_pairs={{0,448},{1,449},{2,450},{3,451},{4,452},{5,453},{6,454},{7,455},{8... | collective-permute-start | bytes 1572872 | tf_op jit(solution)/shard_map/ppermute | solution.py:315
  69.1 1.9 %collective-permute-start.15 = (bf16[2,128,8,128]{3,2,1,0:T(8,128)(2,1)S(1)}, bf16[2,128,8,128]{3,2,1,0:T(8,128)(2,1)S(1)}, u32[]{:S(2)}, u32[]{:S(2)}) collective-permute-start(bf16[2,128,8,128]{3,2,1,0:T(8,128)(2,1)S(1)} %collective-permute-done.13.refs_12_), channel_id=1, source_target_pairs={{0,64},{1,65},{2,66},{3,67},{4,68},{5,69},{6,70},{7,71},{8,72},{9,... | collective-permute-start | bytes 1572872 | tf_op jit(solution)/shard_map/ppermute | solution.py:315
  71.1 2.1 %collective-permute-start.6 = (bf16[2,128,8,128]{3,2,1,0:T(8,128)(2,1)S(1)}, bf16[2,128,8,128]{3,2,1,0:T(8,128)(2,1)S(1)}, u32[]{:S(2)}, u32[]{:S(2)}) collective-permute-start(bf16[2,128,8,128]{3,2,1,0:T(8,128)(2,1)S(1)} %pad_maximum_fusion.2.refs_0_), channel_id=1, source_target_pairs={{0,12},{1,13},{2,14},{3,15},{4,0},{5,1},{6,2},{7,3},{8,4},{9,5},{1... | collective-permute-start | bytes 1572872 | tf_op jit(solution)/shard_map/ppermute | solution.py:315
  73.2 4.4 %collective-permute-start.5 = (bf16[2,128,8,128]{3,2,1,0:T(8,128)(2,1)S(1)}, bf16[2,128,8,128]{3,2,1,0:T(8,128)(2,1)S(1)}, u32[]{:S(2)}, u32[]{:S(2)}) collective-permute-start(bf16[2,128,8,128]{3,2,1,0:T(8,128)(2,1)S(1)} %pad_maximum_fusion.3.refs_1_), channel_id=1, source_target_pairs={{0,4},{1,5},{2,6},{3,7},{4,8},{5,9},{6,10},{7,11},{8,12},{9,13},{1... | collective-permute-start | bytes 1572872 | tf_op jit(solution)/shard_map/ppermute | solution.py:315
  77.6 2.8 %collective-permute-start.8 = (bf16[2,128,8,128]{3,2,1,0:T(8,128)(2,1)S(1)}, bf16[2,128,8,128]{3,2,1,0:T(8,128)(2,1)S(1)}, u32[]{:S(2)}, u32[]{:S(2)}) collective-permute-start(bf16[2,128,8,128]{3,2,1,0:T(8,128)(2,1)S(1)} %collective-permute-done.4.refs_2_), channel_id=1, source_target_pairs={{0,4},{1,5},{2,6},{3,7},{4,8},{5,9},{6,10},{7,11},{8,12},{9,13},{1... | collective-permute-start | bytes 1572872 | tf_op jit(solution)/shard_map/ppermute | solution.py:315
  80.4 2.5 %collective-permute-start.9 = (bf16[2,128,8,128]{3,2,1,0:T(8,128)(2,1)S(1)}, bf16[2,128,8,128]{3,2,1,0:T(8,128)(2,1)S(1)}, u32[]{:S(2)}, u32[]{:S(2)}) collective-permute-start(bf16[2,128,8,128]{3,2,1,0:T(8,128)(2,1)S(1)} %collective-permute-done.7.refs_5_), channel_id=1, source_target_pairs={{0,12},{1,13},{2,14},{3,15},{4,0},{5,1},{6,2},{7,3},{8,4},{9,5},{1... | collective-permute-start | bytes 1572872 | tf_op jit(solution)/shard_map/ppermute | solution.py:315
  83.5 1.9 %collective-permute-start.17 = (bf16[2,128,8,128]{3,2,1,0:T(8,128)(2,1)S(1)}, bf16[2,128,8,128]{3,2,1,0:T(8,128)(2,1)S(1)}, u32[]{:S(2)}, u32[]{:S(2)}) collective-permute-start(bf16[2,128,8,128]{3,2,1,0:T(8,128)(2,1)S(1)} %collective-permute-done.15.refs_14_), channel_id=1, source_target_pairs={{0,64},{1,65},{2,66},{3,67},{4,68},{5,69},{6,70},{7,71},{8,72},{9,... | collective-permute-start | bytes 1572872 | tf_op jit(solution)/shard_map/ppermute | solution.py:315
  85.5 2.7 %collective-permute-done.6.refs_4_ = bf16[2,128,8,128]{3,2,1,0:T(8,128)(2,1)S(1)} collective-permute-done((bf16[2,128,8,128]{3,2,1,0:T(8,128)(2,1)S(1)}, bf16[2,128,8,128]{3,2,1,0:T(8,128)(2,1)S(1)}, u32[]{:S(2)}, u32[]{:S(2)}) %collective-permute-start.6) | collective-permute-done | bytes 524320 | tf_op jit(solution)/shard_map/ppermute | solution.py:315
  88.2 3.1 %collective-permute-start.19 = (bf16[128,8,128]{2,1,0:T(8,128)(2,1)S(1)}, bf16[128,8,128]{2,1,0:T(8,128)(2,1)S(1)}, u32[]{:S(2)}, u32[]{:S(2)}) collective-permute-start(bf16[128,8,128]{2,1,0:T(8,128)(2,1)S(1)} %slice_bitcast_fusion), channel_id=1, source_target_pairs={{0,384},{1,385},{2,386},{3,387},{4,388},{5,389},{6,390},{7,391},{8... | collective-permute-start | bytes 786440 | tf_op jit(solution)/shard_map/ppermute | solution.py:315
  91.3 3.4 %collective-permute-start.18 = (bf16[128,8,128]{2,1,0:T(8,128)(2,1)S(1)}, bf16[128,8,128]{2,1,0:T(8,128)(2,1)S(1)}, u32[]{:S(2)}, u32[]{:S(2)}) collective-permute-start(bf16[128,8,128]{2,1,0:T(8,128)(2,1)S(1)} %slice_bitcast_fusion), channel_id=1, source_target_pairs={{0,448},{1,449},{2,450},{3,451},{4,452},{5,453},{6,454},{7,455},{8... | collective-permute-start | bytes 786440 | tf_op jit(solution)/shard_map/ppermute | solution.py:315
  94.7 2.9 %collective-permute-done.8.refs_6_ = bf16[2,128,8,128]{3,2,1,0:T(8,128)(2,1)S(1)} collective-permute-done((bf16[2,128,8,128]{3,2,1,0:T(8,128)(2,1)S(1)}, bf16[2,128,8,128]{3,2,1,0:T(8,128)(2,1)S(1)}, u32[]{:S(2)}, u32[]{:S(2)}) %collective-permute-start.8) | collective-permute-done | bytes 524320 | tf_op jit(solution)/shard_map/ppermute | solution.py:315
  97.6 1.8 %collective-permute-done.9.refs_7_ = bf16[2,128,8,128]{3,2,1,0:T(8,128)(2,1)S(1)} collective-permute-done((bf16[2,128,8,128]{3,2,1,0:T(8,128)(2,1)S(1)}, bf16[2,128,8,128]{3,2,1,0:T(8,128)(2,1)S(1)}, u32[]{:S(2)}, u32[]{:S(2)}) %collective-permute-start.9) | collective-permute-done | bytes 524320 | tf_op jit(solution)/shard_map/ppermute | solution.py:315
  99.5 9.3 %collective-permute-done.18.refs_17_ = bf16[128,8,128]{2,1,0:T(8,128)(2,1)S(1)} collective-permute-done((bf16[128,8,128]{2,1,0:T(8,128)(2,1)S(1)}, bf16[128,8,128]{2,1,0:T(8,128)(2,1)S(1)}, u32[]{:S(2)}, u32[]{:S(2)}) %collective-permute-start.18) | collective-permute-done | bytes 262176 | tf_op jit(solution)/shard_map/ppermute | solution.py:315
  108.8 6.3 %cross.1 = (bf16[64,128,128]{2,1,0:T(8,128)(2,1)S(1)}, bf16[64,256,128]{2,1,0:T(8,128)(2,1)S(1)}) custom-call(bf16[2,128,8,128]{3,2,1,0:T(8,128)(2,1)S(1)} %pad_maximum_fusion.2.refs_0_, bf16[2,128,8,128]{3,2,1,0:T(8,128)(2,1)S(1)} %pad_maximum_fusion.3.refs_1_, bf16[2,128,8,128]{3,2,1,0:T(8,128)(2,1)S(1)} %collective-permute-done.4.refs_2_, ...), custom_call_target="tpu_custom_call" | custom-call | tf_op jit(solution)/shard_map/cross/pallas_call | solution.py:271
  115.0 5.1 %collective-permute-start.20 = (bf16[64,128,128]{2,1,0:T(8,128)(2,1)S(1)}, bf16[64,128,128]{2,1,0:T(8,128)(2,1)S(1)}, u32[]{:S(2)}, u32[]{:S(2)}) collective-permute-start(bf16[64,128,128]{2,1,0:T(8,128)(2,1)S(1)} %get-tuple-element.12), channel_id=1, source_target_pairs={{0,16},{1,17},{2,18},{3,19},{4,20},{5,21},{6,22},{7,23},{8,24},{9,... | collective-permute-start | bytes 6291464 | tf_op jit(solution)/shard_map/ppermute | solution.py:315
  121.8 2.1 %collective-permute-done.20.got_ref = bf16[64,128,128]{2,1,0:T(8,128)(2,1)S(1)} collective-permute-done((bf16[64,128,128]{2,1,0:T(8,128)(2,1)S(1)}, bf16[64,128,128]{2,1,0:T(8,128)(2,1)S(1)}, u32[]{:S(2)}, u32[]{:S(2)}) %collective-permute-start.20) | collective-permute-done | bytes 2097184 | tf_op jit(solution)/shard_map/ppermute | solution.py:315
  123.9 3.1 %finish.1 = bf16[64,128,128]{2,1,0:T(8,128)(2,1)} custom-call(f32[64,128,128]{2,1,0:T(8,128)S(1)} %lag_own.1.own_ref, bf16[64,128,128]{2,1,0:T(8,128)(2,1)S(1)} %collective-permute-done.20.got_ref), custom_call_target="tpu_custom_call" | custom-call | tf_op jit(solution)/shard_map/finish/pallas_call | solution.py:254
  (21 shorter events, 3.6 us)
Async XLA Ops:
  2.7 3.5 %collective-permute-start = (bf16[512,128]{1,0:T(8,128)(2,1)S(1)}, bf16[512,128]{1,0:T(8,128)(2,1)S(1)}, u32[]{:S(2)}, u32[]{:S(2)}) collective-permute-start(bf16[512,128]{1,0:T(8,128)(2,1)S(1)} %get-tuple-element.10), channel_id=1, source_target_pairs={{0,16},{1,17},{2,18},{3,19},{4,20},{5,21},{6,22},{7,23},{8,24},{9,... | collective-permute-start | bytes 393224 | tf_op jit(solution)/shard_map/ppermute | solution.py:315
  6.4 19.9 %collective-permute-start.12 = (bf16[128,8,128]{2,1,0:T(8,128)(2,1)S(1)}, bf16[128,8,128]{2,1,0:T(8,128)(2,1)S(1)}, u32[]{:S(2)}, u32[]{:S(2)}) collective-permute-start(bf16[128,8,128]{2,1,0:T(8,128)(2,1)S(1)} %bitcast.11), channel_id=1, source_target_pairs={{0,448},{1,449},{2,450},{3,451},{4,452},{5,453},{6,454},{7,455},{8... | collective-permute-start | bytes 786440 | tf_op jit(solution)/shard_map/ppermute | solution.py:315
  11.5 14.8 %collective-permute-start.11 = (bf16[128,8,128]{2,1,0:T(8,128)(2,1)S(1)}, bf16[128,8,128]{2,1,0:T(8,128)(2,1)S(1)}, u32[]{:S(2)}, u32[]{:S(2)}) collective-permute-start(bf16[128,8,128]{2,1,0:T(8,128)(2,1)S(1)} %bitcast.12), channel_id=1, source_target_pairs={{0,64},{1,65},{2,66},{3,67},{4,68},{5,69},{6,70},{7,71},{8,72},{9,... | collective-permute-start | bytes 786440 | tf_op jit(solution)/shard_map/ppermute | solution.py:315
  13.4 22.4 %collective-permute-start.10 = (bf16[128,8,128]{2,1,0:T(8,128)(2,1)S(1)}, bf16[128,8,128]{2,1,0:T(8,128)(2,1)S(1)}, u32[]{:S(2)}, u32[]{:S(2)}) collective-permute-start(bf16[128,8,128]{2,1,0:T(8,128)(2,1)S(1)} %bitcast.13), channel_id=1, source_target_pairs={{0,32},{1,33},{2,34},{3,35},{4,36},{5,37},{6,38},{7,39},{8,40},{9,... | collective-permute-start | bytes 786440 | tf_op jit(solution)/shard_map/ppermute | solution.py:315
  23.1 25.2 %collective-permute-start.1 = (bf16[128,8,128]{2,1,0:T(8,128)(2,1)S(1)}, bf16[128,8,128]{2,1,0:T(8,128)(2,1)S(1)}, u32[]{:S(2)}, u32[]{:S(2)}) collective-permute-start(bf16[128,8,128]{2,1,0:T(8,128)(2,1)S(1)} %bitcast.14), channel_id=1, source_target_pairs={{0,1},{1,2},{2,3},{3,0},{4,5},{5,6},{6,7},{7,4},{8,9},{9,10},{10,1... | collective-permute-start | bytes 786440 | tf_op jit(solution)/shard_map/ppermute | solution.py:315
  35.8 73.0 %copy-start = (bf16[2,128,256]{2,1,0:T(8,128)(2,1)S(1)}, bf16[2,128,256]{2,1,0:T(8,128)(2,1)}, u32[]{:S(2)}) copy-start(bf16[2,128,256]{2,1,0:T(8,128)(2,1)} %constant.8.clone.refs_19_.inv_ref) | copy-start | bytes 393220
  35.9 28.7 %collective-permute-start.14 = (bf16[2,128,8,128]{3,2,1,0:T(8,128)(2,1)S(1)}, bf16[2,128,8,128]{3,2,1,0:T(8,128)(2,1)S(1)}, u32[]{:S(2)}, u32[]{:S(2)}) collective-permute-start(bf16[2,128,8,128]{3,2,1,0:T(8,128)(2,1)S(1)} %get-tuple-element.13), channel_id=1, source_target_pairs={{0,448},{1,449},{2,450},{3,451},{4,452},{5,453},{6,454},{7,455},{8... | collective-permute-start | bytes 1572872 | tf_op jit(solution)/shard_map/ppermute | solution.py:315
  40.2 29.0 %collective-permute-start.13 = (bf16[2,128,8,128]{3,2,1,0:T(8,128)(2,1)S(1)}, bf16[2,128,8,128]{3,2,1,0:T(8,128)(2,1)S(1)}, u32[]{:S(2)}, u32[]{:S(2)}) collective-permute-start(bf16[2,128,8,128]{3,2,1,0:T(8,128)(2,1)S(1)} %get-tuple-element.14), channel_id=1, source_target_pairs={{0,64},{1,65},{2,66},{3,67},{4,68},{5,69},{6,70},{7,71},{8,72},{9,... | collective-permute-start | bytes 1572872 | tf_op jit(solution)/shard_map/ppermute | solution.py:315
  42.1 17.1 %collective-permute-start.3 = (bf16[128,8,128]{2,1,0:T(8,128)(2,1)S(1)}, bf16[128,8,128]{2,1,0:T(8,128)(2,1)S(1)}, u32[]{:S(2)}, u32[]{:S(2)}) collective-permute-start(bf16[128,8,128]{2,1,0:T(8,128)(2,1)S(1)} %bitcast.15), channel_id=1, source_target_pairs={{0,2},{1,3},{2,0},{3,1},{4,6},{5,7},{6,4},{7,5},{8,10},{9,11},{10,... | collective-permute-start | bytes 786440 | tf_op jit(solution)/shard_map/ppermute | solution.py:315
  44.0 18.0 %collective-permute-start.2 = (bf16[128,8,128]{2,1,0:T(8,128)(2,1)S(1)}, bf16[128,8,128]{2,1,0:T(8,128)(2,1)S(1)}, u32[]{:S(2)}, u32[]{:S(2)}) collective-permute-start(bf16[128,8,128]{2,1,0:T(8,128)(2,1)S(1)} %bitcast.16), channel_id=1, source_target_pairs={{0,3},{1,0},{2,1},{3,2},{4,7},{5,4},{6,5},{7,6},{8,11},{9,8},{10,9... | collective-permute-start | bytes 786440 | tf_op jit(solution)/shard_map/ppermute | solution.py:315
  48.4 24.8 %collective-permute-start.4 = (bf16[2,128,8,128]{3,2,1,0:T(8,128)(2,1)S(1)}, bf16[2,128,8,128]{3,2,1,0:T(8,128)(2,1)S(1)}, u32[]{:S(2)}, u32[]{:S(2)}) collective-permute-start(bf16[2,128,8,128]{3,2,1,0:T(8,128)(2,1)S(1)} %pad_maximum_fusion.2.refs_0_), channel_id=1, source_target_pairs={{0,4},{1,5},{2,6},{3,7},{4,8},{5,9},{6,10},{7,11},{8,12},{9,13},{1... | collective-permute-start | bytes 1572872 | tf_op jit(solution)/shard_map/ppermute | solution.py:315
  62.1 15.5 %collective-permute-start.7 = (bf16[2,128,8,128]{3,2,1,0:T(8,128)(2,1)S(1)}, bf16[2,128,8,128]{3,2,1,0:T(8,128)(2,1)S(1)}, u32[]{:S(2)}, u32[]{:S(2)}) collective-permute-start(bf16[2,128,8,128]{3,2,1,0:T(8,128)(2,1)S(1)} %pad_maximum_fusion.3.refs_1_), channel_id=1, source_target_pairs={{0,12},{1,13},{2,14},{3,15},{4,0},{5,1},{6,2},{7,3},{8,4},{9,5},{1... | collective-permute-start | bytes 1572872 | tf_op jit(solution)/shard_map/ppermute | solution.py:315
  64.6 15.9 %collective-permute-start.16 = (bf16[2,128,8,128]{3,2,1,0:T(8,128)(2,1)S(1)}, bf16[2,128,8,128]{3,2,1,0:T(8,128)(2,1)S(1)}, u32[]{:S(2)}, u32[]{:S(2)}) collective-permute-start(bf16[2,128,8,128]{3,2,1,0:T(8,128)(2,1)S(1)} %collective-permute-done.14.refs_13_), channel_id=1, source_target_pairs={{0,448},{1,449},{2,450},{3,451},{4,452},{5,453},{6,454},{7,455},{8... | collective-permute-start | bytes 1572872 | tf_op jit(solution)/shard_map/ppermute | solution.py:315
  69.1 14.4 %collective-permute-start.15 = (bf16[2,128,8,128]{3,2,1,0:T(8,128)(2,1)S(1)}, bf16[2,128,8,128]{3,2,1,0:T(8,128)(2,1)S(1)}, u32[]{:S(2)}, u32[]{:S(2)}) collective-permute-start(bf16[2,128,8,128]{3,2,1,0:T(8,128)(2,1)S(1)} %collective-permute-done.13.refs_12_), channel_id=1, source_target_pairs={{0,64},{1,65},{2,66},{3,67},{4,68},{5,69},{6,70},{7,71},{8,72},{9,... | collective-permute-start | bytes 1572872 | tf_op jit(solution)/shard_map/ppermute | solution.py:315
  71.1 17.1 %collective-permute-start.6 = (bf16[2,128,8,128]{3,2,1,0:T(8,128)(2,1)S(1)}, bf16[2,128,8,128]{3,2,1,0:T(8,128)(2,1)S(1)}, u32[]{:S(2)}, u32[]{:S(2)}) collective-permute-start(bf16[2,128,8,128]{3,2,1,0:T(8,128)(2,1)S(1)} %pad_maximum_fusion.2.refs_0_), channel_id=1, source_target_pairs={{0,12},{1,13},{2,14},{3,15},{4,0},{5,1},{6,2},{7,3},{8,4},{9,5},{1... | collective-permute-start | bytes 1572872 | tf_op jit(solution)/shard_map/ppermute | solution.py:315
  73.2 18.1 %collective-permute-start.5 = (bf16[2,128,8,128]{3,2,1,0:T(8,128)(2,1)S(1)}, bf16[2,128,8,128]{3,2,1,0:T(8,128)(2,1)S(1)}, u32[]{:S(2)}, u32[]{:S(2)}) collective-permute-start(bf16[2,128,8,128]{3,2,1,0:T(8,128)(2,1)S(1)} %pad_maximum_fusion.3.refs_1_), channel_id=1, source_target_pairs={{0,4},{1,5},{2,6},{3,7},{4,8},{5,9},{6,10},{7,11},{8,12},{9,13},{1... | collective-permute-start | bytes 1572872 | tf_op jit(solution)/shard_map/ppermute | solution.py:315
  77.6 20.0 %collective-permute-start.8 = (bf16[2,128,8,128]{3,2,1,0:T(8,128)(2,1)S(1)}, bf16[2,128,8,128]{3,2,1,0:T(8,128)(2,1)S(1)}, u32[]{:S(2)}, u32[]{:S(2)}) collective-permute-start(bf16[2,128,8,128]{3,2,1,0:T(8,128)(2,1)S(1)} %collective-permute-done.4.refs_2_), channel_id=1, source_target_pairs={{0,4},{1,5},{2,6},{3,7},{4,8},{5,9},{6,10},{7,11},{8,12},{9,13},{1... | collective-permute-start | bytes 1572872 | tf_op jit(solution)/shard_map/ppermute | solution.py:315
  80.4 19.0 %collective-permute-start.9 = (bf16[2,128,8,128]{3,2,1,0:T(8,128)(2,1)S(1)}, bf16[2,128,8,128]{3,2,1,0:T(8,128)(2,1)S(1)}, u32[]{:S(2)}, u32[]{:S(2)}) collective-permute-start(bf16[2,128,8,128]{3,2,1,0:T(8,128)(2,1)S(1)} %collective-permute-done.7.refs_5_), channel_id=1, source_target_pairs={{0,12},{1,13},{2,14},{3,15},{4,0},{5,1},{6,2},{7,3},{8,4},{9,5},{1... | collective-permute-start | bytes 1572872 | tf_op jit(solution)/shard_map/ppermute | solution.py:315
  83.5 25.2 %collective-permute-start.17 = (bf16[2,128,8,128]{3,2,1,0:T(8,128)(2,1)S(1)}, bf16[2,128,8,128]{3,2,1,0:T(8,128)(2,1)S(1)}, u32[]{:S(2)}, u32[]{:S(2)}) collective-permute-start(bf16[2,128,8,128]{3,2,1,0:T(8,128)(2,1)S(1)} %collective-permute-done.15.refs_14_), channel_id=1, source_target_pairs={{0,64},{1,65},{2,66},{3,67},{4,68},{5,69},{6,70},{7,71},{8,72},{9,... | collective-permute-start | bytes 1572872 | tf_op jit(solution)/shard_map/ppermute | solution.py:315
  88.2 11.2 %collective-permute-start.19 = (bf16[128,8,128]{2,1,0:T(8,128)(2,1)S(1)}, bf16[128,8,128]{2,1,0:T(8,128)(2,1)S(1)}, u32[]{:S(2)}, u32[]{:S(2)}) collective-permute-start(bf16[128,8,128]{2,1,0:T(8,128)(2,1)S(1)} %slice_bitcast_fusion), channel_id=1, source_target_pairs={{0,384},{1,385},{2,386},{3,387},{4,388},{5,389},{6,390},{7,391},{8... | collective-permute-start | bytes 786440 | tf_op jit(solution)/shard_map/ppermute | solution.py:315
  91.3 17.4 %collective-permute-start.18 = (bf16[128,8,128]{2,1,0:T(8,128)(2,1)S(1)}, bf16[128,8,128]{2,1,0:T(8,128)(2,1)S(1)}, u32[]{:S(2)}, u32[]{:S(2)}) collective-permute-start(bf16[128,8,128]{2,1,0:T(8,128)(2,1)S(1)} %slice_bitcast_fusion), channel_id=1, source_target_pairs={{0,448},{1,449},{2,450},{3,451},{4,452},{5,453},{6,454},{7,455},{8... | collective-permute-start | bytes 786440 | tf_op jit(solution)/shard_map/ppermute | solution.py:315
  115.0 8.9 %collective-permute-start.20 = (bf16[64,128,128]{2,1,0:T(8,128)(2,1)S(1)}, bf16[64,128,128]{2,1,0:T(8,128)(2,1)S(1)}, u32[]{:S(2)}, u32[]{:S(2)}) collective-permute-start(bf16[64,128,128]{2,1,0:T(8,128)(2,1)S(1)} %get-tuple-element.12), channel_id=1, source_target_pairs={{0,16},{1,17},{2,18},{3,19},{4,20},{5,21},{6,22},{7,23},{8,24},{9,... | collective-permute-start | bytes 6291464 | tf_op jit(solution)/shard_map/ppermute | solution.py:315

commit v6 on v5

--- a/solution.py
+++ b/solution.py
@@ -242,26 +242,6 @@
     )(in_vmem(stacked), inverse)
 
 
-def finish_kernel(own_ref, got_ref, out_ref):
-    step = out_ref.shape[0]
-    rows = pl.ds(pl.multiple_of(pl.program_id(0) * step, step), step)
-    out_ref[...] = (own_ref[rows] + got_ref[rows].astype(jnp.float32)).astype(jnp.bfloat16)
-
-
-def finish(own, got):
-    step = 8
-    vmem = pl.BlockSpec(memory_space=pltpu.VMEM)
-    return pl.pallas_call(
-        finish_kernel,
-        out_shape=jax.ShapeDtypeStruct((64, 128, LAGS), jnp.bfloat16),
-        grid=(64 // step,),
-        in_specs=[vmem, vmem],
-        out_specs=pl.BlockSpec((step, 128, LAGS), lambda n: (n, 0, 0)),
-        compiler_params=pltpu.CompilerParams(vmem_limit_bytes=16 * 1024 * 1024),
-        name="finish",
-    )(in_vmem(own), in_vmem(got))
-
-
 UNROLL = 16
 
 
@@ -302,7 +282,6 @@
 STEP_L = [permutation(lambda y, h, c, x, l, d=d: (y, h, c, x, l + d)) for d in range(4)]
 Y_UP = permutation(lambda y, h, c, x, l: (y + 1, h, c, x, l))
 Y_DOWN = permutation(lambda y, h, c, x, l: (y - 1, h, c, x, l))
-Y_DOWN2 = permutation(lambda y, h, c, x, l: (y - 2, h, c, x, l))
 X_UP = permutation(lambda y, h, c, x, l: (y, h, c, x + 1, l))
 X_DOWN = permutation(lambda y, h, c, x, l: (y, h, c, x - 1, l))
 
@@ -333,17 +312,17 @@
     x2_up, x2_down = move(x2, X_UP), move(x2, X_DOWN)
     x1_far = move(x1_up, X_UP)
     up4 = move(up3, Y_UP)
-    far = down3[1]
-    down4 = move(far, Y_DOWN)
+    down4 = move(down3[1], Y_DOWN)
     x2_far = move(x2_down, X_DOWN)
-    down5 = move(far, Y_DOWN2)
+    down5 = move(down4, Y_DOWN)
 
     firsts = (x1, x2, x1_up, x2_up, x1_down, x2_down, x1_far, x2_far)
     seconds = (piece, other, up1, down1, up2, down2, up3, down3, up4, down4, down5)
     table = jnp.asarray(inverse)
     sent, stacked = cross(firsts, seconds, table)
     got = move(sent, SWAP_CORE)
-    return finish(lag_own(stacked, table), got)
+    own = lag_own(stacked, table)
+    return (own + got.astype(jnp.float32)).astype(jnp.bfloat16)
 
 
 def solution(mesh):

time: 128 us -> 128 us (level)
  the two profiles are of different devices: /device:TPU:71 before, /device:TPU:131 now
where the time goes in v6:
time: 128 us; the launch traced here: 127 us
  starting transfers between devices  73.7 us (58%)
  waiting for transfers between devices  40 us (31%)
  Pallas kernels  10.7 us (8%)
  other arithmetic  2.14 us (2%)
    ppermute x21, starting transfers between devices, move(): return lax.ppermute(value, AXES, pairs)  73.7 us
    ppermute x21, waiting for transfers between devices, move(): return lax.ppermute(value, AXES, pairs)  40 us
    pallas_call x1, Pallas kernels, cross(): pl.pallas_call(kernel, out_shape=(pltpu.VMEM((64, 128, LAGS), jnp.bfloat1...  6.26 us
    pallas_call x1, Pallas kernels, whiten(): pl.pallas_call(whiten_kernel, out_shape=(shape, shape), in_specs=[smem, v...  2.69 us
  transfers between devices with their start and end apart: 21, of which 10 were waited for; matrix products, arithmetic and copies ran while one was open for 0% of the time, Pallas kernels for 1%

profile of v6, /device:TPU:131, one launch (start us, length us, event | category | flops | bytes accessed | tf_op | source)
XLA Modules:
  0.0 126.9 jit_solution(17534133342664353305)
XLA Ops:
  0.0 2.7 %whiten.1 = (bf16[512,128]{1,0:T(8,128)(2,1)S(1)}, bf16[512,128]{1,0:T(8,128)(2,1)S(1)}) custom-call(s32[4]{0:T(128)} %flags_ref.1, bf16[256,512]{1,0:T(8,128)(2,1)} %bitcast.22, bf16[3,512,512]{2,1,0:T(8,128)(2,1)} %constant.6.clone.dft_ref, bf16[256,256]{1,0:T(8,128)(2,1)} %constant.7.clone.near_ref), custom_call_target="tpu_custom_call" | custom-call | tf_op jit(solution)/shard_map/whiten/pallas_call | solution.py:101
  2.7 2.6 %collective-permute-start = (bf16[512,128]{1,0:T(8,128)(2,1)S(1)}, bf16[512,128]{1,0:T(8,128)(2,1)S(1)}, u32[]{:S(2)}, u32[]{:S(2)}) collective-permute-start(bf16[512,128]{1,0:T(8,128)(2,1)S(1)} %get-tuple-element.10), channel_id=1, source_target_pairs={{0,16},{1,17},{2,18},{3,19},{4,20},{5,21},{6,22},{7,23},{8,24},{9,... | collective-permute-start | bytes 393224 | tf_op jit(solution)/shard_map/ppermute | solution.py:294
  6.4 5.1 %collective-permute-start.12 = (bf16[128,8,128]{2,1,0:T(8,128)(2,1)S(1)}, bf16[128,8,128]{2,1,0:T(8,128)(2,1)S(1)}, u32[]{:S(2)}, u32[]{:S(2)}) collective-permute-start(bf16[128,8,128]{2,1,0:T(8,128)(2,1)S(1)} %bitcast.11), channel_id=1, source_target_pairs={{0,448},{1,449},{2,450},{3,451},{4,452},{5,453},{6,454},{7,455},{8... | collective-permute-start | bytes 786440 | tf_op jit(solution)/shard_map/ppermute | solution.py:294
  11.5 1.9 %collective-permute-start.11 = (bf16[128,8,128]{2,1,0:T(8,128)(2,1)S(1)}, bf16[128,8,128]{2,1,0:T(8,128)(2,1)S(1)}, u32[]{:S(2)}, u32[]{:S(2)}) collective-permute-start(bf16[128,8,128]{2,1,0:T(8,128)(2,1)S(1)} %bitcast.12), channel_id=1, source_target_pairs={{0,64},{1,65},{2,66},{3,67},{4,68},{5,69},{6,70},{7,71},{8,72},{9,... | collective-permute-start | bytes 786440 | tf_op jit(solution)/shard_map/ppermute | solution.py:294
  13.4 8.8 %collective-permute-start.10 = (bf16[128,8,128]{2,1,0:T(8,128)(2,1)S(1)}, bf16[128,8,128]{2,1,0:T(8,128)(2,1)S(1)}, u32[]{:S(2)}, u32[]{:S(2)}) collective-permute-start(bf16[128,8,128]{2,1,0:T(8,128)(2,1)S(1)} %bitcast.13), channel_id=1, source_target_pairs={{0,32},{1,33},{2,34},{3,35},{4,36},{5,37},{6,38},{7,39},{8,40},{9,... | collective-permute-start | bytes 786440 | tf_op jit(solution)/shard_map/ppermute | solution.py:294
  22.3 12.3 %collective-permute-done.10.refs_9_ = bf16[128,8,128]{2,1,0:T(8,128)(2,1)S(1)} collective-permute-done((bf16[128,8,128]{2,1,0:T(8,128)(2,1)S(1)}, bf16[128,8,128]{2,1,0:T(8,128)(2,1)S(1)}, u32[]{:S(2)}, u32[]{:S(2)}) %collective-permute-start.10) | collective-permute-done | bytes 262176 | tf_op jit(solution)/shard_map/ppermute | solution.py:294
  34.7 4.6 %collective-permute-start.14 = (bf16[2,128,8,128]{3,2,1,0:T(8,128)(2,1)S(1)}, bf16[2,128,8,128]{3,2,1,0:T(8,128)(2,1)S(1)}, u32[]{:S(2)}, u32[]{:S(2)}) collective-permute-start(bf16[2,128,8,128]{3,2,1,0:T(8,128)(2,1)S(1)} %get-tuple-element.13), channel_id=1, source_target_pairs={{0,448},{1,449},{2,450},{3,451},{4,452},{5,453},{6,454},{7,455},{8... | collective-permute-start | bytes 1572872 | tf_op jit(solution)/shard_map/ppermute | solution.py:294
  39.3 1.9 %collective-permute-start.1 = (bf16[128,8,128]{2,1,0:T(8,128)(2,1)S(1)}, bf16[128,8,128]{2,1,0:T(8,128)(2,1)S(1)}, u32[]{:S(2)}, u32[]{:S(2)}) collective-permute-start(bf16[128,8,128]{2,1,0:T(8,128)(2,1)S(1)} %bitcast.14), channel_id=1, source_target_pairs={{0,1},{1,2},{2,3},{3,0},{4,5},{5,6},{6,7},{7,4},{8,9},{9,10},{10,1... | collective-permute-start | bytes 786440 | tf_op jit(solution)/shard_map/ppermute | solution.py:294
  41.2 2.4 %collective-permute-start.3 = (bf16[128,8,128]{2,1,0:T(8,128)(2,1)S(1)}, bf16[128,8,128]{2,1,0:T(8,128)(2,1)S(1)}, u32[]{:S(2)}, u32[]{:S(2)}) collective-permute-start(bf16[128,8,128]{2,1,0:T(8,128)(2,1)S(1)} %bitcast.15), channel_id=1, source_target_pairs={{0,2},{1,3},{2,0},{3,1},{4,6},{5,7},{6,4},{7,5},{8,10},{9,11},{10,... | collective-permute-start | bytes 786440 | tf_op jit(solution)/shard_map/ppermute | solution.py:294
  43.6 2.9 %collective-permute-start.2 = (bf16[128,8,128]{2,1,0:T(8,128)(2,1)S(1)}, bf16[128,8,128]{2,1,0:T(8,128)(2,1)S(1)}, u32[]{:S(2)}, u32[]{:S(2)}) collective-permute-start(bf16[128,8,128]{2,1,0:T(8,128)(2,1)S(1)} %bitcast.16), channel_id=1, source_target_pairs={{0,3},{1,0},{2,1},{3,2},{4,7},{5,4},{6,5},{7,6},{8,11},{9,8},{10,9... | collective-permute-start | bytes 786440 | tf_op jit(solution)/shard_map/ppermute | solution.py:294
  46.5 1.9 %collective-permute-start.13 = (bf16[2,128,8,128]{3,2,1,0:T(8,128)(2,1)S(1)}, bf16[2,128,8,128]{3,2,1,0:T(8,128)(2,1)S(1)}, u32[]{:S(2)}, u32[]{:S(2)}) collective-permute-start(bf16[2,128,8,128]{3,2,1,0:T(8,128)(2,1)S(1)} %get-tuple-element.14), channel_id=1, source_target_pairs={{0,64},{1,65},{2,66},{3,67},{4,68},{5,69},{6,70},{7,71},{8,72},{9,... | collective-permute-start | bytes 1572872 | tf_op jit(solution)/shard_map/ppermute | solution.py:294
  49.8 3.1 %collective-permute-start.4 = (bf16[2,128,8,128]{3,2,1,0:T(8,128)(2,1)S(1)}, bf16[2,128,8,128]{3,2,1,0:T(8,128)(2,1)S(1)}, u32[]{:S(2)}, u32[]{:S(2)}) collective-permute-start(bf16[2,128,8,128]{3,2,1,0:T(8,128)(2,1)S(1)} %pad_maximum_fusion.2.refs_0_), channel_id=1, source_target_pairs={{0,4},{1,5},{2,6},{3,7},{4,8},{5,9},{6,10},{7,11},{8,12},{9,13},{1... | collective-permute-start | bytes 1572872 | tf_op jit(solution)/shard_map/ppermute | solution.py:294
  53.0 4.4 %collective-permute-done.3 = bf16[128,8,128]{2,1,0:T(8,128)(2,1)S(1)} collective-permute-done((bf16[128,8,128]{2,1,0:T(8,128)(2,1)S(1)}, bf16[128,8,128]{2,1,0:T(8,128)(2,1)S(1)}, u32[]{:S(2)}, u32[]{:S(2)}) %collective-permute-start.3) | collective-permute-done | bytes 262176 | tf_op jit(solution)/shard_map/ppermute | solution.py:294
  57.3 5.6 %collective-permute-done.2 = bf16[128,8,128]{2,1,0:T(8,128)(2,1)S(1)} collective-permute-done((bf16[128,8,128]{2,1,0:T(8,128)(2,1)S(1)}, bf16[128,8,128]{2,1,0:T(8,128)(2,1)S(1)}, u32[]{:S(2)}, u32[]{:S(2)}) %collective-permute-start.2) | collective-permute-done | bytes 262176 | tf_op jit(solution)/shard_map/ppermute | solution.py:294
  63.0 2.2 %collective-permute-start.7 = (bf16[2,128,8,128]{3,2,1,0:T(8,128)(2,1)S(1)}, bf16[2,128,8,128]{3,2,1,0:T(8,128)(2,1)S(1)}, u32[]{:S(2)}, u32[]{:S(2)}) collective-permute-start(bf16[2,128,8,128]{3,2,1,0:T(8,128)(2,1)S(1)} %pad_maximum_fusion.3.refs_1_), channel_id=1, source_target_pairs={{0,12},{1,13},{2,14},{3,15},{4,0},{5,1},{6,2},{7,3},{8,4},{9,5},{1... | collective-permute-start | bytes 1572872 | tf_op jit(solution)/shard_map/ppermute | solution.py:294
  65.2 1.9 %collective-permute-start.16 = (bf16[2,128,8,128]{3,2,1,0:T(8,128)(2,1)S(1)}, bf16[2,128,8,128]{3,2,1,0:T(8,128)(2,1)S(1)}, u32[]{:S(2)}, u32[]{:S(2)}) collective-permute-start(bf16[2,128,8,128]{3,2,1,0:T(8,128)(2,1)S(1)} %collective-permute-done.14.refs_13_), channel_id=1, source_target_pairs={{0,448},{1,449},{2,450},{3,451},{4,452},{5,453},{6,454},{7,455},{8... | collective-permute-start | bytes 1572872 | tf_op jit(solution)/shard_map/ppermute | solution.py:294
  67.1 4.4 %collective-permute-start.6 = (bf16[2,128,8,128]{3,2,1,0:T(8,128)(2,1)S(1)}, bf16[2,128,8,128]{3,2,1,0:T(8,128)(2,1)S(1)}, u32[]{:S(2)}, u32[]{:S(2)}) collective-permute-start(bf16[2,128,8,128]{3,2,1,0:T(8,128)(2,1)S(1)} %pad_maximum_fusion.2.refs_0_), channel_id=1, source_target_pairs={{0,12},{1,13},{2,14},{3,15},{4,0},{5,1},{6,2},{7,3},{8,4},{9,5},{1... | collective-permute-start | bytes 1572872 | tf_op jit(solution)/shard_map/ppermute | solution.py:294
  71.5 3.4 %collective-permute-start.15 = (bf16[2,128,8,128]{3,2,1,0:T(8,128)(2,1)S(1)}, bf16[2,128,8,128]{3,2,1,0:T(8,128)(2,1)S(1)}, u32[]{:S(2)}, u32[]{:S(2)}) collective-permute-start(bf16[2,128,8,128]{3,2,1,0:T(8,128)(2,1)S(1)} %collective-permute-done.13.refs_12_), channel_id=1, source_target_pairs={{0,64},{1,65},{2,66},{3,67},{4,68},{5,69},{6,70},{7,71},{8,72},{9,... | collective-permute-start | bytes 1572872 | tf_op jit(solution)/shard_map/ppermute | solution.py:294
  74.9 1.9 %collective-permute-start.5 = (bf16[2,128,8,128]{3,2,1,0:T(8,128)(2,1)S(1)}, bf16[2,128,8,128]{3,2,1,0:T(8,128)(2,1)S(1)}, u32[]{:S(2)}, u32[]{:S(2)}) collective-permute-start(bf16[2,128,8,128]{3,2,1,0:T(8,128)(2,1)S(1)} %pad_maximum_fusion.3.refs_1_), channel_id=1, source_target_pairs={{0,4},{1,5},{2,6},{3,7},{4,8},{5,9},{6,10},{7,11},{8,12},{9,13},{1... | collective-permute-start | bytes 1572872 | tf_op jit(solution)/shard_map/ppermute | solution.py:294
  76.8 2.1 %collective-permute-start.8 = (bf16[2,128,8,128]{3,2,1,0:T(8,128)(2,1)S(1)}, bf16[2,128,8,128]{3,2,1,0:T(8,128)(2,1)S(1)}, u32[]{:S(2)}, u32[]{:S(2)}) collective-permute-start(bf16[2,128,8,128]{3,2,1,0:T(8,128)(2,1)S(1)} %collective-permute-done.4.refs_2_), channel_id=1, source_target_pairs={{0,4},{1,5},{2,6},{3,7},{4,8},{5,9},{6,10},{7,11},{8,12},{9,13},{1... | collective-permute-start | bytes 1572872 | tf_op jit(solution)/shard_map/ppermute | solution.py:294
  78.9 3.8 %collective-permute-start.9 = (bf16[2,128,8,128]{3,2,1,0:T(8,128)(2,1)S(1)}, bf16[2,128,8,128]{3,2,1,0:T(8,128)(2,1)S(1)}, u32[]{:S(2)}, u32[]{:S(2)}) collective-permute-start(bf16[2,128,8,128]{3,2,1,0:T(8,128)(2,1)S(1)} %collective-permute-done.7.refs_5_), channel_id=1, source_target_pairs={{0,12},{1,13},{2,14},{3,15},{4,0},{5,1},{6,2},{7,3},{8,4},{9,5},{1... | collective-permute-start | bytes 1572872 | tf_op jit(solution)/shard_map/ppermute | solution.py:294
  82.8 3.9 %collective-permute-done.6.refs_4_ = bf16[2,128,8,128]{3,2,1,0:T(8,128)(2,1)S(1)} collective-permute-done((bf16[2,128,8,128]{3,2,1,0:T(8,128)(2,1)S(1)}, bf16[2,128,8,128]{3,2,1,0:T(8,128)(2,1)S(1)}, u32[]{:S(2)}, u32[]{:S(2)}) %collective-permute-start.6) | collective-permute-done | bytes 524320 | tf_op jit(solution)/shard_map/ppermute | solution.py:294
  86.7 1.9 %collective-permute-start.18 = (bf16[128,8,128]{2,1,0:T(8,128)(2,1)S(1)}, bf16[128,8,128]{2,1,0:T(8,128)(2,1)S(1)}, u32[]{:S(2)}, u32[]{:S(2)}) collective-permute-start(bf16[128,8,128]{2,1,0:T(8,128)(2,1)S(1)} %slice_bitcast_fusion), channel_id=1, source_target_pairs={{0,448},{1,449},{2,450},{3,451},{4,452},{5,453},{6,454},{7,455},{8... | collective-permute-start | bytes 786440 | tf_op jit(solution)/shard_map/ppermute | solution.py:294
  88.7 3.4 %collective-permute-start.17 = (bf16[2,128,8,128]{3,2,1,0:T(8,128)(2,1)S(1)}, bf16[2,128,8,128]{3,2,1,0:T(8,128)(2,1)S(1)}, u32[]{:S(2)}, u32[]{:S(2)}) collective-permute-start(bf16[2,128,8,128]{3,2,1,0:T(8,128)(2,1)S(1)} %collective-permute-done.15.refs_14_), channel_id=1, source_target_pairs={{0,64},{1,65},{2,66},{3,67},{4,68},{5,69},{6,70},{7,71},{8,72},{9,... | collective-permute-start | bytes 1572872 | tf_op jit(solution)/shard_map/ppermute | solution.py:294
  92.0 2.1 %collective-permute-done.18.refs_17_ = bf16[128,8,128]{2,1,0:T(8,128)(2,1)S(1)} collective-permute-done((bf16[128,8,128]{2,1,0:T(8,128)(2,1)S(1)}, bf16[128,8,128]{2,1,0:T(8,128)(2,1)S(1)}, u32[]{:S(2)}, u32[]{:S(2)}) %collective-permute-start.18) | collective-permute-done | bytes 262176 | tf_op jit(solution)/shard_map/ppermute | solution.py:294
  94.1 2.8 %collective-permute-start.19 = (bf16[128,8,128]{2,1,0:T(8,128)(2,1)S(1)}, bf16[128,8,128]{2,1,0:T(8,128)(2,1)S(1)}, u32[]{:S(2)}, u32[]{:S(2)}) collective-permute-start(bf16[128,8,128]{2,1,0:T(8,128)(2,1)S(1)} %collective-permute-done.18.refs_17_), channel_id=1, source_target_pairs={{0,448},{1,449},{2,450},{3,451},{4,452},{5,453},{6,454},{7,455},{8... | collective-permute-start | bytes 786440 | tf_op jit(solution)/shard_map/ppermute | solution.py:294
  98.5 5.7 %collective-permute-done.19.refs_18_ = bf16[128,8,128]{2,1,0:T(8,128)(2,1)S(1)} collective-permute-done((bf16[128,8,128]{2,1,0:T(8,128)(2,1)S(1)}, bf16[128,8,128]{2,1,0:T(8,128)(2,1)S(1)}, u32[]{:S(2)}, u32[]{:S(2)}) %collective-permute-start.19) | collective-permute-done | bytes 262176 | tf_op jit(solution)/shard_map/ppermute | solution.py:294
  104.2 6.3 %cross.1 = (bf16[64,128,128]{2,1,0:T(8,128)(2,1)S(1)}, bf16[64,256,128]{2,1,0:T(8,128)(2,1)S(1)}) custom-call(bf16[2,128,8,128]{3,2,1,0:T(8,128)(2,1)S(1)} %pad_maximum_fusion.2.refs_0_, bf16[2,128,8,128]{3,2,1,0:T(8,128)(2,1)S(1)} %pad_maximum_fusion.3.refs_1_, bf16[2,128,8,128]{3,2,1,0:T(8,128)(2,1)S(1)} %collective-permute-done.4.refs_2_, ...), custom_call_target="tpu_custom_call" | custom-call | tf_op jit(solution)/shard_map/cross/pallas_call | solution.py:251
  110.5 10.7 %collective-permute-start.20 = (bf16[64,128,128]{2,1,0:T(8,128)(2,1)S(1)}, bf16[64,128,128]{2,1,0:T(8,128)(2,1)S(1)}, u32[]{:S(2)}, u32[]{:S(2)}) collective-permute-start(bf16[64,128,128]{2,1,0:T(8,128)(2,1)S(1)} %get-tuple-element.12), channel_id=1, source_target_pairs={{0,16},{1,17},{2,18},{3,19},{4,20},{5,21},{6,22},{7,23},{8,24},{9,... | collective-permute-start | bytes 6291464 | tf_op jit(solution)/shard_map/ppermute | solution.py:294
  121.2 1.6 %lag_own.1 = f32[64,128,128]{2,1,0:T(8,128)S(1)} custom-call(bf16[64,256,128]{2,1,0:T(8,128)(2,1)S(1)} %get-tuple-element.11.stacked_ref, bf16[2,128,256]{2,1,0:T(8,128)(2,1)S(1)} %copy-done), custom_call_target="tpu_custom_call" | custom-call | flops 536870912 | bytes 8388608 | tf_op jit(solution)/shard_map/lag_own/pallas_call | solution.py:232
  122.8 2.1 %collective-permute-done.20 = bf16[64,128,128]{2,1,0:T(8,128)(2,1)S(1)} collective-permute-done((bf16[64,128,128]{2,1,0:T(8,128)(2,1)S(1)}, bf16[64,128,128]{2,1,0:T(8,128)(2,1)S(1)}, u32[]{:S(2)}, u32[]{:S(2)}) %collective-permute-start.20) | collective-permute-done | bytes 2097184 | tf_op jit(solution)/shard_map/ppermute | solution.py:294
  124.9 2.0 %add_convert_fusion = bf16[64,128,128]{2,1,0:T(8,128)(2,1)} fusion(f32[64,128,128]{2,1,0:T(8,128)S(1)} %lag_own.1, bf16[64,128,128]{2,1,0:T(8,128)(2,1)S(1)} %collective-permute-done.20), kind=kLoop, calls=%fused_computation | loop fusion | flops 3145728 | bytes 8388608 | tf_op jit(solution)/shard_map/convert_element_type | solution.py:325
  (21 shorter events, 4.2 us)
Async XLA Ops:
  2.7 3.6 %collective-permute-start = (bf16[512,128]{1,0:T(8,128)(2,1)S(1)}, bf16[512,128]{1,0:T(8,128)(2,1)S(1)}, u32[]{:S(2)}, u32[]{:S(2)}) collective-permute-start(bf16[512,128]{1,0:T(8,128)(2,1)S(1)} %get-tuple-element.10), channel_id=1, source_target_pairs={{0,16},{1,17},{2,18},{3,19},{4,20},{5,21},{6,22},{7,23},{8,24},{9,... | collective-permute-start | bytes 393224 | tf_op jit(solution)/shard_map/ppermute | solution.py:294
  6.4 15.9 %collective-permute-start.12 = (bf16[128,8,128]{2,1,0:T(8,128)(2,1)S(1)}, bf16[128,8,128]{2,1,0:T(8,128)(2,1)S(1)}, u32[]{:S(2)}, u32[]{:S(2)}) collective-permute-start(bf16[128,8,128]{2,1,0:T(8,128)(2,1)S(1)} %bitcast.11), channel_id=1, source_target_pairs={{0,448},{1,449},{2,450},{3,451},{4,452},{5,453},{6,454},{7,455},{8... | collective-permute-start | bytes 786440 | tf_op jit(solution)/shard_map/ppermute | solution.py:294
  11.5 10.8 %collective-permute-start.11 = (bf16[128,8,128]{2,1,0:T(8,128)(2,1)S(1)}, bf16[128,8,128]{2,1,0:T(8,128)(2,1)S(1)}, u32[]{:S(2)}, u32[]{:S(2)}) collective-permute-start(bf16[128,8,128]{2,1,0:T(8,128)(2,1)S(1)} %bitcast.12), channel_id=1, source_target_pairs={{0,64},{1,65},{2,66},{3,67},{4,68},{5,69},{6,70},{7,71},{8,72},{9,... | collective-permute-start | bytes 786440 | tf_op jit(solution)/shard_map/ppermute | solution.py:294
  13.4 21.2 %collective-permute-start.10 = (bf16[128,8,128]{2,1,0:T(8,128)(2,1)S(1)}, bf16[128,8,128]{2,1,0:T(8,128)(2,1)S(1)}, u32[]{:S(2)}, u32[]{:S(2)}) collective-permute-start(bf16[128,8,128]{2,1,0:T(8,128)(2,1)S(1)} %bitcast.13), channel_id=1, source_target_pairs={{0,32},{1,33},{2,34},{3,35},{4,36},{5,37},{6,38},{7,39},{8,40},{9,... | collective-permute-start | bytes 786440 | tf_op jit(solution)/shard_map/ppermute | solution.py:294
  34.6 69.6 %copy-start = (bf16[2,128,256]{2,1,0:T(8,128)(2,1)S(1)}, bf16[2,128,256]{2,1,0:T(8,128)(2,1)}, u32[]{:S(2)}) copy-start(bf16[2,128,256]{2,1,0:T(8,128)(2,1)} %constant.8.clone.refs_19_.inv_ref) | copy-start | bytes 393220
  34.7 30.5 %collective-permute-start.14 = (bf16[2,128,8,128]{3,2,1,0:T(8,128)(2,1)S(1)}, bf16[2,128,8,128]{3,2,1,0:T(8,128)(2,1)S(1)}, u32[]{:S(2)}, u32[]{:S(2)}) collective-permute-start(bf16[2,128,8,128]{3,2,1,0:T(8,128)(2,1)S(1)} %get-tuple-element.13), channel_id=1, source_target_pairs={{0,448},{1,449},{2,450},{3,451},{4,452},{5,453},{6,454},{7,455},{8... | collective-permute-start | bytes 1572872 | tf_op jit(solution)/shard_map/ppermute | solution.py:294
  39.3 10.5 %collective-permute-start.1 = (bf16[128,8,128]{2,1,0:T(8,128)(2,1)S(1)}, bf16[128,8,128]{2,1,0:T(8,128)(2,1)S(1)}, u32[]{:S(2)}, u32[]{:S(2)}) collective-permute-start(bf16[128,8,128]{2,1,0:T(8,128)(2,1)S(1)} %bitcast.14), channel_id=1, source_target_pairs={{0,1},{1,2},{2,3},{3,0},{4,5},{5,6},{6,7},{7,4},{8,9},{9,10},{10,1... | collective-permute-start | bytes 786440 | tf_op jit(solution)/shard_map/ppermute | solution.py:294
  41.2 16.1 %collective-permute-start.3 = (bf16[128,8,128]{2,1,0:T(8,128)(2,1)S(1)}, bf16[128,8,128]{2,1,0:T(8,128)(2,1)S(1)}, u32[]{:S(2)}, u32[]{:S(2)}) collective-permute-start(bf16[128,8,128]{2,1,0:T(8,128)(2,1)S(1)} %bitcast.15), channel_id=1, source_target_pairs={{0,2},{1,3},{2,0},{3,1},{4,6},{5,7},{6,4},{7,5},{8,10},{9,11},{10,... | collective-permute-start | bytes 786440 | tf_op jit(solution)/shard_map/ppermute | solution.py:294
  43.6 19.4 %collective-permute-start.2 = (bf16[128,8,128]{2,1,0:T(8,128)(2,1)S(1)}, bf16[128,8,128]{2,1,0:T(8,128)(2,1)S(1)}, u32[]{:S(2)}, u32[]{:S(2)}) collective-permute-start(bf16[128,8,128]{2,1,0:T(8,128)(2,1)S(1)} %bitcast.16), channel_id=1, source_target_pairs={{0,3},{1,0},{2,1},{3,2},{4,7},{5,4},{6,5},{7,6},{8,11},{9,8},{10,9... | collective-permute-start | bytes 786440 | tf_op jit(solution)/shard_map/ppermute | solution.py:294
  46.5 25.0 %collective-permute-start.13 = (bf16[2,128,8,128]{3,2,1,0:T(8,128)(2,1)S(1)}, bf16[2,128,8,128]{3,2,1,0:T(8,128)(2,1)S(1)}, u32[]{:S(2)}, u32[]{:S(2)}) collective-permute-start(bf16[2,128,8,128]{3,2,1,0:T(8,128)(2,1)S(1)} %get-tuple-element.14), channel_id=1, source_target_pairs={{0,64},{1,65},{2,66},{3,67},{4,68},{5,69},{6,70},{7,71},{8,72},{9,... | collective-permute-start | bytes 1572872 | tf_op jit(solution)/shard_map/ppermute | solution.py:294
  49.8 25.1 %collective-permute-start.4 = (bf16[2,128,8,128]{3,2,1,0:T(8,128)(2,1)S(1)}, bf16[2,128,8,128]{3,2,1,0:T(8,128)(2,1)S(1)}, u32[]{:S(2)}, u32[]{:S(2)}) collective-permute-start(bf16[2,128,8,128]{3,2,1,0:T(8,128)(2,1)S(1)} %pad_maximum_fusion.2.refs_0_), channel_id=1, source_target_pairs={{0,4},{1,5},{2,6},{3,7},{4,8},{5,9},{6,10},{7,11},{8,12},{9,13},{1... | collective-permute-start | bytes 1572872 | tf_op jit(solution)/shard_map/ppermute | solution.py:294
  63.0 13.8 %collective-permute-start.7 = (bf16[2,128,8,128]{3,2,1,0:T(8,128)(2,1)S(1)}, bf16[2,128,8,128]{3,2,1,0:T(8,128)(2,1)S(1)}, u32[]{:S(2)}, u32[]{:S(2)}) collective-permute-start(bf16[2,128,8,128]{3,2,1,0:T(8,128)(2,1)S(1)} %pad_maximum_fusion.3.refs_1_), channel_id=1, source_target_pairs={{0,12},{1,13},{2,14},{3,15},{4,0},{5,1},{6,2},{7,3},{8,4},{9,5},{1... | collective-permute-start | bytes 1572872 | tf_op jit(solution)/shard_map/ppermute | solution.py:294
  65.2 13.8 %collective-permute-start.16 = (bf16[2,128,8,128]{3,2,1,0:T(8,128)(2,1)S(1)}, bf16[2,128,8,128]{3,2,1,0:T(8,128)(2,1)S(1)}, u32[]{:S(2)}, u32[]{:S(2)}) collective-permute-start(bf16[2,128,8,128]{3,2,1,0:T(8,128)(2,1)S(1)} %collective-permute-done.14.refs_13_), channel_id=1, source_target_pairs={{0,448},{1,449},{2,450},{3,451},{4,452},{5,453},{6,454},{7,455},{8... | collective-permute-start | bytes 1572872 | tf_op jit(solution)/shard_map/ppermute | solution.py:294
  67.1 19.6 %collective-permute-start.6 = (bf16[2,128,8,128]{3,2,1,0:T(8,128)(2,1)S(1)}, bf16[2,128,8,128]{3,2,1,0:T(8,128)(2,1)S(1)}, u32[]{:S(2)}, u32[]{:S(2)}) collective-permute-start(bf16[2,128,8,128]{3,2,1,0:T(8,128)(2,1)S(1)} %pad_maximum_fusion.2.refs_0_), channel_id=1, source_target_pairs={{0,12},{1,13},{2,14},{3,15},{4,0},{5,1},{6,2},{7,3},{8,4},{9,5},{1... | collective-permute-start | bytes 1572872 | tf_op jit(solution)/shard_map/ppermute | solution.py:294
  71.5 17.1 %collective-permute-start.15 = (bf16[2,128,8,128]{3,2,1,0:T(8,128)(2,1)S(1)}, bf16[2,128,8,128]{3,2,1,0:T(8,128)(2,1)S(1)}, u32[]{:S(2)}, u32[]{:S(2)}) collective-permute-start(bf16[2,128,8,128]{3,2,1,0:T(8,128)(2,1)S(1)} %collective-permute-done.13.refs_12_), channel_id=1, source_target_pairs={{0,64},{1,65},{2,66},{3,67},{4,68},{5,69},{6,70},{7,71},{8,72},{9,... | collective-permute-start | bytes 1572872 | tf_op jit(solution)/shard_map/ppermute | solution.py:294
  74.9 22.1 %collective-permute-start.5 = (bf16[2,128,8,128]{3,2,1,0:T(8,128)(2,1)S(1)}, bf16[2,128,8,128]{3,2,1,0:T(8,128)(2,1)S(1)}, u32[]{:S(2)}, u32[]{:S(2)}) collective-permute-start(bf16[2,128,8,128]{3,2,1,0:T(8,128)(2,1)S(1)} %pad_maximum_fusion.3.refs_1_), channel_id=1, source_target_pairs={{0,4},{1,5},{2,6},{3,7},{4,8},{5,9},{6,10},{7,11},{8,12},{9,13},{1... | collective-permute-start | bytes 1572872 | tf_op jit(solution)/shard_map/ppermute | solution.py:294
  76.8 21.7 %collective-permute-start.8 = (bf16[2,128,8,128]{3,2,1,0:T(8,128)(2,1)S(1)}, bf16[2,128,8,128]{3,2,1,0:T(8,128)(2,1)S(1)}, u32[]{:S(2)}, u32[]{:S(2)}) collective-permute-start(bf16[2,128,8,128]{3,2,1,0:T(8,128)(2,1)S(1)} %collective-permute-done.4.refs_2_), channel_id=1, source_target_pairs={{0,4},{1,5},{2,6},{3,7},{4,8},{5,9},{6,10},{7,11},{8,12},{9,13},{1... | collective-permute-start | bytes 1572872 | tf_op jit(solution)/shard_map/ppermute | solution.py:294
  78.9 19.6 %collective-permute-start.9 = (bf16[2,128,8,128]{3,2,1,0:T(8,128)(2,1)S(1)}, bf16[2,128,8,128]{3,2,1,0:T(8,128)(2,1)S(1)}, u32[]{:S(2)}, u32[]{:S(2)}) collective-permute-start(bf16[2,128,8,128]{3,2,1,0:T(8,128)(2,1)S(1)} %collective-permute-done.7.refs_5_), channel_id=1, source_target_pairs={{0,12},{1,13},{2,14},{3,15},{4,0},{5,1},{6,2},{7,3},{8,4},{9,5},{1... | collective-permute-start | bytes 1572872 | tf_op jit(solution)/shard_map/ppermute | solution.py:294
  86.7 7.4 %collective-permute-start.18 = (bf16[128,8,128]{2,1,0:T(8,128)(2,1)S(1)}, bf16[128,8,128]{2,1,0:T(8,128)(2,1)S(1)}, u32[]{:S(2)}, u32[]{:S(2)}) collective-permute-start(bf16[128,8,128]{2,1,0:T(8,128)(2,1)S(1)} %slice_bitcast_fusion), channel_id=1, source_target_pairs={{0,448},{1,449},{2,450},{3,451},{4,452},{5,453},{6,454},{7,455},{8... | collective-permute-start | bytes 786440 | tf_op jit(solution)/shard_map/ppermute | solution.py:294
  88.7 15.5 %collective-permute-start.17 = (bf16[2,128,8,128]{3,2,1,0:T(8,128)(2,1)S(1)}, bf16[2,128,8,128]{3,2,1,0:T(8,128)(2,1)S(1)}, u32[]{:S(2)}, u32[]{:S(2)}) collective-permute-start(bf16[2,128,8,128]{3,2,1,0:T(8,128)(2,1)S(1)} %collective-permute-done.15.refs_14_), channel_id=1, source_target_pairs={{0,64},{1,65},{2,66},{3,67},{4,68},{5,69},{6,70},{7,71},{8,72},{9,... | collective-permute-start | bytes 1572872 | tf_op jit(solution)/shard_map/ppermute | solution.py:294
  94.1 10.1 %collective-permute-start.19 = (bf16[128,8,128]{2,1,0:T(8,128)(2,1)S(1)}, bf16[128,8,128]{2,1,0:T(8,128)(2,1)S(1)}, u32[]{:S(2)}, u32[]{:S(2)}) collective-permute-start(bf16[128,8,128]{2,1,0:T(8,128)(2,1)S(1)} %collective-permute-done.18.refs_17_), channel_id=1, source_target_pairs={{0,448},{1,449},{2,450},{3,451},{4,452},{5,453},{6,454},{7,455},{8... | collective-permute-start | bytes 786440 | tf_op jit(solution)/shard_map/ppermute | solution.py:294
  110.5 14.5 %collective-permute-start.20 = (bf16[64,128,128]{2,1,0:T(8,128)(2,1)S(1)}, bf16[64,128,128]{2,1,0:T(8,128)(2,1)S(1)}, u32[]{:S(2)}, u32[]{:S(2)}) collective-permute-start(bf16[64,128,128]{2,1,0:T(8,128)(2,1)S(1)} %get-tuple-element.12), channel_id=1, source_target_pairs={{0,16},{1,17},{2,18},{3,19},{4,20},{5,21},{6,22},{7,23},{8,24},{9,... | collective-permute-start | bytes 6291464 | tf_op jit(solution)/shard_map/ppermute | solution.py:294
